TPU v7x, 32 devices: a whole 2x2x4 slice. The times are simulated.
32 devices in a mesh: patch: 2 (over x), row: 4 (over y, core), col: 4 (over z).
Axes of the slice: x: 2, y: 2, z: 4, core: 2. Of those that a mesh axis runs over, the one named last changes fastest.
Arguments:
- sky_cube: float32 [512, 128, 512], P(None, ('patch', 'row'), 'col'), parts along dimension 1, may hold values from -40 to 140
- beam_taps: float32 [512, 33], replicated, may hold values from 0 to 0.2
Outputs:
- cleaned_cube: float32 [512, 128, 512], P(None, ('patch', 'row'), 'col'), parts along dimension 1
There are 2 independent parts, one for each index of `patch`. A program takes and returns all parts, laid end to end along the dimension named above; an argument that names none is the same for every part. Nothing has to cross between parts.
All inputs are finite; a program needn't handle non-finite values.
Results may differ from a plain program's by a relative error of at most 0.00085.
Values sent between devices are 32-bit elements; how exact they have to be, the bound alone decides.
No kernel may reach another device: no remote copies, remote signals or barrier semaphores. Data moves between devices by JAX's collectives and lax.ppermute only.
A program may use at most 64 MiB of HBM per device.

v0:
```python
import jax
import jax.numpy as jnp
from jax import lax
from jax.sharding import PartitionSpec as P

MODES = 4
SWEEPS = 3


def padded(array, sides, width):
    for axis, dim in sides:
        peers, length = (lax.axis_size(axis), array.shape[dim])
        up = [(i, (i + 1) % peers) for i in range(peers - 1)]
        down = [(j, i) for i, j in up]
        last = lax.slice_in_dim(array, length - width, length, axis=dim)
        leading = lax.slice_in_dim(array, 0, width, axis=dim)
        before = lax.ppermute(last, axis, up)
        after = lax.ppermute(leading, axis, down)
        array = jnp.concatenate([before, array, after], axis=dim)
    return array


def convolve(padded_field, beam_taps, axis_dim, out_width):
    result = None
    for offset in range(beam_taps.shape[1]):
        piece = lax.slice_in_dim(padded_field, offset, offset + out_width, axis=axis_dim)
        term = beam_taps[:, offset][:, None, None] * piece
        result = term if result is None else result + term
    return result


def orthonormalize(block):
    length = block.shape[0]
    columns = []
    for index in range(block.shape[1]):
        vector = block[:, index]
        for repeat in range(2):
            for earlier in columns:
                vector = vector - jnp.sum(earlier * vector) * earlier
        scale_mean = jnp.mean(vector * vector) + 1e-06
        vector = vector / jnp.sqrt(scale_mean) / jnp.sqrt(jnp.float32(length))
        columns.append(vector)
    return jnp.stack(columns, axis=1)


def leading_modes(gram_matrix, channels):
    scaled_gram = gram_matrix * (channels / jnp.trace(gram_matrix))
    channel_pos = jnp.arange(channels).astype(jnp.float32)
    mode_index = jnp.arange(MODES).astype(jnp.float32)
    cosine_basis = jnp.cos(jnp.pi * mode_index[None, :] * (channel_pos[:, None] + 0.5) / channels)
    basis = orthonormalize(cosine_basis)
    for sweep in range(SWEEPS):
        basis = orthonormalize(
            jnp.dot(
                scaled_gram,
                basis,
                precision=lax.Precision.HIGHEST,
                preferred_element_type=jnp.float32,
            )
        )
    return basis


def per_device(sky_cube, beam_taps):
    margin = beam_taps.shape[1] // 2
    channels, tile_rows, tile_cols = sky_cube.shape
    extended = padded(sky_cube, (("col", 2),), margin)
    smoothed = convolve(extended, beam_taps, 2, tile_cols)
    extended_rows = padded(smoothed, (("row", 1),), margin)
    beamed = convolve(extended_rows, beam_taps, 1, tile_rows)
    flattened = beamed.reshape(channels, tile_rows * tile_cols)
    partial_gram = jnp.dot(
        flattened, flattened.T, precision=lax.Precision.HIGHEST, preferred_element_type=jnp.float32
    )
    gram_matrix = lax.psum(partial_gram, ("row", "col"))
    mode_spectra = leading_modes(gram_matrix, channels)
    coefficients = jnp.dot(
        mode_spectra.T,
        flattened,
        precision=lax.Precision.HIGHEST,
        preferred_element_type=jnp.float32,
    )
    cleaned = flattened - jnp.dot(
        mode_spectra,
        coefficients,
        precision=lax.Precision.HIGHEST,
        preferred_element_type=jnp.float32,
    )
    return cleaned.reshape(channels, tile_rows, tile_cols)


def solution(mesh):
    placed = (P(None, ("patch", "row"), "col"), P())
    return jax.shard_map(
        per_device,
        mesh=mesh,
        in_specs=placed,
        out_specs=P(None, ("patch", "row"), "col"),
        check_vma=False,
    )
```

profile of v0, /device:TPU:0, one launch (start us, length us, event | category | flops | bytes accessed | tf_op | source)
XLA Modules:
  0.0 529.3 jit_solution(5304933710967582449)
XLA Ops:
  6.5 7.9 %fusion.232 = (f32[512,16,16]{2,1,0:T(8,128)}, f32[512,16,16]{2,1,0:T(8,128)}) fusion(f32[512,16,128]{2,1,0:T(8,128)} %param.2), kind=kLoop, calls=%fused_computation.501 | loop fusion | bytes 2097152 | tf_op jit(solution)/shard_map/slice | solution.py:15
  14.5 2.8 copy.12
  17.3 1.3 collective-permute-start.1
  18.6 2.8 copy.11
  21.4 5.6 %collective-permute-start = (f32[512,16,16]{0,2,1:T(8,128)S(1)}, f32[512,16,16]{0,2,1:T(8,128)S(1)}, u32[]{:S(2)}, u32[]{:S(2)}) collective-permute-start(f32[512,16,16]{0,2,1:T(8,128)S(1)} %copy.11), channel_id=1, source_target_pairs={{0,1},{1,2},{2,3},{4,5},{5,6},{6,7},{8,9},{9,10},{10,11},{12,13},{... | collective-permute-start | bytes 1572872 | tf_op jit(solution)/shard_map/ppermute | solution.py:17
  27.1 7.1 %collective-permute-done.1 = f32[512,16,16]{0,2,1:T(8,128)S(1)} collective-permute-done((f32[512,16,16]{0,2,1:T(8,128)S(1)}, f32[512,16,16]{0,2,1:T(8,128)S(1)}, u32[]{:S(2)}, u32[]{:S(2)}) %collective-permute-start.1) | collective-permute-done | bytes 524320 | tf_op jit(solution)/shard_map/ppermute | solution.py:18
  34.2 3.6 copy.8
  38.2 3.7 copy.6
  41.8 124.4 %fusion.91 = f32[512,16,128]{2,1,0:T(8,128)} fusion(f32[512,16,128]{2,1,0:T(8,128)} %param.2, f32[512,16,16]{2,1,0:T(8,128)} %copy.8, f32[512,16,16]{2,1,0:T(8,128)} %copy.6, f32[512]{0:T(512)S(1)} %bitcast.136, f32[512]{0:T(512)S(1)} %bitcast.138, f32[512]{0:T(512)S(1)} %bitcast.142, f32[512]{0:T(512)S(1)} %bitcast.144, f32[512]{0:T(512)S(1)} %bitcast.146, ...), kind=kLoop, calls=%fused_computation.207 | loop fusion | flops 101711872 | bytes 9504768 | tf_op jit(solution)/shard_map/add | solution.py:28
  166.3 1.3 collective-permute-start.3
  167.6 5.0 collective-permute-start.2
  187.5 114.2 %fusion.4 = f32[512,16,128]{2,1,0:T(8,128)S(1)} fusion(f32[512,16,128]{2,1,0:T(8,128)} %fusion.91, f32[512,16,128]{2,1,0:T(8,128)} %collective-permute-done.3, f32[512,16,128]{2,1,0:T(8,128)} %collective-permute-done.2, f32[512]{0:T(512)S(1)} %bitcast.137, f32[512]{0:T(512)S(1)} %bitcast.139, f32[512]{0:T(512)S(1)} %bitcast.143, f32[512]{0:T(512)S(1)} %bitcast.145, ...), kind=kLoop, calls=%fused_computation.120 | loop fusion | flops 99614720 | bytes 16844800 | tf_op jit(solution)/shard_map/add | solution.py:28
  301.7 2.0 copy-done
  303.7 10.8 %fusion.190 = f32[512,512]{1,0:T(8,128)} fusion(f32[512,16,128]{2,1,0:T(8,128)S(1)} %fusion.4), kind=kOutput, calls=%fused_computation.311 | convolution fusion | flops 6442450944 | bytes 5242880 | tf_op jit(solution)/shard_map/dot_general | solution.py:72
  318.3 123.3 %all-reduce.2.cloned.1.call-done = f32[512,512]{1,0:T(8,128)} async-done(((f32[512,512]{1,0:T(8,128)}), f32[512,512]{1,0:T(8,128)}) %all-reduce.2.cloned.1.call-update) | async-done | bytes 1048592 | tf_op jit(solution)/shard_map/psum | solution.py:75
  441.5 2.1 select_reduce_fusion
  444.3 2.2 fusion.197
  446.6 0.7 multiply_reduce_fusion.47
  452.8 0.7 multiply_reduce_fusion.42
  456.1 0.7 multiply_reduce_fusion.37
  459.3 0.7 multiply_reduce_fusion.36
  460.7 0.7 multiply_reduce_fusion.35
  463.5 0.7 multiply_reduce_fusion.33
  464.9 0.7 multiply_reduce_fusion.32
  466.3 2.2 fusion.195
  468.5 0.7 multiply_reduce_fusion.31
  474.8 0.7 multiply_reduce_fusion.26
  478.1 0.7 multiply_reduce_fusion.21
  481.3 0.7 multiply_reduce_fusion.20
  482.7 0.7 multiply_reduce_fusion.19
  485.5 0.7 multiply_reduce_fusion.17
  486.8 0.7 multiply_reduce_fusion.16
  488.3 1.0 fusion.193
  489.3 0.7 multiply_reduce_fusion.15
  490.8 0.7 multiply_reduce_fusion.14
  492.2 0.7 multiply_reduce_fusion.11
  494.1 0.7 multiply_reduce_fusion.12
  495.6 0.7 multiply_reduce_fusion.10
  497.0 0.7 multiply_reduce_fusion.6
  498.9 0.7 multiply_reduce_fusion.5
  502.1 0.7 multiply_reduce_fusion.4
  503.5 0.7 multiply_reduce_fusion.3
  504.9 0.7 multiply_reduce_fusion.2
  506.2 0.7 multiply_reduce_fusion.1
  507.6 0.7 multiply_reduce_fusion
  509.1 5.7 %fusion.180 = f32[4,2048]{1,0:T(4,128)S(1)} fusion(f32[64,8,16,128]{3,2,1,0:T(8,128)} %bitcast.86, f32[512,1]{0,1:T(1,128)S(1)} %divide_multiply_fusion, f32[512,1]{0,1:T(1,128)S(1)} %get-tuple-element.31, f32[512,1]{0,1:T(1,128)S(1)} %get-tuple-element.29, f32[512,1]{0,1:T(1,128)S(1)} %get-tuple-element.46), kind=kOutput, calls=%fused_computation.297 | convolution fusion | flops 50337792 | bytes 4235264 | tf_op jit(solution)/shard_map/dot_general | solution.py:77
  514.8 4.7 fusion.182
  519.5 2.9 copy.14
  (74 shorter events, 17.6 us)
Async XLA Ops:
  6.5 435.0 %all-reduce.2.cloned.1.call-start = ((), (), s32[]{:S(2)}) async-start(), calls=%async_computation | async-start | bytes 2097152 | tf_op jit(solution)/shard_map/psum | solution.py:75
  14.5 12.6 %copy-start.3 = (f32[512,33]{0,1:T(8,128)S(1)}, f32[512,33]{0,1:T(8,128)}, u32[]{:S(2)}) copy-start(f32[512,33]{0,1:T(8,128)} %param.3) | copy-start | bytes 202756
  17.3 16.9 %collective-permute-start.1 = (f32[512,16,16]{0,2,1:T(8,128)S(1)}, f32[512,16,16]{0,2,1:T(8,128)S(1)}, u32[]{:S(2)}, u32[]{:S(2)}) collective-permute-start(f32[512,16,16]{0,2,1:T(8,128)S(1)} %copy.12), channel_id=1, source_target_pairs={{1,0},{2,1},{3,2},{5,4},{6,5},{7,6},{9,8},{10,9},{11,10},{13,12},{... | collective-permute-start | bytes 1572872 | tf_op jit(solution)/shard_map/ppermute | solution.py:18
  21.4 16.8 %collective-permute-start = (f32[512,16,16]{0,2,1:T(8,128)S(1)}, f32[512,16,16]{0,2,1:T(8,128)S(1)}, u32[]{:S(2)}, u32[]{:S(2)}) collective-permute-start(f32[512,16,16]{0,2,1:T(8,128)S(1)} %copy.11), channel_id=1, source_target_pairs={{0,1},{1,2},{2,3},{4,5},{5,6},{6,7},{8,9},{9,10},{10,11},{12,13},{... | collective-permute-start | bytes 1572872 | tf_op jit(solution)/shard_map/ppermute | solution.py:17
  166.3 21.2 %collective-permute-start.3 = (f32[512,16,128]{2,1,0:T(8,128)}, f32[512,16,128]{2,1,0:T(8,128)}, u32[]{:S(2)}, u32[]{:S(2)}) collective-permute-start(f32[512,16,128]{2,1,0:T(8,128)} %fusion.91), channel_id=1, source_target_pairs={{4,0},{8,4},{12,8},{5,1},{9,5},{13,9},{6,2},{10,6},{14,10},{7,3},{... | collective-permute-start | bytes 12582920 | tf_op jit(solution)/shard_map/ppermute | solution.py:18
  167.6 19.9 %collective-permute-start.2 = (f32[512,16,128]{2,1,0:T(8,128)}, f32[512,16,128]{2,1,0:T(8,128)}, u32[]{:S(2)}, u32[]{:S(2)}) collective-permute-start(f32[512,16,128]{2,1,0:T(8,128)} %fusion.91), channel_id=1, source_target_pairs={{0,4},{4,8},{8,12},{1,5},{5,9},{9,13},{2,6},{6,10},{10,14},{3,7},{... | collective-permute-start | bytes 12582920 | tf_op jit(solution)/shard_map/ppermute | solution.py:17
  301.7 2.0 copy-start
  441.5 46.8 %copy-start.2 = (f32[512,512]{1,0:T(8,128)S(1)}, f32[512,512]{1,0:T(8,128)}, u32[]{:S(2)}) copy-start(f32[512,512]{1,0:T(8,128)} %all-reduce.2.cloned.1.call-done) | copy-start | bytes 3145732
  509.1 5.7 %copy-start.1 = (f32[512,16,128]{2,1,0:T(8,128)S(1)}, f32[512,16,128]{2,1,0:T(8,128)}, u32[]{:S(2)}) copy-start(f32[512,16,128]{2,1,0:T(8,128)} %copy-done) | copy-start | bytes 12582916
Sparse Core Ops, SparseCore 0:
  314.6 126.8 all-reduce.1
where the time goes:
time: 530 us; the launch traced here: 529 us
  other arithmetic  276 us (52%)
  waiting for transfers between devices  131 us (25%)
  between operations  57.1 us (11%)
  matrix products  26.6 us (5%)
  local copies, waits for them, and re-layouts  25.8 us (5%)
  starting transfers between devices  13.2 us (2%)
    add x2, other arithmetic, convolve(): result = term if result is None else result + term  239 us
    psum x1, waiting for transfers between devices, per_device(): gram_matrix = lax.psum(partial_gram, ('row', 'col'))  123 us
    reduce_sum x36, other arithmetic, orthonormalize(): vector = vector - jnp.sum(earlier * vector) * earlier  24 us
    dot_general x1, matrix products, per_device(): jnp.dot(flattened, flattened.T, precision=lax.Precision.HIGHEST, preferre...  10.8 us
    ppermute x2, starting transfers between devices, padded(): before = lax.ppermute(last, axis, up)  10.6 us
  transfers between devices with their start and end apart: 5, of which 3 were waited for; matrix products, arithmetic and copies ran while one was open for 3% of the time, Pallas kernels for 0%

commit v1 on v0

v1 whole, which is shorter than its diff:
```python
import functools

import jax
import jax.numpy as jnp
from jax import lax
from jax.experimental import pallas as pl
from jax.experimental.pallas import tpu as pltpu
from jax.sharding import PartitionSpec as P

MODES = 4
SWEEPS = 3
LANES = 128
SUB = 8

ANY = pl.BlockSpec(memory_space=pl.ANY)
VM = pl.BlockSpec(memory_space=pltpu.VMEM)
SM = pl.BlockSpec(memory_space=pltpu.SMEM)
f32 = jnp.float32


def shape(*dims):
    return jax.ShapeDtypeStruct(dims, f32)


def cost(flops, nbytes):
    return pl.CostEstimate(flops=int(flops), bytes_accessed=int(nbytes), transcendentals=0)


def row_taps(buf, taps_ref, out_ref, rows, cols, taps):
    def body(group, carry):
        part = pl.ds(pl.multiple_of(group * SUB, SUB), SUB)
        weights = [taps_ref[a] for a in range(taps)]
        total = [None] * rows
        for r in range(rows + taps - 1):
            x = buf[r, part, :]
            for i in range(max(0, r - taps + 1), min(rows - 1, r) + 1):
                term = weights[r - i] * x
                total[i] = term if total[i] is None else total[i] + term
        for i in range(rows):
            out_ref[i, part, :] = total[i]
        return carry

    lax.fori_loop(0, cols // SUB, body, 0)


def col_taps(buf, taps_ref, out_ref, rows, cols, taps, step=2):
    groups = cols // SUB

    def body(block, carry):
        weights = [taps_ref[a] for a in range(taps)]
        total = {}
        for s in range(SUB * (groups - 1) + taps):
            for q in range(step):
                i = block * step + q
                x = buf[i, pl.ds(s, SUB), :]
                for g in range(groups):
                    a = s - SUB * g
                    if 0 <= a < taps:
                        term = weights[a] * x
                        total[q, g] = term if a == 0 else total[q, g] + term
                        if a == taps - 1:
                            out_ref[i, pl.ds(SUB * g, SUB), :] = total.pop((q, g))
        return carry

    lax.fori_loop(0, rows // step, body, 0)


def copies_in(pairs, sems):
    started = []
    for index, (source, target) in enumerate(pairs):
        copy = pltpu.make_async_copy(source, target, sems.at[index])
        copy.start()
        started.append(copy)
    for copy in started:
        copy.wait()


def prep_kernel(rows, cols, margin, x_ref, raw_ref, first_ref, last_ref):
    for r in range(rows):
        tile = x_ref[pl.ds(r, LANES, stride=rows), :].T
        raw_ref[0, r] = tile
        first_ref[0, r] = tile[:margin]
        last_ref[0, r] = tile[cols - margin:]


def prep(flat, rows, cols, margin, start, count):
    return pl.pallas_call(
        functools.partial(prep_kernel, rows, cols, margin),
        grid=(count,),
        in_specs=[pl.BlockSpec((LANES * rows, cols), lambda k: (k + start, 0))],
        out_specs=[
            pl.BlockSpec((1, rows, cols, LANES), lambda k: (k, 0, 0, 0)),
            pl.BlockSpec((1, rows, margin, LANES), lambda k: (k, 0, 0, 0)),
            pl.BlockSpec((1, rows, margin, LANES), lambda k: (k, 0, 0, 0)),
        ],
        out_shape=[
            shape(count, rows, cols, LANES),
            shape(count, rows, margin, LANES),
            shape(count, rows, margin, LANES),
        ],
        cost_estimate=cost(4e6 * count, 2.5e6 * count),
        name="prep",
    )(flat)


def columns_kernel(which, rows, cols, margin, taps, flip, x_ref, before_ref, after_ref, taps_ref, out_ref, buf, held, sems):
    copies_in(
        [
            (x_ref.at[which], buf.at[:, pl.ds(margin, cols), :]),
            (before_ref.at[which], buf.at[:, pl.ds(0, margin), :]),
            (after_ref.at[which], buf.at[:, pl.ds(margin + cols, margin), :]),
        ],
        sems,
    )
    if not flip:
        col_taps(buf, taps_ref, out_ref, rows, cols, taps)
    else:
        col_taps(buf, taps_ref, held, rows, cols, taps)
        for r in range(rows):
            out_ref[:, r * cols:(r + 1) * cols] = held[r].T


def columns(which, x, before, after, taps, margin, flip):
    _, rows, cols, _ = x.shape
    count = taps.shape[0]
    out = shape(LANES, rows * cols) if flip else shape(rows, cols, LANES)
    return pl.pallas_call(
        functools.partial(columns_kernel, which, rows, cols, margin, count, flip),
        in_specs=[ANY, ANY, ANY, VM],
        out_specs=VM,
        out_shape=out,
        scratch_shapes=[
            pltpu.VMEM((rows, cols + 2 * margin, LANES), f32),
            pltpu.VMEM((rows, cols, LANES), f32),
            pltpu.SemaphoreType.DMA((3,)),
        ],
        cost_estimate=cost(2e7, 2.5e6),
        name="columns",
    )(x, before, after, taps)


def rows_kernel(rows, cols, margin, taps, raw, side_ref, x_ref, near_ref, far_ref, taps_ref, *rest):
    if raw:
        out_ref, first_ref, last_ref, buf, native, sems = rest
    else:
        out_ref, buf, held, sems = rest
    even = side_ref[0] == 0
    near = jnp.where(even, margin + rows, 0)
    far = jnp.where(even, 0, margin + rows)
    if raw:
        copies_in([(x_ref, native.at[0]), (near_ref, native.at[1]), (far_ref, native.at[2])], sems)
        for slot, start in ((0, margin), (1, near), (2, far)):
            for r in range(rows):
                buf[start + r] = native[slot, pl.ds(r, LANES, stride=rows), :].T
        row_taps(buf, taps_ref, out_ref.at[0], rows, cols, taps)
        first_ref[0] = out_ref[0, :, :margin, :]
        last_ref[0] = out_ref[0, :, cols - margin:, :]
    else:
        copies_in(
            [
                (x_ref, buf.at[pl.ds(margin, rows)]),
                (near_ref, buf.at[pl.ds(near, rows)]),
                (far_ref, buf.at[pl.ds(far, rows)]),
            ],
            sems,
        )
        row_taps(buf, taps_ref, held, rows, cols, taps)
        for r in range(rows):
            out_ref[:, r * cols:(r + 1) * cols] = held[r].T


def rows_of(x, near, far, taps, side, rows, cols, margin, raw):
    count = taps.shape[0]
    if raw:
        outs = [shape(1, rows, cols, LANES), shape(1, rows, margin, LANES), shape(1, rows, margin, LANES)]
        extra = pltpu.VMEM((3, LANES * rows, cols), f32)
    else:
        outs = shape(LANES, rows * cols)
        extra = pltpu.VMEM((rows, cols, LANES), f32)
    return pl.pallas_call(
        functools.partial(rows_kernel, rows, cols, margin, count, raw),
        in_specs=[SM, ANY, ANY, ANY, VM],
        out_specs=[VM] * 3 if raw else VM,
        out_shape=outs,
        scratch_shapes=[
            pltpu.VMEM((rows + 2 * margin, cols, LANES), f32),
            extra,
            pltpu.SemaphoreType.DMA((3,)),
        ],
        cost_estimate=cost(2e7, 4e6),
        name="rows_raw" if raw else "rows",
    )(side, x, near, far, taps)


def gram_kernel(chunks, peers, me_ref, *refs):
    xs, outs = refs[:chunks], refs[chunks:chunks + peers]
    high, low, gram, mixed = refs[chunks + peers:]
    for k, x_ref in enumerate(xs):
        x = x_ref[...]
        h = x.astype(jnp.bfloat16)
        high[k * LANES:(k + 1) * LANES, :] = h
        low[k * LANES:(k + 1) * LANES, :] = (x - h.astype(f32)).astype(jnp.bfloat16)
    last = (((1,), (1,)), ((), ()))
    mixed[...] = lax.dot_general(high[...], low[...], last, preferred_element_type=f32)
    gram[...] = lax.dot_general(high[...], high[...], last, preferred_element_type=f32)
    gram[...] += mixed[...] + mixed[...].T
    size = gram.shape[0] // peers
    for d in range(peers):
        piece = me_ref[0] ^ d
        outs[d][...] = gram[pl.ds(pl.multiple_of(piece * size, size), size), :]


def gram_pieces(xs, me, peers):
    chunks = len(xs)
    channels = chunks * LANES
    pixels = xs[0].shape[1]
    return pl.pallas_call(
        functools.partial(gram_kernel, chunks, peers),
        in_specs=[SM] + [VM] * chunks,
        out_specs=[VM] * peers,
        out_shape=[shape(channels // peers, channels)] * peers,
        scratch_shapes=[
            pltpu.VMEM((channels, pixels), jnp.bfloat16),
            pltpu.VMEM((channels, pixels), jnp.bfloat16),
            pltpu.VMEM((channels, channels), f32),
            pltpu.VMEM((channels, channels), f32),
        ],
        cost_estimate=cost(4e9, 5e6),
        name="gram",
    )(me, *xs)


def split_kernel(count, peers, me_ref, *refs):
    parts, outs = refs[:count], refs[count:count + peers]
    total = refs[count + peers]
    value = parts[0][...]
    for part in parts[1:]:
        value = value + part[...]
    total[...] = value
    size = total.shape[0] // peers
    for d in range(peers):
        piece = me_ref[0] ^ d
        outs[d][...] = total[pl.ds(pl.multiple_of(piece * size, size), size), :]


def sum_and_split(parts, me, peers):
    height, width = parts[0].shape
    return pl.pallas_call(
        functools.partial(split_kernel, len(parts), peers),
        in_specs=[SM] + [VM] * len(parts),
        out_specs=[VM] * peers,
        out_shape=[shape(height // peers, width)] * peers,
        scratch_shapes=[pltpu.VMEM((height, width), f32)],
        name="sum_and_split",
    )(me, *parts)


def join_kernel(peers, me_ref, *refs):
    parts, out_ref = refs[:peers], refs[peers]
    size = parts[0].shape[0]
    for d in range(peers):
        piece = me_ref[0] ^ d
        out_ref[pl.ds(pl.multiple_of(piece * size, size), size), :] = parts[d][...]


def join(parts, me):
    peers = len(parts)
    height, width = parts[0].shape
    return pl.pallas_call(
        functools.partial(join_kernel, peers),
        in_specs=[SM] + [VM] * peers,
        out_specs=VM,
        out_shape=shape(height * peers, width),
        name="join",
    )(me, *parts)


def exchange(pieces, axis):
    peers = len(pieces)
    moved = [pieces[0]]
    for d in range(1, peers):
        moved.append(lax.ppermute(pieces[d], axis, [(i, i ^ d) for i in range(peers)]))
    return moved


def dot(u, v):
    return jnp.sum(u * v, axis=1, keepdims=True)


def orthonormal_rows(block, channels):
    done, cross = [], {}
    for index, vector in enumerate(block):
        for repeat in range(2):
            factors = [dot(q, vector) for q in done]
            for j in range(index):
                for i in range(j):
                    factors[j] = factors[j] - factors[i] * cross[i, j]
            for q, factor in zip(done, factors):
                vector = vector - factor * q
        scale_mean = dot(vector, vector) / channels + 1e-06
        vector = vector / jnp.sqrt(scale_mean) / jnp.sqrt(jnp.float32(channels))
        for i, q in enumerate(done):
            cross[i, index] = dot(q, vector)
        done.append(vector)
    return done


def start_kernel(channels, cosine_ref, out_ref):
    rows = orthonormal_rows([cosine_ref[k:k + 1, :] for k in range(MODES)], channels)
    out_ref[...] = jnp.concatenate(rows + [jnp.zeros((SUB - MODES, channels), f32)], axis=0)


def start_basis(channels):
    channel_pos = jnp.arange(channels).astype(f32)
    mode_index = jnp.arange(MODES).astype(f32)
    cosine = jnp.cos(jnp.pi * mode_index[:, None] * (channel_pos[None, :] + 0.5) / channels)
    return pl.pallas_call(
        functools.partial(start_kernel, channels),
        in_specs=[VM],
        out_specs=VM,
        out_shape=shape(SUB, channels),
        name="start_basis",
    )(cosine)


def spread(basis, wide, channels):
    for c in range(0, channels, LANES):
        tall = basis[:, c:c + LANES].T
        for k in range(MODES):
            wide[k, c:c + LANES, :] = jnp.broadcast_to(tall[:, k:k + 1], (LANES, LANES))


def clean_kernel(chunks, peers, rows, cols, me_ref, start_ref, *refs):
    xs, pieces, out_ref = refs[:chunks], refs[chunks:chunks + peers], refs[chunks + peers]
    x_buf, gram, wide, coef, sems, out_buf, out_sems = refs[chunks + peers + 1:]
    channels = chunks * LANES
    started = []
    for k in range(chunks):
        copy = pltpu.make_async_copy(xs[k], x_buf.at[pl.ds(k * LANES, LANES)], sems.at[k])
        copy.start()
        started.append(copy)
    size = channels // peers
    for d in range(peers):
        piece = me_ref[0] ^ d
        gram[pl.ds(pl.multiple_of(piece * size, size), size), :] = pieces[d][...]
    row_id = lax.broadcasted_iota(jnp.int32, (channels, channels), 0)
    col_id = lax.broadcasted_iota(jnp.int32, (channels, channels), 1)
    diagonal = jnp.sum(jnp.where(row_id == col_id, gram[...], 0.0), axis=0, keepdims=True)
    scale = channels / jnp.sum(diagonal, axis=1, keepdims=True)
    basis = start_ref[...]
    for sweep in range(SWEEPS):
        spread(basis, wide, channels)
        totals = [[None] * (channels // LANES) for k in range(MODES)]
        for k in range(MODES):
            for t in range(channels // LANES):
                total = None
                for c in range(0, channels, SUB):
                    term = wide[k, c:c + SUB, :] * gram[c:c + SUB, t * LANES:(t + 1) * LANES]
                    total = term if total is None else total + term
                totals[k][t] = jnp.sum(total, axis=0, keepdims=True)
        vectors = [jnp.concatenate(totals[k], axis=1) * scale for k in range(MODES)]
        new = orthonormal_rows(vectors, channels)
        basis = jnp.concatenate(new + [jnp.zeros((SUB - MODES, channels), f32)], axis=0)
    spread(basis, wide, channels)
    for copy in started:
        copy.wait()

    def one_row(r, carry):
        part = pl.ds(pl.multiple_of(r * cols, cols), cols)
        totals = [None] * MODES
        for c in range(0, channels, SUB):
            x = x_buf[c:c + SUB, part]
            for k in range(MODES):
                term = wide[k, c:c + SUB, :] * x
                totals[k] = term if totals[k] is None else totals[k] + term
        coefs = [jnp.broadcast_to(jnp.sum(total, axis=0, keepdims=True), (SUB, LANES)) for total in totals]
        for c in range(0, channels, SUB):
            value = x_buf[c:c + SUB, part]
            model = wide[0, c:c + SUB, :] * coefs[0]
            for k in range(1, MODES):
                model = model + wide[k, c:c + SUB, :] * coefs[k]
            out_buf[pl.ds(c * rows + r, SUB, stride=rows), :] = value - model
        return carry

    lax.fori_loop(0, rows, one_row, 0)
    copy = pltpu.make_async_copy(out_buf, out_ref, out_sems.at[0])
    copy.start()
    copy.wait()


def clean(xs, pieces, me, start, rows, cols):
    chunks, peers = len(xs), len(pieces)
    channels = chunks * LANES
    return pl.pallas_call(
        functools.partial(clean_kernel, chunks, peers, rows, cols),
        in_specs=[SM, VM] + [ANY] * chunks + [VM] * peers,
        out_specs=ANY,
        out_shape=shape(channels * rows, cols),
        scratch_shapes=[
            pltpu.VMEM((channels, rows * cols), f32),
            pltpu.VMEM((channels, channels), f32),
            pltpu.VMEM((MODES, channels, LANES), f32),
            pltpu.VMEM((SUB, LANES), f32),
            pltpu.SemaphoreType.DMA((chunks,)),
            pltpu.VMEM((channels * rows, cols), f32),
            pltpu.SemaphoreType.DMA((1,)),
        ],
        cost_estimate=cost(4e7, 9e6),
        name="clean",
    )(me, start, *xs, *pieces)


def per_device(sky_cube, beam_taps):
    taps = beam_taps.shape[1]
    margin = taps // 2
    channels, rows, cols = sky_cube.shape
    chunks = channels // LANES
    n_row, n_col = lax.axis_size("row"), lax.axis_size("col")
    me_row = lax.axis_index("row").astype(jnp.int32)
    me_col = lax.axis_index("col").astype(jnp.int32)
    side = jnp.reshape(me_row % 2, (1,))
    near_pairs = [(i, i ^ 1) for i in range(n_row)]
    far_pairs = [(i, ((i + 1) ^ 1) - 1) for i in range(1, n_row - 1)]
    right = [(i, i + 1) for i in range(n_col - 1)]
    left = [(j, i) for i, j in right]

    flat = sky_cube.reshape(channels * rows, cols)
    head = flat[:LANES * rows]
    far0 = lax.ppermute(head, "row", far_pairs)
    near0 = lax.ppermute(head, "row", near_pairs)
    wide_taps = jnp.broadcast_to(
        beam_taps.T.reshape(taps, chunks, 1, LANES).transpose(1, 0, 2, 3), (chunks, taps, SUB, LANES)
    )
    tap = [wide_taps[k] for k in range(chunks)]
    start = start_basis(channels)

    raw, first, last = prep(flat, rows, cols, margin, 1, chunks - 1)
    before = lax.ppermute(last, "col", right)
    after = lax.ppermute(first, "col", left)
    xs = [None] * chunks
    smooth, near, far = [None] * chunks, [None] * chunks, [None] * chunks
    for k in range(1, chunks):
        smooth[k] = columns(k - 1, raw, before, after, tap[k], margin, False)
        far[k] = lax.ppermute(smooth[k], "row", far_pairs)
        near[k] = lax.ppermute(smooth[k], "row", near_pairs)
    mixed, first0, last0 = rows_of(head, near0, far0, tap[0], side, rows, cols, margin, True)
    before0 = lax.ppermute(last0, "col", right)
    after0 = lax.ppermute(first0, "col", left)
    for k in range(1, chunks):
        xs[k] = rows_of(smooth[k], near[k], far[k], tap[k], side, rows, cols, margin, False)
    xs[0] = columns(0, mixed, before0, after0, tap[0], margin, True)

    row_ref, col_ref = jnp.reshape(me_row, (1,)), jnp.reshape(me_col, (1,))
    pieces = exchange(gram_pieces(xs, row_ref, n_row), "row")
    if pieces[0].shape[0] % (SUB * n_col) == 0:
        small = exchange(sum_and_split(pieces, col_ref, n_col), "col")
        mine = functools.reduce(jnp.add, small)
        block = join(exchange([mine] * n_col, "col"), col_ref)
    else:
        mine = functools.reduce(jnp.add, pieces)
        block = functools.reduce(jnp.add, exchange([mine] * n_col, "col"))
    parts = exchange([block] * n_row, "row")
    out = clean(xs, parts, row_ref, start, rows, cols)
    return out.reshape(channels, rows, cols)


def solution(mesh):
    placed = (P(None, ("patch", "row"), "col"), P())
    return jax.shard_map(
        per_device,
        mesh=mesh,
        in_specs=placed,
        out_specs=P(None, ("patch", "row"), "col"),
        check_vma=False,
    )
```

time: 530 us -> 167 us (0.32)
  other arithmetic: 276 us -> 1.61 us
  waiting for transfers between devices: 131 us -> 38.2 us
  Pallas kernels: 0 us -> 79.4 us
  between operations: 57.1 us -> 0.5 us
  matrix products: 26.6 us -> 0 us
  starting transfers between devices: 13.2 us -> 36.9 us
  local copies, waits for them, and re-layouts: 25.8 us -> 9.85 us
    add x3 -> x2, other arithmetic: 239 us -> 0.87 us  [the longest x1 0.86 us: per_device(): mine = functools.reduce(jnp.add, small)]
    psum x1 -> x0, waiting for transfers between devices: 123 us -> none  [per_device(): gram_matrix = lax.psum(partial_gram, ('row', 'col'))]
    pallas_call x0 -> x14, Pallas kernels: none -> 79.4 us  [the longest x4 28.2 us: rows_of(): pl.pallas_call(functools.partial(rows_kernel, rows, cols, margin, count,...]
    reduce_sum x53 -> x0, other arithmetic: 36.6 us -> none  [the longest x36 24 us: orthonormalize(): vector = vector - jnp.sum(earlier * vector) * earlier]
    ppermute x4 -> x24, waiting for transfers between devices: 7.43 us -> 38.2 us  [the longest x12 31.8 us: exchange(): lax.ppermute(pieces[d], axis, [(i, i ^ d) for i in range(peers)])]
    dot_general x6 -> x0, matrix products: 26.6 us -> none  [the longest x1 10.8 us: per_device(): jnp.dot(flattened, flattened.T, precision=lax.Precision.HIGHEST, preferre...]
    ppermute x4 -> x24, starting transfers between devices: 13.2 us -> 36.9 us  [the longest x12 13 us: exchange(): lax.ppermute(pieces[d], axis, [(i, i ^ d) for i in range(peers)])]
    ppermute x2 -> x0, local copies, waits for them, and re-layouts: 7.28 us -> none  [the longest x1 3.65 us: padded(): before = lax.ppermute(last, axis, up)]
  transfers between devices with their start and end apart: 5 -> 24, of which waited for: 3 -> 10; matrix products, arithmetic and copies ran while one was open for 3% -> 3% of each run, Pallas kernels for 0% -> 27%
where the time goes in v1:
time: 167 us; the launch traced here: 166 us
  Pallas kernels  79.4 us (48%)
  waiting for transfers between devices  38.2 us (23%)
  starting transfers between devices  36.9 us (22%)
  local copies, waits for them, and re-layouts  9.85 us (6%)
    ppermute x12, waiting for transfers between devices, exchange(): lax.ppermute(pieces[d], axis, [(i, i ^ d) for i in range(peers)])  31.8 us
    pallas_call x4, Pallas kernels, rows_of(): pl.pallas_call(functools.partial(rows_kernel, rows, cols, margin, count,...  28.2 us
    pallas_call x4, Pallas kernels, columns(): pl.pallas_call(functools.partial(columns_kernel, which, rows, cols, margi...  22.2 us
    ppermute x12, starting transfers between devices, exchange(): lax.ppermute(pieces[d], axis, [(i, i ^ d) for i in range(peers)])  13 us
    pallas_call x1, Pallas kernels, clean(): pl.pallas_call(functools.partial(clean_kernel, chunks, peers, rows, cols)...  12.5 us
    ppermute x3, starting transfers between devices, per_device(): near[k] = lax.ppermute(smooth[k], 'row', near_pairs)  6.15 us
    unnamed x40, local copies, waits for them, and re-layouts  5.72 us
    pallas_call x1, Pallas kernels, gram_pieces(): pl.pallas_call(functools.partial(gram_kernel, chunks, peers), in_specs=[S...  5.54 us
  transfers between devices with their start and end apart: 24, of which 10 were waited for; matrix products, arithmetic and copies ran while one was open for 3% of the time, Pallas kernels for 27%

profile of v1, /device:TPU:0, one launch (start us, length us, event | category | flops | bytes accessed | tf_op | source)
XLA Modules:
  0.0 166.4 jit_solution(221531739274204740)
XLA Ops:
  0.0 5.1 %prep.1 = (f32[3,16,128,128]{3,2,1,0:T(8,128)}, f32[3,16,16,128]{3,2,1,0:T(8,128)}, f32[3,16,16,128]{3,2,1,0:T(8,128)}) custom-call(f32[8192,128]{1,0:T(8,128)} %bitcast.18), custom_call_target="tpu_custom_call" | custom-call | flops 12000000 | bytes 7500000 | tf_op jit(solution)/shard_map/prep/pallas_call | solution.py:87
  5.1 5.0 %collective-permute-start.4 = (f32[3,16,16,128]{3,2,1,0:T(8,128)}, f32[3,16,16,128]{3,2,1,0:T(8,128)S(1)}, u32[]{:S(2)}, u32[]{:S(2)}) collective-permute-start(f32[3,16,16,128]{3,2,1,0:T(8,128)} %get-tuple-element.23), channel_id=1, source_target_pairs={{0,1},{1,2},{2,3},{4,5},{5,6},{6,7},{8,9},{9,10},{10,11},{12,13},{... | collective-permute-start | bytes 1179656 | tf_op jit(solution)/shard_map/ppermute | solution.py:438
  10.1 1.3 collective-permute-start.5
  11.4 1.3 slice.26
  12.7 0.7 collective-permute-start.1
  13.4 2.9 %collective-permute-start = (f32[2048,128]{1,0:T(8,128)S(1)}, f32[2048,128]{1,0:T(8,128)}, u32[]{:S(2)}, u32[]{:S(2)}) collective-permute-start(f32[2048,128]{1,0:T(8,128)S(1)} %bitcast.20), channel_id=1, source_target_pairs={{0,4},{4,0},{8,12},{12,8},{1,5},{5,1},{9,13},{13,9},{2,6},{6,2},{1... | collective-permute-start | bytes 3145736 | tf_op jit(solution)/shard_map/ppermute | solution.py:430
  16.3 2.4 %collective-permute-done.4.before_ref = f32[3,16,16,128]{3,2,1,0:T(8,128)S(1)} collective-permute-done((f32[3,16,16,128]{3,2,1,0:T(8,128)}, f32[3,16,16,128]{3,2,1,0:T(8,128)S(1)}, u32[]{:S(2)}, u32[]{:S(2)}) %collective-permute-start.4) | collective-permute-done | bytes 393248 | tf_op jit(solution)/shard_map/ppermute | solution.py:438
  18.7 4.0 %collective-permute-done.5.after_ref = f32[3,16,16,128]{3,2,1,0:T(8,128)S(1)} collective-permute-done((f32[3,16,16,128]{3,2,1,0:T(8,128)}, f32[3,16,16,128]{3,2,1,0:T(8,128)S(1)}, u32[]{:S(2)}, u32[]{:S(2)}) %collective-permute-start.5) | collective-permute-done | bytes 393248 | tf_op jit(solution)/shard_map/ppermute | solution.py:439
  23.5 5.4 %columns.5.x_ref = f32[16,128,128]{2,1,0:T(8,128)} custom-call(f32[3,16,128,128]{3,2,1,0:T(8,128)} %get-tuple-element.22.x_ref, f32[3,16,16,128]{3,2,1,0:T(8,128)} %copy-done.1, f32[3,16,16,128]{3,2,1,0:T(8,128)} %copy-done.2, f32[33,8,128]{2,1,0:T(8,128)} %broadcast_in_dim.24.taps_ref), custom_call_target="tpu_custom_call" | custom-call | flops 20000000 | bytes 2500000 | tf_op jit(solution)/shard_map/columns/pallas_call | solution.py:127
  29.0 0.7 collective-permute-start.7
  29.8 0.8 broadcast_in_dim.22.taps_ref
  30.8 7.6 %rows_raw.1 = (f32[1,16,128,128]{3,2,1,0:T(8,128)}, f32[1,16,16,128]{3,2,1,0:T(8,128)}, f32[1,16,16,128]{3,2,1,0:T(8,128)}) custom-call(s32[1]{0:T(128)} %bitcast.1.side_ref, f32[2048,128]{1,0:T(8,128)} %bitcast.21, f32[2048,128]{1,0:T(8,128)} %collective-permute-done.near_ref, f32[2048,128]{1,0:T(8,128)} %copy-done.4, f32[33,8,128]{2,1,0:T(8,128)} %broadcast_in_dim.22.taps_ref), custom_call_target="tpu_custom_call" | custom-call | flops 20000000 | bytes 4000000 | tf_op jit(solution)/shard_map/rows_raw/pallas_call | solution.py:180
  38.4 3.5 %collective-permute-start.2 = (f32[1,16,16,128]{3,2,1,0:T(8,128)}, f32[1,16,16,128]{3,2,1,0:T(8,128)S(1)}, u32[]{:S(2)}, u32[]{:S(2)}) collective-permute-start(f32[1,16,16,128]{3,2,1,0:T(8,128)} %get-tuple-element.20), channel_id=1, source_target_pairs={{0,1},{1,2},{2,3},{4,5},{5,6},{6,7},{8,9},{9,10},{10,11},{12,13},{... | collective-permute-start | bytes 393224 | tf_op jit(solution)/shard_map/ppermute | solution.py:447
  41.9 1.3 collective-permute-start.3
  43.2 2.6 %collective-permute-start.6 = (f32[16,128,128]{2,1,0:T(8,128)}, f32[16,128,128]{2,1,0:T(8,128)S(1)}, u32[]{:S(2)}, u32[]{:S(2)}) collective-permute-start(f32[16,128,128]{2,1,0:T(8,128)} %columns.5.x_ref), channel_id=1, source_target_pairs={{0,4},{4,0},{8,12},{12,8},{1,5},{5,1},{9,13},{13,9},{2,6},{6,2},{1... | collective-permute-start | bytes 3145736 | tf_op jit(solution)/shard_map/ppermute | solution.py:445
  46.4 5.4 %columns.6.x_ref = f32[16,128,128]{2,1,0:T(8,128)} custom-call(f32[3,16,128,128]{3,2,1,0:T(8,128)} %get-tuple-element.22.x_ref, f32[3,16,16,128]{3,2,1,0:T(8,128)} %copy-done.1, f32[3,16,16,128]{3,2,1,0:T(8,128)} %copy-done.2, f32[33,8,128]{2,1,0:T(8,128)} %broadcast_in_dim.26.taps_ref), custom_call_target="tpu_custom_call" | custom-call | flops 20000000 | bytes 2500000 | tf_op jit(solution)/shard_map/columns/pallas_call | solution.py:127
  52.7 1.6 collective-permute-start.8
  54.9 5.5 %columns.7.x_ref = f32[16,128,128]{2,1,0:T(8,128)} custom-call(f32[3,16,128,128]{3,2,1,0:T(8,128)} %get-tuple-element.22.x_ref, f32[3,16,16,128]{3,2,1,0:T(8,128)} %copy-done.1, f32[3,16,16,128]{3,2,1,0:T(8,128)} %copy-done.2, f32[33,8,128]{2,1,0:T(8,128)} %broadcast_in_dim.28.taps_ref), custom_call_target="tpu_custom_call" | custom-call | flops 20000000 | bytes 2500000 | tf_op jit(solution)/shard_map/columns/pallas_call | solution.py:127
  60.4 1.6 collective-permute-start.11
  62.0 2.0 %collective-permute-start.10 = (f32[16,128,128]{2,1,0:T(8,128)}, f32[16,128,128]{2,1,0:T(8,128)}, u32[]{:S(2)}, u32[]{:S(2)}) collective-permute-start(f32[16,128,128]{2,1,0:T(8,128)} %columns.7.x_ref), channel_id=1, source_target_pairs={{0,4},{4,0},{8,12},{12,8},{1,5},{5,1},{9,13},{13,9},{2,6},{6,2},{1... | collective-permute-start | bytes 3145736 | tf_op jit(solution)/shard_map/ppermute | solution.py:445
  64.0 5.8 %columns.4.refs_0_ = f32[128,2048]{1,0:T(8,128)} custom-call(f32[1,16,128,128]{3,2,1,0:T(8,128)} %get-tuple-element.19.x_ref, f32[1,16,16,128]{3,2,1,0:T(8,128)} %copy-done.14, f32[1,16,16,128]{3,2,1,0:T(8,128)} %copy-done.15, f32[33,8,128]{2,1,0:T(8,128)} %broadcast_in_dim.22.taps_ref), custom_call_target="tpu_custom_call" | custom-call | flops 20000000 | bytes 2500000 | tf_op jit(solution)/shard_map/columns/pallas_call | solution.py:127
  69.9 1.0 copy-done.6
  70.9 6.9 %rows.3.refs_1_ = f32[128,2048]{1,0:T(8,128)} custom-call(s32[1]{0:T(128)} %bitcast.1.side_ref, f32[16,128,128]{2,1,0:T(8,128)} %columns.5.x_ref, f32[16,128,128]{2,1,0:T(8,128)} %copy-done.6, f32[16,128,128]{2,1,0:T(8,128)} %copy-done.3, f32[33,8,128]{2,1,0:T(8,128)} %broadcast_in_dim.24.taps_ref), custom_call_target="tpu_custom_call" | custom-call | flops 20000000 | bytes 4000000 | tf_op jit(solution)/shard_map/rows/pallas_call | solution.py:180
  77.8 0.9 copy-done.5
  78.7 6.8 %rows.4.refs_2_ = f32[128,2048]{1,0:T(8,128)} custom-call(s32[1]{0:T(128)} %bitcast.1.side_ref, f32[16,128,128]{2,1,0:T(8,128)} %columns.6.x_ref, f32[16,128,128]{2,1,0:T(8,128)} %collective-permute-done.8.near_ref, f32[16,128,128]{2,1,0:T(8,128)} %copy-done.5, f32[33,8,128]{2,1,0:T(8,128)} %broadcast_in_dim.26.taps_ref), custom_call_target="tpu_custom_call" | custom-call | flops 20000000 | bytes 4000000 | tf_op jit(solution)/shard_map/rows/pallas_call | solution.py:180
  85.6 6.8 %rows.5.refs_3_ = f32[128,2048]{1,0:T(8,128)} custom-call(s32[1]{0:T(128)} %bitcast.1.side_ref, f32[16,128,128]{2,1,0:T(8,128)} %columns.7.x_ref, f32[16,128,128]{2,1,0:T(8,128)} %collective-permute-done.10.near_ref, f32[16,128,128]{2,1,0:T(8,128)} %collective-permute-done.11.far_ref, f32[33,8,128]{2,1,0:T(8,128)} %broadcast_in_dim.28.taps_ref), custom_call_target="tpu_custom_call" | custom-call | flops 20000000 | bytes 4000000 | tf_op jit(solution)/shard_map/rows/pallas_call | solution.py:180
  92.4 5.5 %gram.1 = (f32[128,512]{1,0:T(8,128)}, f32[128,512]{1,0:T(8,128)}, f32[128,512]{1,0:T(8,128)}, f32[128,512]{1,0:T(8,128)}) custom-call(s32[1]{0:T(128)} %bitcast.me_ref, f32[128,2048]{1,0:T(8,128)} %columns.4.refs_0_, f32[128,2048]{1,0:T(8,128)} %rows.3.refs_1_, f32[128,2048]{1,0:T(8,128)} %rows.4.refs_2_, f32[128,2048]{1,0:T(8,128)} %rows.5.refs_3_), custom_call_target="tpu_custom_call" | custom-call | flops 4000000000 | bytes 5000000 | tf_op jit(solution)/shard_map/gram/pallas_call | solution.py:217
  98.7 1.2 collective-permute-start.14
  99.9 7.7 %collective-permute-done.13.refs_2_ = f32[128,512]{1,0:T(8,128)S(1)} collective-permute-done((f32[128,512]{1,0:T(8,128)}, f32[128,512]{1,0:T(8,128)S(1)}, u32[]{:S(2)}, u32[]{:S(2)}) %collective-permute-start.13) | collective-permute-done | bytes 262176 | tf_op jit(solution)/shard_map/ppermute | solution.py:282
  107.6 4.3 %collective-permute-done.14.refs_3_ = f32[128,512]{1,0:T(8,128)S(1)} collective-permute-done((f32[128,512]{1,0:T(8,128)}, f32[128,512]{1,0:T(8,128)S(1)}, u32[]{:S(2)}, u32[]{:S(2)}) %collective-permute-start.14) | collective-permute-done | bytes 262176 | tf_op jit(solution)/shard_map/ppermute | solution.py:282
  112.6 2.0 %sum_and_split.1 = (f32[32,512]{1,0:T(8,128)}, f32[32,512]{1,0:T(8,128)}, f32[32,512]{1,0:T(8,128)}, f32[32,512]{1,0:T(8,128)}) custom-call(s32[1]{0:T(128)} %bitcast.10.me_ref, f32[128,512]{1,0:T(8,128)} %get-tuple-element.25.refs_0_, f32[128,512]{1,0:T(8,128)} %copy-done.11, f32[128,512]{1,0:T(8,128)} %copy-done.12, f32[128,512]{1,0:T(8,128)} %copy-done.13), custom_call_target="tpu_custom_call" | custom-call | tf_op jit(solution)/shard_map/sum_and_split/pallas_call | solution.py:248
  114.6 2.4 %collective-permute-start.15 = (f32[32,512]{1,0:T(8,128)}, f32[32,512]{1,0:T(8,128)S(1)}, u32[]{:S(2)}, u32[]{:S(2)}) collective-permute-start(f32[32,512]{1,0:T(8,128)} %get-tuple-element.30), channel_id=1, source_target_pairs={{0,1},{1,0},{2,3},{3,2},{4,5},{5,4},{6,7},{7,6},{8,9},{9,8},{10,11... | collective-permute-start | bytes 196616 | tf_op jit(solution)/shard_map/ppermute | solution.py:282
  116.9 1.3 collective-permute-start.16
  118.3 1.2 collective-permute-start.17
  119.9 5.7 %collective-permute-done.16 = f32[32,512]{1,0:T(8,128)S(1)} collective-permute-done((f32[32,512]{1,0:T(8,128)}, f32[32,512]{1,0:T(8,128)S(1)}, u32[]{:S(2)}, u32[]{:S(2)}) %collective-permute-start.16) | collective-permute-done | bytes 65568 | tf_op jit(solution)/shard_map/ppermute | solution.py:282
  125.6 0.9 add_add_fusion.refs_0_
  126.4 2.2 %collective-permute-start.20 = (f32[32,512]{1,0:T(8,128)S(1)}, f32[32,512]{1,0:T(8,128)S(1)}, u32[]{:S(2)}, u32[]{:S(2)}) collective-permute-start(f32[32,512]{1,0:T(8,128)S(1)} %add_add_fusion.refs_0_), channel_id=1, source_target_pairs={{0,3},{1,2},{2,1},{3,0},{4,7},{5,6},{6,5},{7,4},{8,11},{9,10},{10,... | collective-permute-start | bytes 196616 | tf_op jit(solution)/shard_map/ppermute | solution.py:282
  128.7 0.8 collective-permute-start.19
  129.5 1.4 collective-permute-start.18
  130.9 2.5 %collective-permute-done.20.refs_3_ = f32[32,512]{1,0:T(8,128)S(1)} collective-permute-done((f32[32,512]{1,0:T(8,128)S(1)}, f32[32,512]{1,0:T(8,128)S(1)}, u32[]{:S(2)}, u32[]{:S(2)}) %collective-permute-start.20) | collective-permute-done | bytes 65568 | tf_op jit(solution)/shard_map/ppermute | solution.py:282
  133.4 1.9 %collective-permute-done.19.refs_2_ = f32[32,512]{1,0:T(8,128)S(1)} collective-permute-done((f32[32,512]{1,0:T(8,128)S(1)}, f32[32,512]{1,0:T(8,128)S(1)}, u32[]{:S(2)}, u32[]{:S(2)}) %collective-permute-start.19) | collective-permute-done | bytes 65568 | tf_op jit(solution)/shard_map/ppermute | solution.py:282
  136.6 1.7 join.1.refs_4_
  138.3 1.2 collective-permute-start.22
  140.1 0.7 multiply_cosine_fusion.cosine_ref
  140.9 2.2 %start_basis.1.start_ref = f32[8,512]{1,0:T(8,128)} custom-call(f32[4,512]{1,0:T(4,128)} %multiply_cosine_fusion.cosine_ref), custom_call_target="tpu_custom_call" | custom-call | tf_op jit(solution)/shard_map/start_basis/pallas_call | solution.py:317
  143.1 4.0 %collective-permute-done.23.refs_7_ = f32[128,512]{1,0:T(8,128)S(1)} collective-permute-done((f32[128,512]{1,0:T(8,128)}, f32[128,512]{1,0:T(8,128)S(1)}, u32[]{:S(2)}, u32[]{:S(2)}) %collective-permute-start.23) | collective-permute-done | bytes 262176 | tf_op jit(solution)/shard_map/ppermute | solution.py:282
  147.1 5.2 %collective-permute-done.22.refs_6_ = f32[128,512]{1,0:T(8,128)S(1)} collective-permute-done((f32[128,512]{1,0:T(8,128)}, f32[128,512]{1,0:T(8,128)S(1)}, u32[]{:S(2)}, u32[]{:S(2)}) %collective-permute-start.22) | collective-permute-done | bytes 262176 | tf_op jit(solution)/shard_map/ppermute | solution.py:282
  153.7 12.5 %clean.1 = f32[8192,128]{1,0:T(8,128)} custom-call(s32[1]{0:T(128)} %bitcast.me_ref, f32[8,512]{1,0:T(8,128)} %start_basis.1.start_ref, f32[128,2048]{1,0:T(8,128)} %columns.4.refs_0_, f32[128,2048]{1,0:T(8,128)} %rows.3.refs_1_, f32[128,2048]{1,0:T(8,128)} %rows.4.refs_2_, f32[128,2048]{1,0:T(8,128)} %rows.5.refs_3_, f32[128,512]{1,0:T(8,128)} %join.1.refs_4_, ...), custom_call_target="tpu_custom_call" | custom-call | flops 40000000 | bytes 9000000 | tf_op jit(solution)/shard_map/clean/pallas_call | solution.py:394
  (66 shorter events, 8.5 us)
Async XLA Ops:
  0.0 16.3 %copy-start.16 = (f32[512,33]{0,1:T(8,128)S(1)}, f32[512,33]{0,1:T(8,128)}, u32[]{:S(2)}) copy-start(f32[512,33]{0,1:T(8,128)} %param.3) | copy-start | bytes 202756
  5.1 13.6 %collective-permute-start.4 = (f32[3,16,16,128]{3,2,1,0:T(8,128)}, f32[3,16,16,128]{3,2,1,0:T(8,128)S(1)}, u32[]{:S(2)}, u32[]{:S(2)}) collective-permute-start(f32[3,16,16,128]{3,2,1,0:T(8,128)} %get-tuple-element.23), channel_id=1, source_target_pairs={{0,1},{1,2},{2,3},{4,5},{5,6},{6,7},{8,9},{9,10},{10,11},{12,13},{... | collective-permute-start | bytes 1179656 | tf_op jit(solution)/shard_map/ppermute | solution.py:438
  10.1 12.7 %collective-permute-start.5 = (f32[3,16,16,128]{3,2,1,0:T(8,128)}, f32[3,16,16,128]{3,2,1,0:T(8,128)S(1)}, u32[]{:S(2)}, u32[]{:S(2)}) collective-permute-start(f32[3,16,16,128]{3,2,1,0:T(8,128)} %get-tuple-element.24), channel_id=1, source_target_pairs={{1,0},{2,1},{3,2},{5,4},{6,5},{7,6},{9,8},{10,9},{11,10},{13,12},{... | collective-permute-start | bytes 1179656 | tf_op jit(solution)/shard_map/ppermute | solution.py:439
  12.7 17.9 %copy-start = (f32[128,16,128]{2,1,0:T(8,128)}, f32[128,16,128]{2,1,0:T(8,128)S(1)}, u32[]{:S(2)}) copy-start(f32[128,16,128]{2,1,0:T(8,128)S(1)} %slice.26) | copy-start | bytes 3145732
  12.7 17.1 %collective-permute-start.1 = (f32[2048,128]{1,0:T(8,128)S(1)}, f32[2048,128]{1,0:T(8,128)S(1)}, u32[]{:S(2)}, u32[]{:S(2)}) collective-permute-start(f32[2048,128]{1,0:T(8,128)S(1)} %bitcast.19), channel_id=1, source_target_pairs={{4,8},{8,4},{5,9},{9,5},{6,10},{10,6},{7,11},{11,7},{20,24},{24,20... | collective-permute-start | bytes 3145736 | tf_op jit(solution)/shard_map/ppermute | solution.py:429
  13.4 16.4 %collective-permute-start = (f32[2048,128]{1,0:T(8,128)S(1)}, f32[2048,128]{1,0:T(8,128)}, u32[]{:S(2)}, u32[]{:S(2)}) collective-permute-start(f32[2048,128]{1,0:T(8,128)S(1)} %bitcast.20), channel_id=1, source_target_pairs={{0,4},{4,0},{8,12},{12,8},{1,5},{5,1},{9,13},{13,9},{2,6},{6,2},{1... | collective-permute-start | bytes 3145736 | tf_op jit(solution)/shard_map/ppermute | solution.py:430
  18.7 4.7 %copy-start.1 = (f32[3,16,16,128]{3,2,1,0:T(8,128)}, f32[3,16,16,128]{3,2,1,0:T(8,128)S(1)}, u32[]{:S(2)}) copy-start(f32[3,16,16,128]{3,2,1,0:T(8,128)S(1)} %collective-permute-done.4.before_ref) | copy-start | bytes 1179652
  22.7 0.8 copy-start.2
  29.0 33.1 %collective-permute-start.7 = (f32[16,128,128]{2,1,0:T(8,128)}, f32[16,128,128]{2,1,0:T(8,128)S(1)}, u32[]{:S(2)}, u32[]{:S(2)}) collective-permute-start(f32[16,128,128]{2,1,0:T(8,128)} %columns.5.x_ref), channel_id=1, source_target_pairs={{4,8},{8,4},{5,9},{9,5},{6,10},{10,6},{7,11},{11,7},{20,24},{24,20... | collective-permute-start | bytes 3145736 | tf_op jit(solution)/shard_map/ppermute | solution.py:444
  29.7 1.1 copy-start.4
  38.4 14.2 %collective-permute-start.2 = (f32[1,16,16,128]{3,2,1,0:T(8,128)}, f32[1,16,16,128]{3,2,1,0:T(8,128)S(1)}, u32[]{:S(2)}, u32[]{:S(2)}) collective-permute-start(f32[1,16,16,128]{3,2,1,0:T(8,128)} %get-tuple-element.20), channel_id=1, source_target_pairs={{0,1},{1,2},{2,3},{4,5},{5,6},{6,7},{8,9},{9,10},{10,11},{12,13},{... | collective-permute-start | bytes 393224 | tf_op jit(solution)/shard_map/ppermute | solution.py:447
  41.9 18.5 %collective-permute-start.3 = (f32[1,16,16,128]{3,2,1,0:T(8,128)}, f32[1,16,16,128]{3,2,1,0:T(8,128)S(1)}, u32[]{:S(2)}, u32[]{:S(2)}) collective-permute-start(f32[1,16,16,128]{3,2,1,0:T(8,128)} %get-tuple-element.21), channel_id=1, source_target_pairs={{1,0},{2,1},{3,2},{5,4},{6,5},{7,6},{9,8},{10,9},{11,10},{13,12},{... | collective-permute-start | bytes 393224 | tf_op jit(solution)/shard_map/ppermute | solution.py:448
  43.2 26.7 %collective-permute-start.6 = (f32[16,128,128]{2,1,0:T(8,128)}, f32[16,128,128]{2,1,0:T(8,128)S(1)}, u32[]{:S(2)}, u32[]{:S(2)}) collective-permute-start(f32[16,128,128]{2,1,0:T(8,128)} %columns.5.x_ref), channel_id=1, source_target_pairs={{0,4},{4,0},{8,12},{12,8},{1,5},{5,1},{9,13},{13,9},{2,6},{6,2},{1... | collective-permute-start | bytes 3145736 | tf_op jit(solution)/shard_map/ppermute | solution.py:445
  51.9 25.8 %collective-permute-start.9 = (f32[16,128,128]{2,1,0:T(8,128)}, f32[16,128,128]{2,1,0:T(8,128)S(1)}, u32[]{:S(2)}, u32[]{:S(2)}) collective-permute-start(f32[16,128,128]{2,1,0:T(8,128)} %columns.6.x_ref), channel_id=1, source_target_pairs={{4,8},{8,4},{5,9},{9,5},{6,10},{10,6},{7,11},{11,7},{20,24},{24,20... | collective-permute-start | bytes 3145736 | tf_op jit(solution)/shard_map/ppermute | solution.py:444
  52.6 11.4 %copy-start.14 = (f32[1,16,16,128]{3,2,1,0:T(8,128)}, f32[1,16,16,128]{3,2,1,0:T(8,128)S(1)}, u32[]{:S(2)}) copy-start(f32[1,16,16,128]{3,2,1,0:T(8,128)S(1)} %collective-permute-done.2.before_ref) | copy-start | bytes 393220
  52.7 25.1 %collective-permute-start.8 = (f32[16,128,128]{2,1,0:T(8,128)}, f32[16,128,128]{2,1,0:T(8,128)}, u32[]{:S(2)}, u32[]{:S(2)}) collective-permute-start(f32[16,128,128]{2,1,0:T(8,128)} %columns.6.x_ref), channel_id=1, source_target_pairs={{0,4},{4,0},{8,12},{12,8},{1,5},{5,1},{9,13},{13,9},{2,6},{6,2},{1... | collective-permute-start | bytes 3145736 | tf_op jit(solution)/shard_map/ppermute | solution.py:445
  60.4 3.7 %copy-start.15 = (f32[1,16,16,128]{3,2,1,0:T(8,128)}, f32[1,16,16,128]{3,2,1,0:T(8,128)S(1)}, u32[]{:S(2)}) copy-start(f32[1,16,16,128]{3,2,1,0:T(8,128)S(1)} %collective-permute-done.3.after_ref) | copy-start | bytes 393220
  60.4 25.2 %collective-permute-start.11 = (f32[16,128,128]{2,1,0:T(8,128)}, f32[16,128,128]{2,1,0:T(8,128)}, u32[]{:S(2)}, u32[]{:S(2)}) collective-permute-start(f32[16,128,128]{2,1,0:T(8,128)} %columns.7.x_ref), channel_id=1, source_target_pairs={{4,8},{8,4},{5,9},{9,5},{6,10},{10,6},{7,11},{11,7},{20,24},{24,20... | collective-permute-start | bytes 3145736 | tf_op jit(solution)/shard_map/ppermute | solution.py:444
  62.0 7.8 %copy-start.3 = (f32[16,128,128]{2,1,0:T(8,128)}, f32[16,128,128]{2,1,0:T(8,128)S(1)}, u32[]{:S(2)}) copy-start(f32[16,128,128]{2,1,0:T(8,128)S(1)} %collective-permute-done.7.far_ref) | copy-start | bytes 3145732
  62.0 23.5 %collective-permute-start.10 = (f32[16,128,128]{2,1,0:T(8,128)}, f32[16,128,128]{2,1,0:T(8,128)}, u32[]{:S(2)}, u32[]{:S(2)}) collective-permute-start(f32[16,128,128]{2,1,0:T(8,128)} %columns.7.x_ref), channel_id=1, source_target_pairs={{0,4},{4,0},{8,12},{12,8},{1,5},{5,1},{9,13},{13,9},{2,6},{6,2},{1... | collective-permute-start | bytes 3145736 | tf_op jit(solution)/shard_map/ppermute | solution.py:445
  69.9 1.0 copy-start.6
  77.8 1.0 copy-start.5
  98.0 1.9 %collective-permute-start.12 = (f32[128,512]{1,0:T(8,128)}, f32[128,512]{1,0:T(8,128)S(1)}, u32[]{:S(2)}, u32[]{:S(2)}) collective-permute-start(f32[128,512]{1,0:T(8,128)} %get-tuple-element.26), channel_id=1, source_target_pairs={{0,4},{4,0},{8,12},{12,8},{1,5},{5,1},{9,13},{13,9},{2,6},{6,2},{1... | collective-permute-start | bytes 786440 | tf_op jit(solution)/shard_map/ppermute | solution.py:282
  98.2 9.4 %collective-permute-start.13 = (f32[128,512]{1,0:T(8,128)}, f32[128,512]{1,0:T(8,128)S(1)}, u32[]{:S(2)}, u32[]{:S(2)}) collective-permute-start(f32[128,512]{1,0:T(8,128)} %get-tuple-element.27), channel_id=1, source_target_pairs={{0,8},{4,12},{8,0},{12,4},{1,9},{5,13},{9,1},{13,5},{2,10},{6,14},... | collective-permute-start | bytes 786440 | tf_op jit(solution)/shard_map/ppermute | solution.py:282
  98.7 13.2 %collective-permute-start.14 = (f32[128,512]{1,0:T(8,128)}, f32[128,512]{1,0:T(8,128)S(1)}, u32[]{:S(2)}, u32[]{:S(2)}) collective-permute-start(f32[128,512]{1,0:T(8,128)} %get-tuple-element.28), channel_id=1, source_target_pairs={{0,12},{4,8},{8,4},{12,0},{1,13},{5,9},{9,5},{13,1},{2,14},{6,10},... | collective-permute-start | bytes 786440 | tf_op jit(solution)/shard_map/ppermute | solution.py:282
  99.9 12.0 %copy-start.11 = (f32[128,512]{1,0:T(8,128)}, f32[128,512]{1,0:T(8,128)S(1)}, u32[]{:S(2)}) copy-start(f32[128,512]{1,0:T(8,128)S(1)} %collective-permute-done.12.refs_1_) | copy-start | bytes 786436
  107.6 4.3 %copy-start.12 = (f32[128,512]{1,0:T(8,128)}, f32[128,512]{1,0:T(8,128)S(1)}, u32[]{:S(2)}) copy-start(f32[128,512]{1,0:T(8,128)S(1)} %collective-permute-done.13.refs_2_) | copy-start | bytes 786436
  111.9 0.7 copy-start.13
  114.6 5.3 %collective-permute-start.15 = (f32[32,512]{1,0:T(8,128)}, f32[32,512]{1,0:T(8,128)S(1)}, u32[]{:S(2)}, u32[]{:S(2)}) collective-permute-start(f32[32,512]{1,0:T(8,128)} %get-tuple-element.30), channel_id=1, source_target_pairs={{0,1},{1,0},{2,3},{3,2},{4,5},{5,4},{6,7},{7,6},{8,9},{9,8},{10,11... | collective-permute-start | bytes 196616 | tf_op jit(solution)/shard_map/ppermute | solution.py:282
  116.9 8.6 %collective-permute-start.16 = (f32[32,512]{1,0:T(8,128)}, f32[32,512]{1,0:T(8,128)S(1)}, u32[]{:S(2)}, u32[]{:S(2)}) collective-permute-start(f32[32,512]{1,0:T(8,128)} %get-tuple-element.31), channel_id=1, source_target_pairs={{0,2},{1,3},{2,0},{3,1},{4,6},{5,7},{6,4},{7,5},{8,10},{9,11},{10,... | collective-permute-start | bytes 196616 | tf_op jit(solution)/shard_map/ppermute | solution.py:282
  118.3 7.3 %collective-permute-start.17 = (f32[32,512]{1,0:T(8,128)}, f32[32,512]{1,0:T(8,128)S(1)}, u32[]{:S(2)}, u32[]{:S(2)}) collective-permute-start(f32[32,512]{1,0:T(8,128)} %get-tuple-element.32), channel_id=1, source_target_pairs={{0,3},{1,2},{2,1},{3,0},{4,7},{5,6},{6,5},{7,4},{8,11},{9,10},{10,... | collective-permute-start | bytes 196616 | tf_op jit(solution)/shard_map/ppermute | solution.py:282
  126.4 8.9 %copy-start.10 = (f32[32,512]{1,0:T(8,128)}, f32[32,512]{1,0:T(8,128)S(1)}, u32[]{:S(2)}) copy-start(f32[32,512]{1,0:T(8,128)S(1)} %add_add_fusion.refs_0_) | copy-start | bytes 196612
  126.4 7.0 %collective-permute-start.20 = (f32[32,512]{1,0:T(8,128)S(1)}, f32[32,512]{1,0:T(8,128)S(1)}, u32[]{:S(2)}, u32[]{:S(2)}) collective-permute-start(f32[32,512]{1,0:T(8,128)S(1)} %add_add_fusion.refs_0_), channel_id=1, source_target_pairs={{0,3},{1,2},{2,1},{3,0},{4,7},{5,6},{6,5},{7,4},{8,11},{9,10},{10,... | collective-permute-start | bytes 196616 | tf_op jit(solution)/shard_map/ppermute | solution.py:282
  128.7 6.7 %collective-permute-start.19 = (f32[32,512]{1,0:T(8,128)S(1)}, f32[32,512]{1,0:T(8,128)S(1)}, u32[]{:S(2)}, u32[]{:S(2)}) collective-permute-start(f32[32,512]{1,0:T(8,128)S(1)} %add_add_fusion.refs_0_), channel_id=1, source_target_pairs={{0,2},{1,3},{2,0},{3,1},{4,6},{5,7},{6,4},{7,5},{8,10},{9,11},{10,... | collective-permute-start | bytes 196616 | tf_op jit(solution)/shard_map/ppermute | solution.py:282
  129.5 5.9 %collective-permute-start.18 = (f32[32,512]{1,0:T(8,128)S(1)}, f32[32,512]{1,0:T(8,128)S(1)}, u32[]{:S(2)}, u32[]{:S(2)}) collective-permute-start(f32[32,512]{1,0:T(8,128)S(1)} %add_add_fusion.refs_0_), channel_id=1, source_target_pairs={{0,1},{1,0},{2,3},{3,2},{4,5},{5,4},{6,7},{7,6},{8,9},{9,8},{10,11... | collective-permute-start | bytes 196616 | tf_op jit(solution)/shard_map/ppermute | solution.py:282
  133.4 1.9 %copy-start.17 = (f32[32,512]{1,0:T(8,128)}, f32[32,512]{1,0:T(8,128)S(1)}, u32[]{:S(2)}) copy-start(f32[32,512]{1,0:T(8,128)S(1)} %collective-permute-done.20.refs_3_) | copy-start | bytes 196612
  135.3 0.6 copy-start.18
  136.0 0.6 copy-start.19
  138.3 8.8 %collective-permute-start.23 = (f32[128,512]{1,0:T(8,128)}, f32[128,512]{1,0:T(8,128)S(1)}, u32[]{:S(2)}, u32[]{:S(2)}) collective-permute-start(f32[128,512]{1,0:T(8,128)} %join.1.refs_4_), channel_id=1, source_target_pairs={{0,12},{4,8},{8,4},{12,0},{1,13},{5,9},{9,5},{13,1},{2,14},{6,10},... | collective-permute-start | bytes 786440 | tf_op jit(solution)/shard_map/ppermute | solution.py:282
  138.3 13.9 %collective-permute-start.22 = (f32[128,512]{1,0:T(8,128)}, f32[128,512]{1,0:T(8,128)S(1)}, u32[]{:S(2)}, u32[]{:S(2)}) collective-permute-start(f32[128,512]{1,0:T(8,128)} %join.1.refs_4_), channel_id=1, source_target_pairs={{0,8},{4,12},{8,0},{12,4},{1,9},{5,13},{9,1},{13,5},{2,10},{6,14},... | collective-permute-start | bytes 786440 | tf_op jit(solution)/shard_map/ppermute | solution.py:282
  139.5 12.8 %collective-permute-start.21 = (f32[128,512]{1,0:T(8,128)}, f32[128,512]{1,0:T(8,128)S(1)}, u32[]{:S(2)}, u32[]{:S(2)}) collective-permute-start(f32[128,512]{1,0:T(8,128)} %join.1.refs_4_), channel_id=1, source_target_pairs={{0,4},{4,0},{8,12},{12,8},{1,5},{5,1},{9,13},{13,9},{2,6},{6,2},{1... | collective-permute-start | bytes 786440 | tf_op jit(solution)/shard_map/ppermute | solution.py:282
  147.1 5.2 %copy-start.7 = (f32[128,512]{1,0:T(8,128)}, f32[128,512]{1,0:T(8,128)S(1)}, u32[]{:S(2)}) copy-start(f32[128,512]{1,0:T(8,128)S(1)} %collective-permute-done.23.refs_7_) | copy-start | bytes 786436
  152.3 0.7 copy-start.8
  153.0 0.7 copy-start.9

commit v2 on v1

v2 whole, which is shorter than its diff:
```python
import functools

import jax
import jax.numpy as jnp
from jax import lax
from jax.experimental import pallas as pl
from jax.experimental.pallas import tpu as pltpu
from jax.sharding import PartitionSpec as P

MODES = 4
SWEEPS = 3
LANES = 128
SUB = 8

ANY = pl.BlockSpec(memory_space=pl.ANY)
VM = pl.BlockSpec(memory_space=pltpu.VMEM)
SM = pl.BlockSpec(memory_space=pltpu.SMEM)
f32 = jnp.float32


def shape(*dims):
    return jax.ShapeDtypeStruct(dims, f32)


def cost(flops, nbytes):
    return pl.CostEstimate(flops=int(flops), bytes_accessed=int(nbytes), transcendentals=0)


def row_taps(buf, taps_ref, out_ref, rows, taps, first, count):
    def body(group, carry):
        part = pl.ds(pl.multiple_of(group * SUB, SUB), SUB)
        weights = [taps_ref[a] for a in range(taps)]
        total = [None] * rows
        for r in range(rows + taps - 1):
            x = buf[r, part, :]
            for i in range(max(0, r - taps + 1), min(rows - 1, r) + 1):
                term = weights[r - i] * x
                total[i] = term if total[i] is None else total[i] + term
        for i in range(rows):
            out_ref[i, part, :] = total[i]
        return carry

    lax.fori_loop(first, first + count, body, 0)


def col_taps(buf, taps_ref, out_ref, cols, taps, first, count, step=2):
    groups = cols // SUB

    def body(block, carry):
        weights = [taps_ref[a] for a in range(taps)]
        total = {}
        for s in range(SUB * (groups - 1) + taps):
            for q in range(step):
                i = block * step + q
                x = buf[i, pl.ds(s, SUB), :]
                for g in range(groups):
                    a = s - SUB * g
                    if 0 <= a < taps:
                        term = weights[a] * x
                        total[q, g] = term if a == 0 else total[q, g] + term
                        if a == taps - 1:
                            out_ref[i, pl.ds(SUB * g, SUB), :] = total.pop((q, g))
        return carry

    lax.fori_loop(first // step, (first + count) // step, body, 0)


PARTS = 4


def start_all(pairs, sems):
    started = []
    for index, (source, target) in enumerate(pairs):
        copy = pltpu.make_async_copy(source, target, sems.at[index])
        copy.start()
        started.append(copy)
    return started


def prep_kernel(rows, cols, margin, x_ref, raw_ref, first_ref, last_ref):
    for r in range(rows):
        tile = x_ref[pl.ds(r, LANES, stride=rows), :].T
        raw_ref[0, r] = tile
        first_ref[0, r] = tile[:margin]
        last_ref[0, r] = tile[cols - margin:]


def prep(flat, rows, cols, margin, start, count):
    return pl.pallas_call(
        functools.partial(prep_kernel, rows, cols, margin),
        grid=(count,),
        in_specs=[pl.BlockSpec((LANES * rows, cols), lambda k: (k + start, 0))],
        out_specs=[
            pl.BlockSpec((1, rows, cols, LANES), lambda k: (k, 0, 0, 0)),
            pl.BlockSpec((1, rows, margin, LANES), lambda k: (k, 0, 0, 0)),
            pl.BlockSpec((1, rows, margin, LANES), lambda k: (k, 0, 0, 0)),
        ],
        out_shape=[
            shape(count, rows, cols, LANES),
            shape(count, rows, margin, LANES),
            shape(count, rows, margin, LANES),
        ],
        cost_estimate=cost(4e6 * count, 2.5e6 * count),
        name="prep",
    )(flat)


def columns_kernel(which, rows, cols, margin, taps, flip, x_ref, before_ref, after_ref, taps_ref, out_ref, buf, held, sems):
    share = rows // PARTS
    pairs = []
    for p in range(PARTS):
        part = pl.ds(p * share, share)
        pairs += [
            (x_ref.at[which, part], buf.at[part, pl.ds(margin, cols), :]),
            (before_ref.at[which, part], buf.at[part, pl.ds(0, margin), :]),
            (after_ref.at[which, part], buf.at[part, pl.ds(margin + cols, margin), :]),
        ]
    started = start_all(pairs, sems)
    for p in range(PARTS):
        for copy in started[3 * p:3 * p + 3]:
            copy.wait()
        col_taps(buf, taps_ref.at[0], held if flip else out_ref, cols, taps, p * share, share)
        if flip:
            for r in range(p * share, p * share + share):
                out_ref[:, r * cols:(r + 1) * cols] = held[r].T


def columns(which, x, before, after, wide_taps, chunk, margin, flip):
    _, rows, cols, _ = x.shape
    taps = wide_taps.shape[1]
    out = (LANES, rows * cols) if flip else (rows, cols, LANES)
    return pl.pallas_call(
        functools.partial(columns_kernel, which, rows, cols, margin, taps, flip),
        grid=(1,),
        in_specs=[ANY, ANY, ANY, pl.BlockSpec((1, taps, SUB, LANES), lambda k: (chunk, 0, 0, 0))],
        out_specs=pl.BlockSpec(out, lambda k: (0,) * len(out)),
        out_shape=shape(*out),
        scratch_shapes=[
            pltpu.VMEM((rows, cols + 2 * margin, LANES), f32),
            pltpu.VMEM((rows, cols, LANES), f32),
            pltpu.SemaphoreType.DMA((3 * PARTS,)),
        ],
        cost_estimate=cost(2e7, 2.5e6),
        name="columns",
    )(x, before, after, wide_taps)


def raw_rows_kernel(count, rows, cols, margin, taps, side_ref, x_ref, near_ref, far_ref, taps_ref, out_ref, first_ref, last_ref, buf, native, sems):
    even = side_ref[0] == 0
    near = jnp.where(even, margin + rows, 0)
    far = jnp.where(even, 0, margin + rows)
    height = LANES * rows
    pairs = []
    for n in range(count):
        part = pl.ds(n * height, height)
        for slot, source in enumerate((x_ref, near_ref, far_ref)):
            pairs.append((source.at[part], native.at[n, slot]))
    started = start_all(pairs, sems)
    for n in range(count):
        for slot, start in enumerate((margin, near, far)):
            started[3 * n + slot].wait()
            for r in range(rows):
                buf[start + r] = native[n, slot, pl.ds(r, LANES, stride=rows), :].T
        row_taps(buf, taps_ref.at[n], out_ref.at[n], rows, taps, 0, cols // SUB)
        first_ref[n] = out_ref[n, :, :margin, :]
        last_ref[n] = out_ref[n, :, cols - margin:, :]


def raw_rows(x, near, far, wide_taps, side, rows, cols, margin):
    count = x.shape[0] // (LANES * rows)
    taps = wide_taps.shape[1]
    return pl.pallas_call(
        functools.partial(raw_rows_kernel, count, rows, cols, margin, taps),
        in_specs=[SM, ANY, ANY, ANY, VM],
        out_specs=[VM] * 3,
        out_shape=[
            shape(count, rows, cols, LANES),
            shape(count, rows, margin, LANES),
            shape(count, rows, margin, LANES),
        ],
        scratch_shapes=[
            pltpu.VMEM((rows + 2 * margin, cols, LANES), f32),
            pltpu.VMEM((count, 3, LANES * rows, cols), f32),
            pltpu.SemaphoreType.DMA((3 * count,)),
        ],
        cost_estimate=cost(3e7 * count, 4e6 * count),
        name="raw_rows",
    )(side, x, near, far, wide_taps)


def rows_kernel(rows, cols, margin, taps, side_ref, x_ref, near_ref, far_ref, taps_ref, out_ref, buf, held, sems):
    even = side_ref[0] == 0
    near = jnp.where(even, margin + rows, 0)
    far = jnp.where(even, 0, margin + rows)
    share = cols // PARTS
    pairs = []
    for p in range(PARTS):
        part = pl.ds(p * share, share)
        for source, start in ((x_ref, margin), (near_ref, near), (far_ref, far)):
            pairs.append((source.at[:, part, :], buf.at[pl.ds(start, rows), part, :]))
    started = start_all(pairs, sems)
    for p in range(PARTS):
        for copy in started[3 * p:3 * p + 3]:
            copy.wait()
        row_taps(buf, taps_ref.at[0], held, rows, taps, p * share // SUB, share // SUB)
    for r in range(rows):
        out_ref[:, r * cols:(r + 1) * cols] = held[r].T


def rows_of(x, near, far, wide_taps, chunk, side, margin):
    rows, cols, _ = x.shape
    taps = wide_taps.shape[1]
    return pl.pallas_call(
        functools.partial(rows_kernel, rows, cols, margin, taps),
        grid=(1,),
        in_specs=[SM, ANY, ANY, ANY, pl.BlockSpec((1, taps, SUB, LANES), lambda k: (chunk, 0, 0, 0))],
        out_specs=pl.BlockSpec((LANES, rows * cols), lambda k: (0, 0)),
        out_shape=shape(LANES, rows * cols),
        scratch_shapes=[
            pltpu.VMEM((rows + 2 * margin, cols, LANES), f32),
            pltpu.VMEM((rows, cols, LANES), f32),
            pltpu.SemaphoreType.DMA((3 * PARTS,)),
        ],
        cost_estimate=cost(2e7, 4e6),
        name="rows",
    )(side, x, near, far, wide_taps)


def upper(chunks):
    return [(i, j) for i in range(chunks) for j in range(i, chunks)]


def gram_kernel(chunks, peers, me_ref, *refs):
    xs, outs = refs[:chunks], refs[chunks:chunks + peers]
    high, low, packed = refs[chunks + peers:]
    for k, x_ref in enumerate(xs):
        x = x_ref[...]
        h = x.astype(jnp.bfloat16)
        high[k * LANES:(k + 1) * LANES, :] = h
        low[k * LANES:(k + 1) * LANES, :] = (x - h.astype(f32)).astype(jnp.bfloat16)
    last = (((1,), (1,)), ((), ()))
    mixed = lax.dot_general(high[...], low[...], last, preferred_element_type=f32)
    gram = lax.dot_general(high[...], high[...], last, preferred_element_type=f32)
    for index, (i, j) in enumerate(upper(chunks)):
        a, b = slice(i * LANES, (i + 1) * LANES), slice(j * LANES, (j + 1) * LANES)
        packed[index * LANES:(index + 1) * LANES, :] = gram[a, b] + mixed[a, b] + mixed[b, a].T
    size = packed.shape[0] // peers
    for d in range(peers):
        piece = me_ref[0] ^ d
        outs[d][...] = packed[pl.ds(pl.multiple_of(piece * size, size), size), :]


def gram_pieces(xs, me, peers):
    chunks = len(xs)
    channels, pixels = chunks * LANES, xs[0].shape[1]
    height = len(upper(chunks)) * LANES
    return pl.pallas_call(
        functools.partial(gram_kernel, chunks, peers),
        in_specs=[SM] + [VM] * chunks,
        out_specs=[VM] * peers,
        out_shape=[shape(height // peers, LANES)] * peers,
        scratch_shapes=[
            pltpu.VMEM((channels, pixels), jnp.bfloat16),
            pltpu.VMEM((channels, pixels), jnp.bfloat16),
            pltpu.VMEM((height, LANES), f32),
        ],
        cost_estimate=cost(4e9, 5e6),
        name="gram",
    )(me, *xs)


def split_kernel(count, peers, me_ref, *refs):
    parts, outs = refs[:count], refs[count:count + peers]
    total = refs[count + peers]
    value = parts[0][...]
    for part in parts[1:]:
        value = value + part[...]
    total[...] = value
    size = total.shape[0] // peers
    for d in range(peers):
        piece = me_ref[0] ^ d
        outs[d][...] = total[pl.ds(pl.multiple_of(piece * size, size), size), :]


def sum_and_split(parts, me, peers):
    height, width = parts[0].shape
    return pl.pallas_call(
        functools.partial(split_kernel, len(parts), peers),
        in_specs=[SM] + [VM] * len(parts),
        out_specs=[VM] * peers,
        out_shape=[shape(height // peers, width)] * peers,
        scratch_shapes=[pltpu.VMEM((height, width), f32)],
        name="sum_and_split",
    )(me, *parts)


def join_kernel(peers, me_ref, *refs):
    parts, out_ref = refs[:peers], refs[peers]
    size = parts[0].shape[0]
    for d in range(peers):
        piece = me_ref[0] ^ d
        out_ref[pl.ds(pl.multiple_of(piece * size, size), size), :] = parts[d][...]


def join(parts, me):
    peers = len(parts)
    height, width = parts[0].shape
    return pl.pallas_call(
        functools.partial(join_kernel, peers),
        in_specs=[SM] + [VM] * peers,
        out_specs=VM,
        out_shape=shape(height * peers, width),
        name="join",
    )(me, *parts)


def exchange(pieces, axis):
    peers = len(pieces)
    moved = [pieces[0]]
    for d in range(1, peers):
        moved.append(lax.ppermute(pieces[d], axis, [(i, i ^ d) for i in range(peers)]))
    return moved


def dot(u, v):
    return jnp.sum(u * v, axis=1, keepdims=True)


def orthonormal_rows(block, channels):
    done, cross = [], {}
    for index, vector in enumerate(block):
        for repeat in range(2):
            factors = [dot(q, vector) for q in done]
            for j in range(index):
                for i in range(j):
                    factors[j] = factors[j] - factors[i] * cross[i, j]
            for q, factor in zip(done, factors):
                vector = vector - factor * q
        scale_mean = dot(vector, vector) / channels + 1e-06
        vector = vector / jnp.sqrt(scale_mean) / jnp.sqrt(jnp.float32(channels))
        for i, q in enumerate(done):
            cross[i, index] = dot(q, vector)
        done.append(vector)
    return done


def start_kernel(channels, cosine_ref, out_ref):
    rows = orthonormal_rows([cosine_ref[k:k + 1, :] for k in range(MODES)], channels)
    out_ref[...] = jnp.concatenate(rows + [jnp.zeros((SUB - MODES, channels), f32)], axis=0)


def start_basis(channels):
    channel_pos = jnp.arange(channels).astype(f32)
    mode_index = jnp.arange(MODES).astype(f32)
    cosine = jnp.cos(jnp.pi * mode_index[:, None] * (channel_pos[None, :] + 0.5) / channels)
    return pl.pallas_call(
        functools.partial(start_kernel, channels),
        in_specs=[VM],
        out_specs=VM,
        out_shape=shape(SUB, channels),
        name="start_basis",
    )(cosine)


def spread(basis, wide, channels):
    for c in range(0, channels, LANES):
        tall = basis[:, c:c + LANES].T
        for k in range(MODES):
            wide[k, c:c + LANES, :] = jnp.broadcast_to(tall[:, k:k + 1], (LANES, LANES))


def load_all(xs, x_buf, sems):
    return start_all([(x, x_buf.at[pl.ds(k * LANES, LANES)]) for k, x in enumerate(xs)], sems)


def project(x_buf, wide, part, channels):
    totals = [None] * MODES
    for c in range(0, channels, SUB):
        x = x_buf[c:c + SUB, part]
        for k in range(MODES):
            term = wide[k, c:c + SUB, :] * x
            totals[k] = term if totals[k] is None else totals[k] + term
    return [jnp.broadcast_to(jnp.sum(total, axis=0, keepdims=True), (SUB, LANES)) for total in totals]


def clean_kernel(chunks, peers, rows, cols, me_ref, start_ref, *refs):
    xs, pieces, out_ref = refs[:chunks], refs[chunks:chunks + peers], refs[chunks + peers]
    x_buf, packed, gram, wide, coef, out_buf, sems, out_sems = refs[chunks + peers + 1:]
    channels = chunks * LANES
    started = load_all(xs, x_buf, sems)
    size = packed.shape[0] // peers
    for d in range(peers):
        piece = me_ref[0] ^ d
        packed[pl.ds(pl.multiple_of(piece * size, size), size), :] = pieces[d][...]
    diagonal = jnp.zeros((1, LANES), f32)
    row_id = lax.broadcasted_iota(jnp.int32, (LANES, LANES), 0)
    col_id = lax.broadcasted_iota(jnp.int32, (LANES, LANES), 1)
    for index, (i, j) in enumerate(upper(chunks)):
        block = packed[index * LANES:(index + 1) * LANES, :]
        gram[i * LANES:(i + 1) * LANES, j * LANES:(j + 1) * LANES] = block
        if i != j:
            gram[j * LANES:(j + 1) * LANES, i * LANES:(i + 1) * LANES] = block.T
        else:
            diagonal = diagonal + jnp.sum(jnp.where(row_id == col_id, block, 0.0), axis=0, keepdims=True)
    scale = channels / jnp.sum(diagonal, axis=1, keepdims=True)
    basis = start_ref[...]
    for sweep in range(SWEEPS):
        spread(basis, wide, channels)
        vectors = []
        for k in range(MODES):
            row = []
            for t in range(chunks):
                lanes = slice(t * LANES, (t + 1) * LANES)
                total = None
                for c in range(0, channels, SUB):
                    term = wide[k, c:c + SUB, :] * gram[c:c + SUB, lanes]
                    total = term if total is None else total + term
                row.append(jnp.sum(total, axis=0, keepdims=True))
            vectors.append(jnp.concatenate(row, axis=1) * scale)
        new = orthonormal_rows(vectors, channels)
        basis = jnp.concatenate(new + [jnp.zeros((SUB - MODES, channels), f32)], axis=0)
    spread(basis, wide, channels)
    for copy in started:
        copy.wait()

    def coefficients(r, carry):
        values = project(x_buf, wide, pl.ds(pl.multiple_of(r * cols, cols), cols), channels)
        for k in range(MODES):
            coef[r, k] = values[k]
        return carry

    lax.fori_loop(0, rows, coefficients, 0)
    copies = []
    for n in range(chunks):
        def subtract(r, carry):
            part = pl.ds(pl.multiple_of(r * cols, cols), cols)
            factors = [coef[r, k] for k in range(MODES)]
            for c in range(n * LANES, (n + 1) * LANES, SUB):
                model = wide[0, c:c + SUB, :] * factors[0]
                for k in range(1, MODES):
                    model = model + wide[k, c:c + SUB, :] * factors[k]
                out_buf[pl.ds(c * rows + r, SUB, stride=rows), :] = x_buf[c:c + SUB, part] - model
            return carry

        lax.fori_loop(0, rows, subtract, 0)
        block = pl.ds(n * LANES * rows, LANES * rows)
        copy = pltpu.make_async_copy(out_buf.at[block], out_ref.at[block], out_sems.at[n])
        copy.start()
        copies.append(copy)
    for copy in copies:
        copy.wait()


def clean(xs, pieces, me, start, rows, cols):
    chunks, channels = len(xs), len(xs) * LANES
    return pl.pallas_call(
        functools.partial(clean_kernel, chunks, len(pieces), rows, cols),
        in_specs=[SM, VM] + [ANY] * chunks + [VM] * len(pieces),
        out_specs=ANY,
        out_shape=shape(channels * rows, cols),
        scratch_shapes=[
            pltpu.VMEM((channels, rows * cols), f32),
            pltpu.VMEM((len(upper(chunks)) * LANES, LANES), f32),
            pltpu.VMEM((channels, channels), f32),
            pltpu.VMEM((MODES, channels, LANES), f32),
            pltpu.VMEM((rows, MODES, SUB, LANES), f32),
            pltpu.VMEM((channels * rows, cols), f32),
            pltpu.SemaphoreType.DMA((chunks,)),
            pltpu.SemaphoreType.DMA((chunks,)),
        ],
        cost_estimate=cost(4e7, 9e6),
        name="clean",
    )(me, start, *xs, *pieces)


def per_device(sky_cube, beam_taps):
    taps = beam_taps.shape[1]
    margin = taps // 2
    channels, rows, cols = sky_cube.shape
    chunks = channels // LANES
    n_row, n_col = lax.axis_size("row"), lax.axis_size("col")
    me_row = lax.axis_index("row").astype(jnp.int32)
    me_col = lax.axis_index("col").astype(jnp.int32)
    side = jnp.reshape(me_row % 2, (1,))
    near_pairs = [(i, i ^ 1) for i in range(n_row)]
    far_pairs = [(i, ((i + 1) ^ 1) - 1) for i in range(1, n_row - 1)]
    right = [(i, i + 1) for i in range(n_col - 1)]
    left = [(j, i) for i, j in right]

    height = LANES * rows
    flat = sky_cube.reshape(channels * rows, cols)
    ahead = chunks // 2
    head = flat[:ahead * height]
    head, body = lax.optimization_barrier((head, flat))
    far_head = lax.ppermute(head, "row", far_pairs)
    near_head = lax.ppermute(head, "row", near_pairs)
    wide_taps = jnp.broadcast_to(
        beam_taps.T.reshape(taps, chunks, 1, LANES).transpose(1, 0, 2, 3), (chunks, taps, SUB, LANES)
    )
    start = start_basis(channels)

    raw, first, last = prep(body, rows, cols, margin, ahead, chunks - ahead)
    before = lax.ppermute(last, "col", right)
    after = lax.ppermute(first, "col", left)
    raw, wide_taps, start = lax.optimization_barrier((raw, wide_taps, start))
    xs = [None] * chunks
    smooth, near, far = [None] * chunks, [None] * chunks, [None] * chunks
    for k in range(ahead, chunks):
        smooth[k] = columns(k - ahead, raw, before, after, wide_taps, k, margin, False)
        far[k] = lax.ppermute(smooth[k], "row", far_pairs)
        near[k] = lax.ppermute(smooth[k], "row", near_pairs)
    mixed, first_head, last_head = raw_rows(head, near_head, far_head, wide_taps, side, rows, cols, margin)
    before_head = lax.ppermute(last_head, "col", right)
    after_head = lax.ppermute(first_head, "col", left)
    for k in range(ahead, chunks - 1):
        xs[k] = rows_of(smooth[k], near[k], far[k], wide_taps, k, side, margin)
    for k in range(ahead):
        xs[k] = columns(k, mixed, before_head, after_head, wide_taps, k, margin, True)
    k = chunks - 1
    xs[k] = rows_of(smooth[k], near[k], far[k], wide_taps, k, side, margin)

    row_ref, col_ref = jnp.reshape(me_row, (1,)), jnp.reshape(me_col, (1,))
    pieces = exchange(gram_pieces(xs, row_ref, n_row), "row")
    if pieces[0].shape[0] % (SUB * n_col) == 0:
        small = exchange(sum_and_split(pieces, col_ref, n_col), "col")
        mine = functools.reduce(jnp.add, small)
        block = join(exchange([mine] * n_col, "col"), col_ref)
    else:
        mine = functools.reduce(jnp.add, pieces)
        block = functools.reduce(jnp.add, exchange([mine] * n_col, "col"))
    out = clean(xs, exchange([block] * n_row, "row"), row_ref, start, rows, cols)
    return out.reshape(channels, rows, cols)


def solution(mesh):
    placed = (P(None, ("patch", "row"), "col"), P())
    return jax.shard_map(
        per_device,
        mesh=mesh,
        in_specs=placed,
        out_specs=P(None, ("patch", "row"), "col"),
        check_vma=False,
    )
```

time: 167 us -> 143 us (0.86)
  waiting for transfers between devices: 38.2 us -> 29.8 us
  Pallas kernels: 79.4 us -> 72.7 us
  starting transfers between devices: 36.9 us -> 32 us
  local copies, waits for them, and re-layouts: 9.85 us -> 6.07 us
    ppermute x12, waiting for transfers between devices: 31.8 us -> 24 us  [exchange(): lax.ppermute(pieces[d], axis, [(i, i ^ d) for i in range(peers)])]
    ppermute x3 -> x2, starting transfers between devices: 6.15 us -> 1.49 us  [per_device(): near[k] = lax.ppermute(smooth[k], 'row', near_pairs)]
    pallas_call x5 -> x4, Pallas kernels: 40.7 us -> 36.4 us  [the longest x1 12.4 us: clean(): pl.pallas_call(functools.partial(clean_kernel, chunks, len(pieces), rows,...]
    unnamed x40 -> x34, local copies, waits for them, and re-layouts: 5.72 us -> 3.47 us
    pallas_call x1, Pallas kernels: 5.07 us -> 3.09 us  [prep(): pl.pallas_call(functools.partial(prep_kernel, rows, cols, margin), grid=(...]
    broadcast_in_dim x5 -> x1, local copies, waits for them, and re-layouts: 2.8 us -> 0.85 us  [per_device(): jnp.broadcast_to(beam_taps.T.reshape(taps, chunks, 1, LANES).transpose(1,...]
  transfers between devices with their start and end apart: 24 -> 22, of which waited for: 10 -> 11; matrix products, arithmetic and copies ran while one was open for 3% -> 1% of each run, Pallas kernels for 27% -> 28%
where the time goes in v2:
time: 143 us
  Pallas kernels  72.7 us (51%)
  starting transfers between devices  32 us (22%)
  waiting for transfers between devices  29.8 us (21%)
  local copies, waits for them, and re-layouts  6.07 us (4%)
  other arithmetic  1.54 us (1%)
    ppermute x12, waiting for transfers between devices, exchange(): lax.ppermute(pieces[d], axis, [(i, i ^ d) for i in range(peers)])  24 us
    pallas_call x4, Pallas kernels, columns(): pl.pallas_call(functools.partial(columns_kernel, which, rows, cols, margi...  22.2 us
    ppermute x12, starting transfers between devices, exchange(): lax.ppermute(pieces[d], axis, [(i, i ^ d) for i in range(peers)])  13.8 us
    pallas_call x1, Pallas kernels, clean(): pl.pallas_call(functools.partial(clean_kernel, chunks, len(pieces), rows,...  12.4 us
    pallas_call x2, Pallas kernels, rows_of(): pl.pallas_call(functools.partial(rows_kernel, rows, cols, margin, taps),...  12.4 us
    pallas_call x1, Pallas kernels, raw_rows(): pl.pallas_call(functools.partial(raw_rows_kernel, count, rows, cols, marg...  11.6 us
    pallas_call x1, Pallas kernels, gram_pieces(): pl.pallas_call(functools.partial(gram_kernel, chunks, peers), in_specs=[S...  5.4 us
    ppermute x1, starting transfers between devices, per_device(): before = lax.ppermute(last, 'col', right)  4.66 us
  transfers between devices with their start and end apart: 22, of which 11 were waited for; matrix products, arithmetic and copies ran while one was open for 1% of the time, Pallas kernels for 28%

profile of v2, /device:TPU:0, one launch (start us, length us, event | category | flops | bytes accessed | tf_op | source)
XLA Modules:
  0.0 142.6 jit_solution(11356717901245732944)
XLA Ops:
  0.0 1.7 %slice.6 = f32[256,16,128]{2,1,0:T(8,128)S(1)} slice(f32[512,16,128]{2,1,0:T(8,128)} %param.2), slice={[0:256], [0:16], [0:128]} | slice | bytes 4194304 | tf_op jit(solution)/shard_map/slice | solution.py:493
  2.3 2.0 %collective-permute-start.1 = (f32[4096,128]{1,0:T(8,128)S(1)}, f32[4096,128]{1,0:T(8,128)}, u32[]{:S(2)}, u32[]{:S(2)}) collective-permute-start(f32[4096,128]{1,0:T(8,128)S(1)} %bitcast.14), channel_id=1, source_target_pairs={{4,8},{8,4},{5,9},{9,5},{6,10},{10,6},{7,11},{11,7},{20,24},{24,20... | collective-permute-start | bytes 6291464 | tf_op jit(solution)/shard_map/ppermute | solution.py:495
  4.3 3.1 %prep.1 = (f32[2,16,128,128]{3,2,1,0:T(8,128)}, f32[2,16,16,128]{3,2,1,0:T(8,128)}, f32[2,16,16,128]{3,2,1,0:T(8,128)}) custom-call(f32[8192,128]{1,0:T(8,128)} %bitcast.12), custom_call_target="tpu_custom_call" | custom-call | flops 8000000 | bytes 5000000 | tf_op jit(solution)/shard_map/prep/pallas_call | solution.py:89
  7.4 4.7 %collective-permute-start.4 = (f32[2,16,16,128]{3,2,1,0:T(8,128)}, f32[2,16,16,128]{3,2,1,0:T(8,128)S(1)}, u32[]{:S(2)}, u32[]{:S(2)}) collective-permute-start(f32[2,16,16,128]{3,2,1,0:T(8,128)} %get-tuple-element.33), channel_id=1, source_target_pairs={{0,1},{1,2},{2,3},{4,5},{5,6},{6,7},{8,9},{9,10},{10,11},{12,13},{... | collective-permute-start | bytes 786440 | tf_op jit(solution)/shard_map/ppermute | solution.py:503
  12.0 1.3 collective-permute-start.5
  13.4 0.7 multiply_cosine_fusion.cosine_ref
  14.1 2.2 %start_basis.1.start_ref = f32[8,512]{1,0:T(8,128)} custom-call(f32[4,512]{1,0:T(4,128)} %multiply_cosine_fusion.cosine_ref), custom_call_target="tpu_custom_call" | custom-call | tf_op jit(solution)/shard_map/start_basis/pallas_call | solution.py:356
  16.4 0.8 broadcast_in_dim.10.taps_ref
  17.2 1.2 collective-permute-done.4.before_ref
  18.4 4.6 %collective-permute-done.5.after_ref = f32[2,16,16,128]{3,2,1,0:T(8,128)S(1)} collective-permute-done((f32[2,16,16,128]{3,2,1,0:T(8,128)}, f32[2,16,16,128]{3,2,1,0:T(8,128)S(1)}, u32[]{:S(2)}, u32[]{:S(2)}) %collective-permute-start.5) | collective-permute-done | bytes 262176 | tf_op jit(solution)/shard_map/ppermute | solution.py:504
  23.0 0.7 copy-done.4
  23.7 5.3 %columns.7.x_ref = f32[16,128,128]{2,1,0:T(8,128)} custom-call(f32[2,16,128,128]{3,2,1,0:T(8,128)} %get-tuple-element.32.x_ref, f32[2,16,16,128]{3,2,1,0:T(8,128)} %copy-done.3, f32[2,16,16,128]{3,2,1,0:T(8,128)} %copy-done.4, f32[4,33,8,128]{3,2,1,0:T(8,128)} %broadcast_in_dim.10.taps_ref), custom_call_target="tpu_custom_call" | custom-call | flops 20000000 | bytes 2500000 | tf_op jit(solution)/shard_map/columns/pallas_call | solution.py:132
  29.3 1.6 %collective-permute-start.9 = (f32[16,128,128]{2,1,0:T(8,128)}, f32[16,128,128]{2,1,0:T(8,128)}, u32[]{:S(2)}, u32[]{:S(2)}) collective-permute-start(f32[16,128,128]{2,1,0:T(8,128)} %columns.7.x_ref), channel_id=1, source_target_pairs={{4,8},{8,4},{5,9},{9,5},{6,10},{10,6},{7,11},{11,7},{20,24},{24,20... | collective-permute-start | bytes 3145736 | tf_op jit(solution)/shard_map/ppermute | solution.py:510
  30.9 5.2 %columns.6.x_ref = f32[16,128,128]{2,1,0:T(8,128)} custom-call(f32[2,16,128,128]{3,2,1,0:T(8,128)} %get-tuple-element.32.x_ref, f32[2,16,16,128]{3,2,1,0:T(8,128)} %copy-done.3, f32[2,16,16,128]{3,2,1,0:T(8,128)} %copy-done.4, f32[4,33,8,128]{3,2,1,0:T(8,128)} %broadcast_in_dim.10.taps_ref), custom_call_target="tpu_custom_call" | custom-call | flops 20000000 | bytes 2500000 | tf_op jit(solution)/shard_map/columns/pallas_call | solution.py:132
  36.2 1.3 collective-permute-start.6
  37.5 1.6 %collective-permute-start.7 = (f32[16,128,128]{2,1,0:T(8,128)}, f32[16,128,128]{2,1,0:T(8,128)}, u32[]{:S(2)}, u32[]{:S(2)}) collective-permute-start(f32[16,128,128]{2,1,0:T(8,128)} %columns.6.x_ref), channel_id=1, source_target_pairs={{4,8},{8,4},{5,9},{9,5},{6,10},{10,6},{7,11},{11,7},{20,24},{24,20... | collective-permute-start | bytes 3145736 | tf_op jit(solution)/shard_map/ppermute | solution.py:510
  39.1 11.6 %raw_rows.1 = (f32[2,16,128,128]{3,2,1,0:T(8,128)}, f32[2,16,16,128]{3,2,1,0:T(8,128)}, f32[2,16,16,128]{3,2,1,0:T(8,128)}) custom-call(s32[1]{0:T(128)} %bitcast.6.side_ref, f32[4096,128]{1,0:T(8,128)} %bitcast.15, f32[4096,128]{1,0:T(8,128)} %collective-permute-done.near_ref, f32[4096,128]{1,0:T(8,128)} %collective-permute-done.1.far_ref, ...), custom_call_target="tpu_custom_call" | custom-call | flops 60000000 | bytes 8000000 | tf_op jit(solution)/shard_map/raw_rows/pallas_call | solution.py:172
  50.7 3.5 %collective-permute-start.2 = (f32[2,16,16,128]{3,2,1,0:T(8,128)}, f32[2,16,16,128]{3,2,1,0:T(8,128)S(1)}, u32[]{:S(2)}, u32[]{:S(2)}) collective-permute-start(f32[2,16,16,128]{3,2,1,0:T(8,128)} %get-tuple-element.30), channel_id=1, source_target_pairs={{0,1},{1,2},{2,3},{4,5},{5,6},{6,7},{8,9},{9,10},{10,11},{12,13},{... | collective-permute-start | bytes 786440 | tf_op jit(solution)/shard_map/ppermute | solution.py:513
  54.2 1.5 %collective-permute-start.3 = (f32[2,16,16,128]{3,2,1,0:T(8,128)}, f32[2,16,16,128]{3,2,1,0:T(8,128)S(1)}, u32[]{:S(2)}, u32[]{:S(2)}) collective-permute-start(f32[2,16,16,128]{3,2,1,0:T(8,128)} %get-tuple-element.31), channel_id=1, source_target_pairs={{1,0},{2,1},{3,2},{5,4},{6,5},{7,6},{9,8},{10,9},{11,10},{13,12},{... | collective-permute-start | bytes 786440 | tf_op jit(solution)/shard_map/ppermute | solution.py:514
  55.7 6.2 %rows.3.refs_3_ = f32[128,2048]{1,0:T(8,128)} custom-call(s32[1]{0:T(128)} %bitcast.6.side_ref, f32[16,128,128]{2,1,0:T(8,128)} %columns.7.x_ref, f32[16,128,128]{2,1,0:T(8,128)} %copy-done.1, f32[16,128,128]{2,1,0:T(8,128)} %collective-permute-done.9.far_ref, f32[4,33,8,128]{3,2,1,0:T(8,128)} %broadcast_in_dim.10.taps_ref), custom_call_target="tpu_custom_call" | custom-call | flops 20000000 | bytes 4000000 | tf_op jit(solution)/shard_map/rows/pallas_call | solution.py:213
  61.9 6.2 %rows.2.refs_2_ = f32[128,2048]{1,0:T(8,128)} custom-call(s32[1]{0:T(128)} %bitcast.6.side_ref, f32[16,128,128]{2,1,0:T(8,128)} %columns.6.x_ref, f32[16,128,128]{2,1,0:T(8,128)} %collective-permute-done.6.near_ref, f32[16,128,128]{2,1,0:T(8,128)} %collective-permute-done.7.far_ref, f32[4,33,8,128]{3,2,1,0:T(8,128)} %broadcast_in_dim.10.taps_ref), custom_call_target="tpu_custom_call" | custom-call | flops 20000000 | bytes 4000000 | tf_op jit(solution)/shard_map/rows/pallas_call | solution.py:213
  68.2 0.7 copy-done.2
  68.9 5.8 %columns.5.refs_1_ = f32[128,2048]{1,0:T(8,128)} custom-call(f32[2,16,128,128]{3,2,1,0:T(8,128)} %get-tuple-element.29.x_ref, f32[2,16,16,128]{3,2,1,0:T(8,128)} %copy-done.2, f32[2,16,16,128]{3,2,1,0:T(8,128)} %copy-done.5, f32[4,33,8,128]{3,2,1,0:T(8,128)} %broadcast_in_dim.10.taps_ref), custom_call_target="tpu_custom_call" | custom-call | flops 20000000 | bytes 2500000 | tf_op jit(solution)/shard_map/columns/pallas_call | solution.py:132
  74.7 5.8 %columns.4.refs_0_ = f32[128,2048]{1,0:T(8,128)} custom-call(f32[2,16,128,128]{3,2,1,0:T(8,128)} %get-tuple-element.29.x_ref, f32[2,16,16,128]{3,2,1,0:T(8,128)} %copy-done.2, f32[2,16,16,128]{3,2,1,0:T(8,128)} %copy-done.5, f32[4,33,8,128]{3,2,1,0:T(8,128)} %broadcast_in_dim.10.taps_ref), custom_call_target="tpu_custom_call" | custom-call | flops 20000000 | bytes 2500000 | tf_op jit(solution)/shard_map/columns/pallas_call | solution.py:132
  80.5 5.4 %gram.1 = (f32[320,128]{1,0:T(8,128)}, f32[320,128]{1,0:T(8,128)}, f32[320,128]{1,0:T(8,128)}, f32[320,128]{1,0:T(8,128)}) custom-call(s32[1]{0:T(128)} %bitcast.me_ref, f32[128,2048]{1,0:T(8,128)} %columns.4.refs_0_, f32[128,2048]{1,0:T(8,128)} %columns.5.refs_1_, f32[128,2048]{1,0:T(8,128)} %rows.2.refs_2_, f32[128,2048]{1,0:T(8,128)} %rows.3.refs_3_), custom_call_target="tpu_custom_call" | custom-call | flops 4000000000 | bytes 5000000 | tf_op jit(solution)/shard_map/gram/pallas_call | solution.py:257
  85.9 1.2 collective-permute-start.10
  87.2 0.8 collective-permute-start.11
  88.5 5.9 %collective-permute-done.11.refs_2_ = f32[320,128]{1,0:T(8,128)S(1)} collective-permute-done((f32[320,128]{1,0:T(8,128)}, f32[320,128]{1,0:T(8,128)S(1)}, u32[]{:S(2)}, u32[]{:S(2)}) %collective-permute-start.11) | collective-permute-done | bytes 163872 | tf_op jit(solution)/shard_map/ppermute | solution.py:321
  94.4 1.6 %collective-permute-done.12.refs_3_ = f32[320,128]{1,0:T(8,128)S(1)} collective-permute-done((f32[320,128]{1,0:T(8,128)}, f32[320,128]{1,0:T(8,128)S(1)}, u32[]{:S(2)}, u32[]{:S(2)}) %collective-permute-start.12) | collective-permute-done | bytes 163872 | tf_op jit(solution)/shard_map/ppermute | solution.py:321
  96.0 0.7 copy-done.9
  96.7 1.9 %sum_and_split.1 = (f32[80,128]{1,0:T(8,128)}, f32[80,128]{1,0:T(8,128)}, f32[80,128]{1,0:T(8,128)}, f32[80,128]{1,0:T(8,128)}) custom-call(s32[1]{0:T(128)} %bitcast.7.me_ref, f32[320,128]{1,0:T(8,128)} %get-tuple-element.35.refs_0_, f32[320,128]{1,0:T(8,128)} %copy-done.7, f32[320,128]{1,0:T(8,128)} %copy-done.8, f32[320,128]{1,0:T(8,128)} %copy-done.9), custom_call_target="tpu_custom_call" | custom-call | tf_op jit(solution)/shard_map/sum_and_split/pallas_call | solution.py:287
  98.5 2.5 %collective-permute-start.13 = (f32[80,128]{1,0:T(8,128)}, f32[80,128]{1,0:T(8,128)S(1)}, u32[]{:S(2)}, u32[]{:S(2)}) collective-permute-start(f32[80,128]{1,0:T(8,128)} %get-tuple-element.40), channel_id=1, source_target_pairs={{0,1},{1,0},{2,3},{3,2},{4,5},{5,4},{6,7},{7,6},{8,9},{9,8},{10,11... | collective-permute-start | bytes 122888 | tf_op jit(solution)/shard_map/ppermute | solution.py:321
  101.0 1.2 collective-permute-start.14
  102.2 1.3 collective-permute-start.15
  103.7 3.4 %collective-permute-done.14 = f32[80,128]{1,0:T(8,128)S(1)} collective-permute-done((f32[80,128]{1,0:T(8,128)}, f32[80,128]{1,0:T(8,128)S(1)}, u32[]{:S(2)}, u32[]{:S(2)}) %collective-permute-start.14) | collective-permute-done | bytes 40992 | tf_op jit(solution)/shard_map/ppermute | solution.py:321
  107.1 1.2 collective-permute-done.15
  108.2 0.8 add_add_fusion.refs_0_
  109.0 1.1 collective-permute-start.16
  110.1 1.4 collective-permute-start.17
  111.5 2.0 %collective-permute-start.18 = (f32[80,128]{1,0:T(8,128)S(1)}, f32[80,128]{1,0:T(8,128)S(1)}, u32[]{:S(2)}, u32[]{:S(2)}) collective-permute-start(f32[80,128]{1,0:T(8,128)S(1)} %add_add_fusion.refs_0_), channel_id=1, source_target_pairs={{0,3},{1,2},{2,1},{3,0},{4,7},{5,6},{6,5},{7,4},{8,11},{9,10},{10,... | collective-permute-start | bytes 122888 | tf_op jit(solution)/shard_map/ppermute | solution.py:321
  113.5 2.7 %collective-permute-done.17.refs_2_ = f32[80,128]{1,0:T(8,128)S(1)} collective-permute-done((f32[80,128]{1,0:T(8,128)S(1)}, f32[80,128]{1,0:T(8,128)S(1)}, u32[]{:S(2)}, u32[]{:S(2)}) %collective-permute-start.17) | collective-permute-done | bytes 40992 | tf_op jit(solution)/shard_map/ppermute | solution.py:321
  116.2 1.1 collective-permute-done.18.refs_3_
  117.9 1.5 %join.1.refs_4_ = f32[320,128]{1,0:T(8,128)} custom-call(s32[1]{0:T(128)} %bitcast.7.me_ref, f32[80,128]{1,0:T(8,128)} %copy-done.6, f32[80,128]{1,0:T(8,128)} %copy-done.14, f32[80,128]{1,0:T(8,128)} %copy-done.15, f32[80,128]{1,0:T(8,128)} %copy-done.16), custom_call_target="tpu_custom_call" | custom-call | tf_op jit(solution)/shard_map/join/pallas_call | solution.py:308
  119.5 1.7 %collective-permute-start.20 = (f32[320,128]{1,0:T(8,128)}, f32[320,128]{1,0:T(8,128)S(1)}, u32[]{:S(2)}, u32[]{:S(2)}) collective-permute-start(f32[320,128]{1,0:T(8,128)} %join.1.refs_4_), channel_id=1, source_target_pairs={{0,8},{4,12},{8,0},{12,4},{1,9},{5,13},{9,1},{13,5},{2,10},{6,14},... | collective-permute-start | bytes 491528 | tf_op jit(solution)/shard_map/ppermute | solution.py:321
  121.3 5.4 %collective-permute-done.20.refs_6_ = f32[320,128]{1,0:T(8,128)S(1)} collective-permute-done((f32[320,128]{1,0:T(8,128)}, f32[320,128]{1,0:T(8,128)S(1)}, u32[]{:S(2)}, u32[]{:S(2)}) %collective-permute-start.20) | collective-permute-done | bytes 163872 | tf_op jit(solution)/shard_map/ppermute | solution.py:321
  126.7 2.6 %collective-permute-done.21.refs_7_ = f32[320,128]{1,0:T(8,128)S(1)} collective-permute-done((f32[320,128]{1,0:T(8,128)}, f32[320,128]{1,0:T(8,128)S(1)}, u32[]{:S(2)}, u32[]{:S(2)}) %collective-permute-start.21) | collective-permute-done | bytes 163872 | tf_op jit(solution)/shard_map/ppermute | solution.py:321
  129.3 0.7 copy-done.12
  130.0 12.4 %clean.1 = f32[8192,128]{1,0:T(8,128)} custom-call(s32[1]{0:T(128)} %bitcast.me_ref, f32[8,512]{1,0:T(8,128)} %start_basis.1.start_ref, f32[128,2048]{1,0:T(8,128)} %columns.4.refs_0_, f32[128,2048]{1,0:T(8,128)} %columns.5.refs_1_, f32[128,2048]{1,0:T(8,128)} %rows.2.refs_2_, f32[128,2048]{1,0:T(8,128)} %rows.3.refs_3_, f32[320,128]{1,0:T(8,128)} %join.1.refs_4_, ...), custom_call_target="tpu_custom_call" | custom-call | flops 40000000 | bytes 9000000 | tf_op jit(solution)/shard_map/clean/pallas_call | solution.py:456
  (51 shorter events, 2.5 us)
Async XLA Ops:
  1.7 5.6 %copy-start = (f32[256,16,128]{2,1,0:T(8,128)}, f32[256,16,128]{2,1,0:T(8,128)S(1)}, u32[]{:S(2)}) copy-start(f32[256,16,128]{2,1,0:T(8,128)S(1)} %slice.6) | copy-start | bytes 6291460
  1.7 11.6 %copy-start.13 = (f32[512,33]{0,1:T(8,128)S(1)}, f32[512,33]{0,1:T(8,128)}, u32[]{:S(2)}) copy-start(f32[512,33]{0,1:T(8,128)} %param.3) | copy-start | bytes 202756
  1.8 35.7 %collective-permute-start = (f32[4096,128]{1,0:T(8,128)S(1)}, f32[4096,128]{1,0:T(8,128)}, u32[]{:S(2)}, u32[]{:S(2)}) collective-permute-start(f32[4096,128]{1,0:T(8,128)S(1)} %bitcast.13), channel_id=1, source_target_pairs={{0,4},{4,0},{8,12},{12,8},{1,5},{5,1},{9,13},{13,9},{2,6},{6,2},{1... | collective-permute-start | bytes 6291464 | tf_op jit(solution)/shard_map/ppermute | solution.py:496
  2.3 36.8 %collective-permute-start.1 = (f32[4096,128]{1,0:T(8,128)S(1)}, f32[4096,128]{1,0:T(8,128)}, u32[]{:S(2)}, u32[]{:S(2)}) collective-permute-start(f32[4096,128]{1,0:T(8,128)S(1)} %bitcast.14), channel_id=1, source_target_pairs={{4,8},{8,4},{5,9},{9,5},{6,10},{10,6},{7,11},{11,7},{20,24},{24,20... | collective-permute-start | bytes 6291464 | tf_op jit(solution)/shard_map/ppermute | solution.py:495
  7.4 11.0 %collective-permute-start.4 = (f32[2,16,16,128]{3,2,1,0:T(8,128)}, f32[2,16,16,128]{3,2,1,0:T(8,128)S(1)}, u32[]{:S(2)}, u32[]{:S(2)}) collective-permute-start(f32[2,16,16,128]{3,2,1,0:T(8,128)} %get-tuple-element.33), channel_id=1, source_target_pairs={{0,1},{1,2},{2,3},{4,5},{5,6},{6,7},{8,9},{9,10},{10,11},{12,13},{... | collective-permute-start | bytes 786440 | tf_op jit(solution)/shard_map/ppermute | solution.py:503
  12.0 11.0 %collective-permute-start.5 = (f32[2,16,16,128]{3,2,1,0:T(8,128)}, f32[2,16,16,128]{3,2,1,0:T(8,128)S(1)}, u32[]{:S(2)}, u32[]{:S(2)}) collective-permute-start(f32[2,16,16,128]{3,2,1,0:T(8,128)} %get-tuple-element.34), channel_id=1, source_target_pairs={{1,0},{2,1},{3,2},{5,4},{6,5},{7,6},{9,8},{10,9},{11,10},{13,12},{... | collective-permute-start | bytes 786440 | tf_op jit(solution)/shard_map/ppermute | solution.py:504
  18.4 4.6 %copy-start.3 = (f32[2,16,16,128]{3,2,1,0:T(8,128)}, f32[2,16,16,128]{3,2,1,0:T(8,128)S(1)}, u32[]{:S(2)}) copy-start(f32[2,16,16,128]{3,2,1,0:T(8,128)S(1)} %collective-permute-done.4.before_ref) | copy-start | bytes 786436
  23.0 0.7 copy-start.4
  29.1 25.1 %collective-permute-start.8 = (f32[16,128,128]{2,1,0:T(8,128)}, f32[16,128,128]{2,1,0:T(8,128)S(1)}, u32[]{:S(2)}, u32[]{:S(2)}) collective-permute-start(f32[16,128,128]{2,1,0:T(8,128)} %columns.7.x_ref), channel_id=1, source_target_pairs={{0,4},{4,0},{8,12},{12,8},{1,5},{5,1},{9,13},{13,9},{2,6},{6,2},{1... | collective-permute-start | bytes 3145736 | tf_op jit(solution)/shard_map/ppermute | solution.py:511
  29.3 26.4 %collective-permute-start.9 = (f32[16,128,128]{2,1,0:T(8,128)}, f32[16,128,128]{2,1,0:T(8,128)}, u32[]{:S(2)}, u32[]{:S(2)}) collective-permute-start(f32[16,128,128]{2,1,0:T(8,128)} %columns.7.x_ref), channel_id=1, source_target_pairs={{4,8},{8,4},{5,9},{9,5},{6,10},{10,6},{7,11},{11,7},{20,24},{24,20... | collective-permute-start | bytes 3145736 | tf_op jit(solution)/shard_map/ppermute | solution.py:510
  36.2 25.7 %collective-permute-start.6 = (f32[16,128,128]{2,1,0:T(8,128)}, f32[16,128,128]{2,1,0:T(8,128)}, u32[]{:S(2)}, u32[]{:S(2)}) collective-permute-start(f32[16,128,128]{2,1,0:T(8,128)} %columns.6.x_ref), channel_id=1, source_target_pairs={{0,4},{4,0},{8,12},{12,8},{1,5},{5,1},{9,13},{13,9},{2,6},{6,2},{1... | collective-permute-start | bytes 3145736 | tf_op jit(solution)/shard_map/ppermute | solution.py:511
  37.5 24.5 %collective-permute-start.7 = (f32[16,128,128]{2,1,0:T(8,128)}, f32[16,128,128]{2,1,0:T(8,128)}, u32[]{:S(2)}, u32[]{:S(2)}) collective-permute-start(f32[16,128,128]{2,1,0:T(8,128)} %columns.6.x_ref), channel_id=1, source_target_pairs={{4,8},{8,4},{5,9},{9,5},{6,10},{10,6},{7,11},{11,7},{20,24},{24,20... | collective-permute-start | bytes 3145736 | tf_op jit(solution)/shard_map/ppermute | solution.py:510
  50.7 17.5 %collective-permute-start.2 = (f32[2,16,16,128]{3,2,1,0:T(8,128)}, f32[2,16,16,128]{3,2,1,0:T(8,128)S(1)}, u32[]{:S(2)}, u32[]{:S(2)}) collective-permute-start(f32[2,16,16,128]{3,2,1,0:T(8,128)} %get-tuple-element.30), channel_id=1, source_target_pairs={{0,1},{1,2},{2,3},{4,5},{5,6},{6,7},{8,9},{9,10},{10,11},{12,13},{... | collective-permute-start | bytes 786440 | tf_op jit(solution)/shard_map/ppermute | solution.py:513
  54.2 1.5 %copy-start.1 = (f32[16,128,128]{2,1,0:T(8,128)}, f32[16,128,128]{2,1,0:T(8,128)S(1)}, u32[]{:S(2)}) copy-start(f32[16,128,128]{2,1,0:T(8,128)S(1)} %collective-permute-done.8.near_ref) | copy-start | bytes 3145732
  54.2 14.0 %collective-permute-start.3 = (f32[2,16,16,128]{3,2,1,0:T(8,128)}, f32[2,16,16,128]{3,2,1,0:T(8,128)S(1)}, u32[]{:S(2)}, u32[]{:S(2)}) collective-permute-start(f32[2,16,16,128]{3,2,1,0:T(8,128)} %get-tuple-element.31), channel_id=1, source_target_pairs={{1,0},{2,1},{3,2},{5,4},{6,5},{7,6},{9,8},{10,9},{11,10},{13,12},{... | collective-permute-start | bytes 786440 | tf_op jit(solution)/shard_map/ppermute | solution.py:514
  68.1 0.7 copy-start.2
  68.2 0.8 copy-start.5
  85.9 2.6 %collective-permute-start.10 = (f32[320,128]{1,0:T(8,128)}, f32[320,128]{1,0:T(8,128)S(1)}, u32[]{:S(2)}, u32[]{:S(2)}) collective-permute-start(f32[320,128]{1,0:T(8,128)} %get-tuple-element.36), channel_id=1, source_target_pairs={{0,4},{4,0},{8,12},{12,8},{1,5},{5,1},{9,13},{13,9},{2,6},{6,2},{1... | collective-permute-start | bytes 491528 | tf_op jit(solution)/shard_map/ppermute | solution.py:321
  87.2 7.3 %collective-permute-start.11 = (f32[320,128]{1,0:T(8,128)}, f32[320,128]{1,0:T(8,128)S(1)}, u32[]{:S(2)}, u32[]{:S(2)}) collective-permute-start(f32[320,128]{1,0:T(8,128)} %get-tuple-element.37), channel_id=1, source_target_pairs={{0,8},{4,12},{8,0},{12,4},{1,9},{5,13},{9,1},{13,5},{2,10},{6,14},... | collective-permute-start | bytes 491528 | tf_op jit(solution)/shard_map/ppermute | solution.py:321
  87.9 8.1 %collective-permute-start.12 = (f32[320,128]{1,0:T(8,128)}, f32[320,128]{1,0:T(8,128)S(1)}, u32[]{:S(2)}, u32[]{:S(2)}) collective-permute-start(f32[320,128]{1,0:T(8,128)} %get-tuple-element.38), channel_id=1, source_target_pairs={{0,12},{4,8},{8,4},{12,0},{1,13},{5,9},{9,5},{13,1},{2,14},{6,10},... | collective-permute-start | bytes 491528 | tf_op jit(solution)/shard_map/ppermute | solution.py:321
  88.5 7.5 %copy-start.7 = (f32[320,128]{1,0:T(8,128)}, f32[320,128]{1,0:T(8,128)S(1)}, u32[]{:S(2)}) copy-start(f32[320,128]{1,0:T(8,128)S(1)} %collective-permute-done.10.refs_1_) | copy-start | bytes 491524
  94.4 1.6 %copy-start.8 = (f32[320,128]{1,0:T(8,128)}, f32[320,128]{1,0:T(8,128)S(1)}, u32[]{:S(2)}) copy-start(f32[320,128]{1,0:T(8,128)S(1)} %collective-permute-done.11.refs_2_) | copy-start | bytes 491524
  96.0 0.7 copy-start.9
  98.5 5.1 %collective-permute-start.13 = (f32[80,128]{1,0:T(8,128)}, f32[80,128]{1,0:T(8,128)S(1)}, u32[]{:S(2)}, u32[]{:S(2)}) collective-permute-start(f32[80,128]{1,0:T(8,128)} %get-tuple-element.40), channel_id=1, source_target_pairs={{0,1},{1,0},{2,3},{3,2},{4,5},{5,4},{6,7},{7,6},{8,9},{9,8},{10,11... | collective-permute-start | bytes 122888 | tf_op jit(solution)/shard_map/ppermute | solution.py:321
  101.0 6.0 %collective-permute-start.14 = (f32[80,128]{1,0:T(8,128)}, f32[80,128]{1,0:T(8,128)S(1)}, u32[]{:S(2)}, u32[]{:S(2)}) collective-permute-start(f32[80,128]{1,0:T(8,128)} %get-tuple-element.41), channel_id=1, source_target_pairs={{0,2},{1,3},{2,0},{3,1},{4,6},{5,7},{6,4},{7,5},{8,10},{9,11},{10,... | collective-permute-start | bytes 122888 | tf_op jit(solution)/shard_map/ppermute | solution.py:321
  102.2 6.0 %collective-permute-start.15 = (f32[80,128]{1,0:T(8,128)}, f32[80,128]{1,0:T(8,128)S(1)}, u32[]{:S(2)}, u32[]{:S(2)}) collective-permute-start(f32[80,128]{1,0:T(8,128)} %get-tuple-element.42), channel_id=1, source_target_pairs={{0,3},{1,2},{2,1},{3,0},{4,7},{5,6},{6,5},{7,4},{8,11},{9,10},{10,... | collective-permute-start | bytes 122888 | tf_op jit(solution)/shard_map/ppermute | solution.py:321
  109.0 8.3 %copy-start.6 = (f32[80,128]{1,0:T(8,128)}, f32[80,128]{1,0:T(8,128)S(1)}, u32[]{:S(2)}) copy-start(f32[80,128]{1,0:T(8,128)S(1)} %add_add_fusion.refs_0_) | copy-start | bytes 122884
  109.0 4.5 %collective-permute-start.16 = (f32[80,128]{1,0:T(8,128)S(1)}, f32[80,128]{1,0:T(8,128)S(1)}, u32[]{:S(2)}, u32[]{:S(2)}) collective-permute-start(f32[80,128]{1,0:T(8,128)S(1)} %add_add_fusion.refs_0_), channel_id=1, source_target_pairs={{0,1},{1,0},{2,3},{3,2},{4,5},{5,4},{6,7},{7,6},{8,9},{9,8},{10,11... | collective-permute-start | bytes 122888 | tf_op jit(solution)/shard_map/ppermute | solution.py:321
  110.1 6.0 %collective-permute-start.17 = (f32[80,128]{1,0:T(8,128)S(1)}, f32[80,128]{1,0:T(8,128)S(1)}, u32[]{:S(2)}, u32[]{:S(2)}) collective-permute-start(f32[80,128]{1,0:T(8,128)S(1)} %add_add_fusion.refs_0_), channel_id=1, source_target_pairs={{0,2},{1,3},{2,0},{3,1},{4,6},{5,7},{6,4},{7,5},{8,10},{9,11},{10,... | collective-permute-start | bytes 122888 | tf_op jit(solution)/shard_map/ppermute | solution.py:321
  111.5 5.8 %collective-permute-start.18 = (f32[80,128]{1,0:T(8,128)S(1)}, f32[80,128]{1,0:T(8,128)S(1)}, u32[]{:S(2)}, u32[]{:S(2)}) collective-permute-start(f32[80,128]{1,0:T(8,128)S(1)} %add_add_fusion.refs_0_), channel_id=1, source_target_pairs={{0,3},{1,2},{2,1},{3,0},{4,7},{5,6},{6,5},{7,4},{8,11},{9,10},{10,... | collective-permute-start | bytes 122888 | tf_op jit(solution)/shard_map/ppermute | solution.py:321
  113.5 3.8 %copy-start.14 = (f32[80,128]{1,0:T(8,128)}, f32[80,128]{1,0:T(8,128)S(1)}, u32[]{:S(2)}) copy-start(f32[80,128]{1,0:T(8,128)S(1)} %collective-permute-done.16.refs_1_) | copy-start | bytes 122884
  116.2 1.1 copy-start.15
  117.3 0.6 copy-start.16
  119.5 1.9 %collective-permute-start.19 = (f32[320,128]{1,0:T(8,128)}, f32[320,128]{1,0:T(8,128)S(1)}, u32[]{:S(2)}, u32[]{:S(2)}) collective-permute-start(f32[320,128]{1,0:T(8,128)} %join.1.refs_4_), channel_id=1, source_target_pairs={{0,4},{4,0},{8,12},{12,8},{1,5},{5,1},{9,13},{13,9},{2,6},{6,2},{1... | collective-permute-start | bytes 491528 | tf_op jit(solution)/shard_map/ppermute | solution.py:321
  119.5 7.3 %collective-permute-start.20 = (f32[320,128]{1,0:T(8,128)}, f32[320,128]{1,0:T(8,128)S(1)}, u32[]{:S(2)}, u32[]{:S(2)}) collective-permute-start(f32[320,128]{1,0:T(8,128)} %join.1.refs_4_), channel_id=1, source_target_pairs={{0,8},{4,12},{8,0},{12,4},{1,9},{5,13},{9,1},{13,5},{2,10},{6,14},... | collective-permute-start | bytes 491528 | tf_op jit(solution)/shard_map/ppermute | solution.py:321
  121.2 8.1 %collective-permute-start.21 = (f32[320,128]{1,0:T(8,128)}, f32[320,128]{1,0:T(8,128)S(1)}, u32[]{:S(2)}, u32[]{:S(2)}) collective-permute-start(f32[320,128]{1,0:T(8,128)} %join.1.refs_4_), channel_id=1, source_target_pairs={{0,12},{4,8},{8,4},{12,0},{1,13},{5,9},{9,5},{13,1},{2,14},{6,10},... | collective-permute-start | bytes 491528 | tf_op jit(solution)/shard_map/ppermute | solution.py:321
  121.3 8.0 %copy-start.10 = (f32[320,128]{1,0:T(8,128)}, f32[320,128]{1,0:T(8,128)S(1)}, u32[]{:S(2)}) copy-start(f32[320,128]{1,0:T(8,128)S(1)} %collective-permute-done.19.refs_5_) | copy-start | bytes 491524
  126.7 2.6 %copy-start.11 = (f32[320,128]{1,0:T(8,128)}, f32[320,128]{1,0:T(8,128)S(1)}, u32[]{:S(2)}) copy-start(f32[320,128]{1,0:T(8,128)S(1)} %collective-permute-done.20.refs_6_) | copy-start | bytes 491524
  129.3 0.7 copy-start.12

commit v3 on v2

--- a/solution.py
+++ b/solution.py
@@ -16,6 +16,7 @@
 VM = pl.BlockSpec(memory_space=pltpu.VMEM)
 SM = pl.BlockSpec(memory_space=pltpu.SMEM)
 f32 = jnp.float32
+GRANT = pltpu.CompilerParams(vmem_limit_bytes=24 * 2**20)
 
 
 def shape(*dims):
@@ -26,40 +27,112 @@
     return pl.CostEstimate(flops=int(flops), bytes_accessed=int(nbytes), transcendentals=0)
 
 
+PHASES = ((0, 1, 2, 3), (0, 1), (2, 3), (0, 2), (0,), (2,), (1, 3), (1,), (3,))
+
+
+def short_count(combo, taps):
+    return max(len(range(p, taps, 4)) for p in PHASES[combo])
+
+
+def padded_taps(beam_taps, chunks):
+    channels, taps = beam_taps.shape
+    height = -(-4 * short_count(0, taps) // SUB) * SUB
+    return jnp.pad(beam_taps, ((0, 0), (0, height - taps))).reshape(chunks, LANES, height).transpose(0, 2, 1)
+
+
+def short_taps(taps_ref, short, taps):
+    depth = short_count(0, taps)
+    phases = [taps_ref[pl.ds(p, depth, stride=4), :] for p in range(4)]
+    for index, combo in enumerate(PHASES):
+        short[index * depth:(index + 1) * depth, :] = functools.reduce(jnp.add, [phases[p] for p in combo])
+
+
+def short_scratch(taps):
+    return pltpu.VMEM((len(PHASES) * short_count(0, taps), LANES), f32)
+
+
+def tap(taps_ref, index):
+    return jnp.broadcast_to(taps_ref[index:index + 1, :], (SUB, LANES))
+
+
+def halves(even, odd):
+    return [odd, [p - q for p, q in zip(even, odd)], [p - q for p, q in zip(even[1:], odd)]]
+
+
+def add_to(total, term):
+    return term if total is None else total + term
+
+
 def row_taps(buf, taps_ref, out_ref, rows, taps, first, count):
+    depth = short_count(0, taps)
+
     def body(group, carry):
         part = pl.ds(pl.multiple_of(group * SUB, SUB), SUB)
-        weights = [taps_ref[a] for a in range(taps)]
-        total = [None] * rows
-        for r in range(rows + taps - 1):
-            x = buf[r, part, :]
-            for i in range(max(0, r - taps + 1), min(rows - 1, r) + 1):
-                term = weights[r - i] * x
-                total[i] = term if total[i] is None else total[i] + term
-        for i in range(rows):
-            out_ref[i, part, :] = total[i]
+        x = [buf[r, part, :] for r in range(rows + taps - 1)]
+        base = None
+        for s, z in enumerate(halves(x[0::2], x[1::2])):
+            sums = []
+            for t, w in enumerate(halves(z[0::2], z[1::2])):
+                combo = 3 * s + t
+                totals = [None] * (rows // 4)
+                for k in range(short_count(combo, taps)):
+                    weight = tap(taps_ref, combo * depth + k)
+                    totals = [add_to(total, weight * w[n + k]) for n, total in enumerate(totals)]
+                sums.append(totals)
+            both = []
+            for n in range(rows // 4):
+                both += [sums[0][n] + sums[1][n], sums[0][n] + sums[2][n]]
+            if s == 0:
+                base = both
+            else:
+                for m in range(rows // 2):
+                    out_ref[2 * m + s - 1, part, :] = base[m] + both[m]
         return carry
 
     lax.fori_loop(first, first + count, body, 0)
 
 
-def col_taps(buf, taps_ref, out_ref, cols, taps, first, count, step=2):
-    groups = cols // SUB
+def col_taps(buf, taps_ref, out_ref, streams, cols, taps, first, count, step=2):
+    depth = short_count(0, taps)
+    groups = cols // (4 * SUB)
+    length = streams.shape[2]
 
     def body(block, carry):
-        weights = [taps_ref[a] for a in range(taps)]
-        total = {}
-        for s in range(SUB * (groups - 1) + taps):
-            for q in range(step):
-                i = block * step + q
-                x = buf[i, pl.ds(s, SUB), :]
-                for g in range(groups):
-                    a = s - SUB * g
-                    if 0 <= a < taps:
-                        term = weights[a] * x
-                        total[q, g] = term if a == 0 else total[q, g] + term
-                        if a == taps - 1:
-                            out_ref[i, pl.ds(SUB * g, SUB), :] = total.pop((q, g))
+        for q in range(step):
+            i = block * step + q
+            for m in range(0, length, SUB):
+                p = [buf[i, pl.ds(4 * m + d, SUB, stride=4), :] for d in range(7)]
+                z = [
+                    (p[1], p[3], p[5]),
+                    (p[0] - p[1], p[2] - p[3], p[4] - p[5]),
+                    (p[2] - p[1], p[4] - p[3], p[6] - p[5]),
+                ]
+                for s, (even, odd, after) in enumerate(z):
+                    streams[q, 3 * s, pl.ds(m, SUB), :] = odd
+                    streams[q, 3 * s + 1, pl.ds(m, SUB), :] = even - odd
+                    streams[q, 3 * s + 2, pl.ds(m, SUB), :] = after - odd
+        where = [(q, g) for q in range(step) for g in range(groups)]
+        base = None
+        for s in range(3):
+            sums = []
+            for t in range(3):
+                combo = 3 * s + t
+                totals = [None] * len(where)
+                for k in range(short_count(combo, taps)):
+                    weight = tap(taps_ref, combo * depth + k)
+                    totals = [
+                        add_to(total, weight * streams[q, combo, pl.ds(SUB * g + k, SUB), :])
+                        for total, (q, g) in zip(totals, where)
+                    ]
+                sums.append(totals)
+            both = [[sums[0][n] + sums[1 + odd][n] for odd in range(2)] for n in range(len(where))]
+            if s == 0:
+                base = both
+            else:
+                for n, (q, g) in enumerate(where):
+                    for odd in range(2):
+                        at = pl.ds(4 * SUB * g + 2 * odd + s - 1, SUB, stride=4)
+                        out_ref[block * step + q, at, :] = base[n][odd] + both[n][odd]
         return carry
 
     lax.fori_loop(first // step, (first + count) // step, body, 0)
@@ -101,11 +174,12 @@
             shape(count, rows, margin, LANES),
         ],
         cost_estimate=cost(4e6 * count, 2.5e6 * count),
+        compiler_params=GRANT,
         name="prep",
     )(flat)
 
 
-def columns_kernel(which, rows, cols, margin, taps, flip, x_ref, before_ref, after_ref, taps_ref, out_ref, buf, held, sems):
+def columns_kernel(which, rows, cols, margin, taps, flip, x_ref, before_ref, after_ref, taps_ref, out_ref, buf, held, streams, short, sems):
     share = rows // PARTS
     pairs = []
     for p in range(PARTS):
@@ -116,10 +190,11 @@
             (after_ref.at[which, part], buf.at[part, pl.ds(margin + cols, margin), :]),
         ]
     started = start_all(pairs, sems)
+    short_taps(taps_ref.at[0], short, taps)
     for p in range(PARTS):
         for copy in started[3 * p:3 * p + 3]:
             copy.wait()
-        col_taps(buf, taps_ref.at[0], held if flip else out_ref, cols, taps, p * share, share)
+        col_taps(buf, short, held if flip else out_ref, streams, cols, taps, p * share, share)
         if flip:
             for r in range(p * share, p * share + share):
                 out_ref[:, r * cols:(r + 1) * cols] = held[r].T
@@ -127,25 +202,28 @@
 
 def columns(which, x, before, after, wide_taps, chunk, margin, flip):
     _, rows, cols, _ = x.shape
-    taps = wide_taps.shape[1]
+    taps = 2 * margin + 1
     out = (LANES, rows * cols) if flip else (rows, cols, LANES)
     return pl.pallas_call(
         functools.partial(columns_kernel, which, rows, cols, margin, taps, flip),
         grid=(1,),
-        in_specs=[ANY, ANY, ANY, pl.BlockSpec((1, taps, SUB, LANES), lambda k: (chunk, 0, 0, 0))],
+        in_specs=[ANY, ANY, ANY, pl.BlockSpec((1,) + wide_taps.shape[1:], lambda k: (chunk, 0, 0))],
         out_specs=pl.BlockSpec(out, lambda k: (0,) * len(out)),
         out_shape=shape(*out),
         scratch_shapes=[
-            pltpu.VMEM((rows, cols + 2 * margin, LANES), f32),
+            pltpu.VMEM((rows, cols + 2 * margin + SUB, LANES), f32),
             pltpu.VMEM((rows, cols, LANES), f32),
+            pltpu.VMEM((2, len(PHASES), (cols + 2 * margin) // 4, LANES), f32),
+            short_scratch(taps),
             pltpu.SemaphoreType.DMA((3 * PARTS,)),
         ],
         cost_estimate=cost(2e7, 2.5e6),
+        compiler_params=GRANT,
         name="columns",
     )(x, before, after, wide_taps)
 
 
-def raw_rows_kernel(count, rows, cols, margin, taps, side_ref, x_ref, near_ref, far_ref, taps_ref, out_ref, first_ref, last_ref, buf, native, sems):
+def raw_rows_kernel(count, rows, cols, margin, taps, side_ref, x_ref, near_ref, far_ref, taps_ref, out_ref, first_ref, last_ref, buf, native, short, sems):
     even = side_ref[0] == 0
     near = jnp.where(even, margin + rows, 0)
     far = jnp.where(even, 0, margin + rows)
@@ -161,14 +239,15 @@
             started[3 * n + slot].wait()
             for r in range(rows):
                 buf[start + r] = native[n, slot, pl.ds(r, LANES, stride=rows), :].T
-        row_taps(buf, taps_ref.at[n], out_ref.at[n], rows, taps, 0, cols // SUB)
+        short_taps(taps_ref.at[n], short, taps)
+        row_taps(buf, short, out_ref.at[n], rows, taps, 0, cols // SUB)
         first_ref[n] = out_ref[n, :, :margin, :]
         last_ref[n] = out_ref[n, :, cols - margin:, :]
 
 
 def raw_rows(x, near, far, wide_taps, side, rows, cols, margin):
     count = x.shape[0] // (LANES * rows)
-    taps = wide_taps.shape[1]
+    taps = 2 * margin + 1
     return pl.pallas_call(
         functools.partial(raw_rows_kernel, count, rows, cols, margin, taps),
         in_specs=[SM, ANY, ANY, ANY, VM],
@@ -181,14 +260,16 @@
         scratch_shapes=[
             pltpu.VMEM((rows + 2 * margin, cols, LANES), f32),
             pltpu.VMEM((count, 3, LANES * rows, cols), f32),
+            short_scratch(taps),
             pltpu.SemaphoreType.DMA((3 * count,)),
         ],
         cost_estimate=cost(3e7 * count, 4e6 * count),
+        compiler_params=GRANT,
         name="raw_rows",
     )(side, x, near, far, wide_taps)
 
 
-def rows_kernel(rows, cols, margin, taps, side_ref, x_ref, near_ref, far_ref, taps_ref, out_ref, buf, held, sems):
+def rows_kernel(rows, cols, margin, taps, side_ref, x_ref, near_ref, far_ref, taps_ref, out_ref, buf, held, short, sems):
     even = side_ref[0] == 0
     near = jnp.where(even, margin + rows, 0)
     far = jnp.where(even, 0, margin + rows)
@@ -199,29 +280,32 @@
         for source, start in ((x_ref, margin), (near_ref, near), (far_ref, far)):
             pairs.append((source.at[:, part, :], buf.at[pl.ds(start, rows), part, :]))
     started = start_all(pairs, sems)
+    short_taps(taps_ref.at[0], short, taps)
     for p in range(PARTS):
         for copy in started[3 * p:3 * p + 3]:
             copy.wait()
-        row_taps(buf, taps_ref.at[0], held, rows, taps, p * share // SUB, share // SUB)
+        row_taps(buf, short, held, rows, taps, p * share // SUB, share // SUB)
     for r in range(rows):
         out_ref[:, r * cols:(r + 1) * cols] = held[r].T
 
 
 def rows_of(x, near, far, wide_taps, chunk, side, margin):
     rows, cols, _ = x.shape
-    taps = wide_taps.shape[1]
+    taps = 2 * margin + 1
     return pl.pallas_call(
         functools.partial(rows_kernel, rows, cols, margin, taps),
         grid=(1,),
-        in_specs=[SM, ANY, ANY, ANY, pl.BlockSpec((1, taps, SUB, LANES), lambda k: (chunk, 0, 0, 0))],
+        in_specs=[SM, ANY, ANY, ANY, pl.BlockSpec((1,) + wide_taps.shape[1:], lambda k: (chunk, 0, 0))],
         out_specs=pl.BlockSpec((LANES, rows * cols), lambda k: (0, 0)),
         out_shape=shape(LANES, rows * cols),
         scratch_shapes=[
             pltpu.VMEM((rows + 2 * margin, cols, LANES), f32),
             pltpu.VMEM((rows, cols, LANES), f32),
+            short_scratch(taps),
             pltpu.SemaphoreType.DMA((3 * PARTS,)),
         ],
         cost_estimate=cost(2e7, 4e6),
+        compiler_params=GRANT,
         name="rows",
     )(side, x, near, far, wide_taps)
 
@@ -230,9 +314,12 @@
     return [(i, j) for i in range(chunks) for j in range(i, chunks)]
 
 
-def gram_kernel(chunks, peers, me_ref, *refs):
+def gram_kernel(chunks, peers, me_ref, cosine_ref, *refs):
     xs, outs = refs[:chunks], refs[chunks:chunks + peers]
-    high, low, packed = refs[chunks + peers:]
+    start_ref, high, low, packed = refs[chunks + peers:]
+    channels = chunks * LANES
+    start = orthonormal_rows([cosine_ref[k:k + 1, :] for k in range(MODES)], channels)
+    start_ref[...] = jnp.concatenate(start + [jnp.zeros((SUB - MODES, channels), f32)], axis=0)
     for k, x_ref in enumerate(xs):
         x = x_ref[...]
         h = x.astype(jnp.bfloat16)
@@ -250,31 +337,34 @@
         outs[d][...] = packed[pl.ds(pl.multiple_of(piece * size, size), size), :]
 
 
-def gram_pieces(xs, me, peers):
+def gram_pieces(xs, cosine, me, peers):
     chunks = len(xs)
     channels, pixels = chunks * LANES, xs[0].shape[1]
     height = len(upper(chunks)) * LANES
     return pl.pallas_call(
         functools.partial(gram_kernel, chunks, peers),
-        in_specs=[SM] + [VM] * chunks,
-        out_specs=[VM] * peers,
-        out_shape=[shape(height // peers, LANES)] * peers,
+        in_specs=[SM, VM] + [VM] * chunks,
+        out_specs=[VM] * (peers + 1),
+        out_shape=[shape(height // peers, LANES)] * peers + [shape(SUB, channels)],
         scratch_shapes=[
             pltpu.VMEM((channels, pixels), jnp.bfloat16),
             pltpu.VMEM((channels, pixels), jnp.bfloat16),
             pltpu.VMEM((height, LANES), f32),
         ],
         cost_estimate=cost(4e9, 5e6),
+        compiler_params=GRANT,
         name="gram",
-    )(me, *xs)
+    )(me, cosine, *xs)
 
 
 def split_kernel(count, peers, me_ref, *refs):
     parts, outs = refs[:count], refs[count:count + peers]
-    total = refs[count + peers]
-    value = parts[0][...]
-    for part in parts[1:]:
-        value = value + part[...]
+    held, total, sems = refs[count + peers:]
+    for copy in start_all([(part, held.at[n]) for n, part in enumerate(parts)], sems):
+        copy.wait()
+    value = held[0]
+    for n in range(1, count):
+        value = value + held[n]
     total[...] = value
     size = total.shape[0] // peers
     for d in range(peers):
@@ -286,20 +376,30 @@
     height, width = parts[0].shape
     return pl.pallas_call(
         functools.partial(split_kernel, len(parts), peers),
-        in_specs=[SM] + [VM] * len(parts),
+        in_specs=[SM] + [ANY] * len(parts),
         out_specs=[VM] * peers,
         out_shape=[shape(height // peers, width)] * peers,
-        scratch_shapes=[pltpu.VMEM((height, width), f32)],
+        scratch_shapes=[
+            pltpu.VMEM((len(parts), height, width), f32),
+            pltpu.VMEM((height, width), f32),
+            pltpu.SemaphoreType.DMA((len(parts),)),
+        ],
+        compiler_params=GRANT,
         name="sum_and_split",
     )(me, *parts)
 
 
+def place(pieces, target, me, sems):
+    size = target.shape[0] // len(pieces)
+    pairs = []
+    for d, piece in enumerate(pieces):
+        pairs.append((piece, target.at[pl.ds(pl.multiple_of((me ^ d) * size, size), size)]))
+    return start_all(pairs, sems)
+
+
 def join_kernel(peers, me_ref, *refs):
-    parts, out_ref = refs[:peers], refs[peers]
-    size = parts[0].shape[0]
-    for d in range(peers):
-        piece = me_ref[0] ^ d
-        out_ref[pl.ds(pl.multiple_of(piece * size, size), size), :] = parts[d][...]
+    for copy in place(refs[:peers], refs[peers], me_ref[0], refs[peers + 1]):
+        copy.wait()
 
 
 def join(parts, me):
@@ -307,9 +407,11 @@
     height, width = parts[0].shape
     return pl.pallas_call(
         functools.partial(join_kernel, peers),
-        in_specs=[SM] + [VM] * peers,
+        in_specs=[SM] + [ANY] * peers,
         out_specs=VM,
         out_shape=shape(height * peers, width),
+        scratch_shapes=[pltpu.SemaphoreType.DMA((peers,))],
+        compiler_params=GRANT,
         name="join",
     )(me, *parts)
 
@@ -344,22 +446,10 @@
     return done
 
 
-def start_kernel(channels, cosine_ref, out_ref):
-    rows = orthonormal_rows([cosine_ref[k:k + 1, :] for k in range(MODES)], channels)
-    out_ref[...] = jnp.concatenate(rows + [jnp.zeros((SUB - MODES, channels), f32)], axis=0)
-
-
-def start_basis(channels):
+def cosine_rows(channels):
     channel_pos = jnp.arange(channels).astype(f32)
     mode_index = jnp.arange(MODES).astype(f32)
-    cosine = jnp.cos(jnp.pi * mode_index[:, None] * (channel_pos[None, :] + 0.5) / channels)
-    return pl.pallas_call(
-        functools.partial(start_kernel, channels),
-        in_specs=[VM],
-        out_specs=VM,
-        out_shape=shape(SUB, channels),
-        name="start_basis",
-    )(cosine)
+    return jnp.cos(jnp.pi * mode_index[:, None] * (channel_pos[None, :] + 0.5) / channels)
 
 
 def spread(basis, wide, channels):
@@ -385,13 +475,12 @@
 
 def clean_kernel(chunks, peers, rows, cols, me_ref, start_ref, *refs):
     xs, pieces, out_ref = refs[:chunks], refs[chunks:chunks + peers], refs[chunks + peers]
-    x_buf, packed, gram, wide, coef, out_buf, sems, out_sems = refs[chunks + peers + 1:]
+    x_buf, packed, gram, wide, coef, out_buf, sems, piece_sems, out_sems = refs[chunks + peers + 1:]
     channels = chunks * LANES
+    placed = place(pieces, packed, me_ref[0], piece_sems)
     started = load_all(xs, x_buf, sems)
-    size = packed.shape[0] // peers
-    for d in range(peers):
-        piece = me_ref[0] ^ d
-        packed[pl.ds(pl.multiple_of(piece * size, size), size), :] = pieces[d][...]
+    for copy in placed:
+        copy.wait()
     diagonal = jnp.zeros((1, LANES), f32)
     row_id = lax.broadcasted_iota(jnp.int32, (LANES, LANES), 0)
     col_id = lax.broadcasted_iota(jnp.int32, (LANES, LANES), 1)
@@ -455,7 +544,7 @@
     chunks, channels = len(xs), len(xs) * LANES
     return pl.pallas_call(
         functools.partial(clean_kernel, chunks, len(pieces), rows, cols),
-        in_specs=[SM, VM] + [ANY] * chunks + [VM] * len(pieces),
+        in_specs=[SM, VM] + [ANY] * (chunks + len(pieces)),
         out_specs=ANY,
         out_shape=shape(channels * rows, cols),
         scratch_shapes=[
@@ -466,9 +555,11 @@
             pltpu.VMEM((rows, MODES, SUB, LANES), f32),
             pltpu.VMEM((channels * rows, cols), f32),
             pltpu.SemaphoreType.DMA((chunks,)),
+            pltpu.SemaphoreType.DMA((len(pieces),)),
             pltpu.SemaphoreType.DMA((chunks,)),
         ],
         cost_estimate=cost(4e7, 9e6),
+        compiler_params=GRANT,
         name="clean",
     )(me, start, *xs, *pieces)
 
@@ -490,19 +581,16 @@
     height = LANES * rows
     flat = sky_cube.reshape(channels * rows, cols)
     ahead = chunks // 2
-    head = flat[:ahead * height]
-    head, body = lax.optimization_barrier((head, flat))
+    wide_taps = padded_taps(beam_taps, chunks)
+    cosine = cosine_rows(channels)
+
+    head, body = lax.optimization_barrier((flat[:ahead * height], flat))
     far_head = lax.ppermute(head, "row", far_pairs)
     near_head = lax.ppermute(head, "row", near_pairs)
-    wide_taps = jnp.broadcast_to(
-        beam_taps.T.reshape(taps, chunks, 1, LANES).transpose(1, 0, 2, 3), (chunks, taps, SUB, LANES)
-    )
-    start = start_basis(channels)
-
     raw, first, last = prep(body, rows, cols, margin, ahead, chunks - ahead)
     before = lax.ppermute(last, "col", right)
     after = lax.ppermute(first, "col", left)
-    raw, wide_taps, start = lax.optimization_barrier((raw, wide_taps, start))
+    raw, wide_taps, cosine = lax.optimization_barrier((raw, wide_taps, cosine))
     xs = [None] * chunks
     smooth, near, far = [None] * chunks, [None] * chunks, [None] * chunks
     for k in range(ahead, chunks):
@@ -512,15 +600,14 @@
     mixed, first_head, last_head = raw_rows(head, near_head, far_head, wide_taps, side, rows, cols, margin)
     before_head = lax.ppermute(last_head, "col", right)
     after_head = lax.ppermute(first_head, "col", left)
-    for k in range(ahead, chunks - 1):
+    for k in range(ahead, chunks):
         xs[k] = rows_of(smooth[k], near[k], far[k], wide_taps, k, side, margin)
     for k in range(ahead):
         xs[k] = columns(k, mixed, before_head, after_head, wide_taps, k, margin, True)
-    k = chunks - 1
-    xs[k] = rows_of(smooth[k], near[k], far[k], wide_taps, k, side, margin)
 
     row_ref, col_ref = jnp.reshape(me_row, (1,)), jnp.reshape(me_col, (1,))
-    pieces = exchange(gram_pieces(xs, row_ref, n_row), "row")
+    *pieces, start = gram_pieces(xs, cosine, row_ref, n_row)
+    pieces = exchange(pieces, "row")
     if pieces[0].shape[0] % (SUB * n_col) == 0:
         small = exchange(sum_and_split(pieces, col_ref, n_col), "col")
         mine = functools.reduce(jnp.add, small)

time: 143 us -> 117 us (0.82)
  Pallas kernels: 72.7 us -> 41.5 us
  waiting for transfers between devices: 29.8 us -> 35.8 us
    pallas_call x4, Pallas kernels: 22.2 us -> 9.33 us  [columns(): pl.pallas_call(functools.partial(columns_kernel, which, rows, cols, margi...]
    pallas_call x2, Pallas kernels: 12.4 us -> 7.12 us  [rows_of(): pl.pallas_call(functools.partial(rows_kernel, rows, cols, margin, taps),...]
    pallas_call x1, Pallas kernels: 11.6 us -> 7.07 us  [raw_rows(): pl.pallas_call(functools.partial(raw_rows_kernel, count, rows, cols, marg...]
    pallas_call x2 -> x1, Pallas kernels: 3.77 us -> 0.22 us  [join(): pl.pallas_call(functools.partial(join_kernel, peers), in_specs=[SM] + [AN...]
    ppermute x1, waiting for transfers between devices: 1.18 us -> 4.58 us  [per_device(): before = lax.ppermute(last, 'col', right)]
    pallas_call x1, Pallas kernels: 3.09 us -> 0.76 us  [prep(): pl.pallas_call(functools.partial(prep_kernel, rows, cols, margin), grid=(...]
    ppermute x1, waiting for transfers between devices: 0.01 us -> 2.28 us  [per_device(): after_head = lax.ppermute(first_head, 'col', left)]
    pallas_call x1, Pallas kernels: 5.4 us -> 3.21 us  [gram_pieces(): pl.pallas_call(functools.partial(gram_kernel, chunks, peers), in_specs=[S...]
  transfers between devices with their start and end apart: 22 -> 22, of which waited for: 11 -> 11; matrix products, arithmetic and copies ran while one was open for 1% -> 0% of each run, Pallas kernels for 28% -> 17%
where the time goes in v3:
time: 117 us
  Pallas kernels  41.5 us (35%)
  waiting for transfers between devices  35.8 us (31%)
  starting transfers between devices  33.1 us (28%)
  local copies, waits for them, and re-layouts  6.04 us (5%)
    ppermute x12, waiting for transfers between devices, exchange(): lax.ppermute(pieces[d], axis, [(i, i ^ d) for i in range(peers)])  24.2 us
    ppermute x12, starting transfers between devices, exchange(): lax.ppermute(pieces[d], axis, [(i, i ^ d) for i in range(peers)])  14.9 us
    pallas_call x1, Pallas kernels, clean(): pl.pallas_call(functools.partial(clean_kernel, chunks, len(pieces), rows,...  12.4 us
    pallas_call x4, Pallas kernels, columns(): pl.pallas_call(functools.partial(columns_kernel, which, rows, cols, margi...  9.33 us
    pallas_call x2, Pallas kernels, rows_of(): pl.pallas_call(functools.partial(rows_kernel, rows, cols, margin, taps),...  7.12 us
    pallas_call x1, Pallas kernels, raw_rows(): pl.pallas_call(functools.partial(raw_rows_kernel, count, rows, cols, marg...  7.07 us
    ppermute x1, waiting for transfers between devices, per_device(): after = lax.ppermute(first, 'col', left)  4.69 us
    ppermute x1, waiting for transfers between devices, per_device(): before = lax.ppermute(last, 'col', right)  4.58 us
  transfers between devices with their start and end apart: 22, of which 11 were waited for; matrix products, arithmetic and copies ran while one was open for 0% of the time, Pallas kernels for 17%

profile of v3, /device:TPU:0, one launch (start us, length us, event | category | flops | bytes accessed | tf_op | source)
XLA Modules:
  0.0 117.1 jit_solution(14083010469005062935)
XLA Ops:
  0.0 1.9 %slice.6 = f32[256,16,128]{2,1,0:T(8,128)S(1)} slice(f32[512,16,128]{2,1,0:T(8,128)} %param.2), slice={[0:256], [0:16], [0:128]} | slice | bytes 4194304 | tf_op jit(solution)/shard_map/slice | solution.py:587
  1.9 0.6 collective-permute-start
  2.5 2.0 %collective-permute-start.1 = (f32[4096,128]{1,0:T(8,128)S(1)}, f32[4096,128]{1,0:T(8,128)}, u32[]{:S(2)}, u32[]{:S(2)}) collective-permute-start(f32[4096,128]{1,0:T(8,128)S(1)} %bitcast.15), channel_id=1, source_target_pairs={{4,8},{8,4},{5,9},{9,5},{6,10},{10,6},{7,11},{11,7},{20,24},{24,20... | collective-permute-start | bytes 6291464 | tf_op jit(solution)/shard_map/ppermute | solution.py:588
  4.5 0.8 prep.1
  5.2 4.5 %collective-permute-start.4 = (f32[2,16,16,128]{3,2,1,0:T(8,128)S(1)}, f32[2,16,16,128]{3,2,1,0:T(8,128)S(1)}, u32[]{:S(2)}, u32[]{:S(2)}) collective-permute-start(f32[2,16,16,128]{3,2,1,0:T(8,128)S(1)} %get-tuple-element.34), channel_id=1, source_target_pairs={{0,1},{1,2},{2,3},{4,5},{5,6},{6,7},{8,9},{9,10},{10,11},{12,13},{... | collective-permute-start | bytes 786440 | tf_op jit(solution)/shard_map/ppermute | solution.py:591
  9.7 1.3 %collective-permute-start.5 = (f32[2,16,16,128]{3,2,1,0:T(8,128)S(1)}, f32[2,16,16,128]{3,2,1,0:T(8,128)S(1)}, u32[]{:S(2)}, u32[]{:S(2)}) collective-permute-start(f32[2,16,16,128]{3,2,1,0:T(8,128)S(1)} %get-tuple-element.35), channel_id=1, source_target_pairs={{1,0},{2,1},{3,2},{5,4},{6,5},{7,6},{9,8},{10,9},{11,10},{13,12},{... | collective-permute-start | bytes 786440 | tf_op jit(solution)/shard_map/ppermute | solution.py:592
  11.1 0.1 multiply_cosine_fusion.cosine_ref
  11.2 4.6 %collective-permute-done.4.before_ref = f32[2,16,16,128]{3,2,1,0:T(8,128)S(1)} collective-permute-done((f32[2,16,16,128]{3,2,1,0:T(8,128)S(1)}, f32[2,16,16,128]{3,2,1,0:T(8,128)S(1)}, u32[]{:S(2)}, u32[]{:S(2)}) %collective-permute-start.4) | collective-permute-done | bytes 262176 | tf_op jit(solution)/shard_map/ppermute | solution.py:591
  15.8 4.7 %collective-permute-done.5.after_ref = f32[2,16,16,128]{3,2,1,0:T(8,128)S(1)} collective-permute-done((f32[2,16,16,128]{3,2,1,0:T(8,128)S(1)}, f32[2,16,16,128]{3,2,1,0:T(8,128)S(1)}, u32[]{:S(2)}, u32[]{:S(2)}) %collective-permute-start.5) | collective-permute-done | bytes 262176 | tf_op jit(solution)/shard_map/ppermute | solution.py:592
  20.5 2.8 %columns.7.x_ref = f32[16,128,128]{2,1,0:T(8,128)} custom-call(f32[2,16,128,128]{3,2,1,0:T(8,128)S(1)} %get-tuple-element.33.x_ref, f32[2,16,16,128]{3,2,1,0:T(8,128)S(1)} %collective-permute-done.4.before_ref, f32[2,16,16,128]{3,2,1,0:T(8,128)S(1)} %collective-permute-done.5.after_ref, f32[4,40,128]{2,1,0:T(8,128)S(1)} %bitcast_bitcast_fusion.taps_ref), custom_call_target="tpu_custom_call" | custom-call | flops 20000000 | bytes 2500000 | tf_op jit(solution)/shard_map/columns/pallas_call | solution.py:207
  23.3 0.2 collective-permute-start.8
  23.5 1.6 %collective-permute-start.9 = (f32[16,128,128]{2,1,0:T(8,128)}, f32[16,128,128]{2,1,0:T(8,128)}, u32[]{:S(2)}, u32[]{:S(2)}) collective-permute-start(f32[16,128,128]{2,1,0:T(8,128)} %columns.7.x_ref), channel_id=1, source_target_pairs={{4,8},{8,4},{5,9},{9,5},{6,10},{10,6},{7,11},{11,7},{20,24},{24,20... | collective-permute-start | bytes 3145736 | tf_op jit(solution)/shard_map/ppermute | solution.py:598
  25.2 1.8 %columns.6.x_ref = f32[16,128,128]{2,1,0:T(8,128)S(1)} custom-call(f32[2,16,128,128]{3,2,1,0:T(8,128)S(1)} %get-tuple-element.33.x_ref, f32[2,16,16,128]{3,2,1,0:T(8,128)S(1)} %collective-permute-done.4.before_ref, f32[2,16,16,128]{3,2,1,0:T(8,128)S(1)} %collective-permute-done.5.after_ref, f32[4,40,128]{2,1,0:T(8,128)S(1)} %bitcast_bitcast_fusion.taps_ref), custom_call_target="tpu_custom_call" | custom-call | flops 20000000 | bytes 2500000 | tf_op jit(solution)/shard_map/columns/pallas_call | solution.py:207
  27.0 1.4 %collective-permute-start.6 = (f32[16,128,128]{2,1,0:T(8,128)S(1)}, f32[16,128,128]{2,1,0:T(8,128)}, u32[]{:S(2)}, u32[]{:S(2)}) collective-permute-start(f32[16,128,128]{2,1,0:T(8,128)S(1)} %columns.6.x_ref), channel_id=1, source_target_pairs={{0,4},{4,0},{8,12},{12,8},{1,5},{5,1},{9,13},{13,9},{2,6},{6,2},{1... | collective-permute-start | bytes 3145736 | tf_op jit(solution)/shard_map/ppermute | solution.py:599
  28.4 1.3 %copy-done.3 = f32[4096,128]{1,0:T(8,128)} copy-done((f32[4096,128]{1,0:T(8,128)}, f32[4096,128]{1,0:T(8,128)S(1)}, u32[]{:S(2)}) %copy-start.3) | copy-done | bytes 2097176
  29.7 1.6 %collective-permute-start.7 = (f32[16,128,128]{2,1,0:T(8,128)S(1)}, f32[16,128,128]{2,1,0:T(8,128)}, u32[]{:S(2)}, u32[]{:S(2)}) collective-permute-start(f32[16,128,128]{2,1,0:T(8,128)S(1)} %columns.6.x_ref), channel_id=1, source_target_pairs={{4,8},{8,4},{5,9},{9,5},{6,10},{10,6},{7,11},{11,7},{20,24},{24,20... | collective-permute-start | bytes 3145736 | tf_op jit(solution)/shard_map/ppermute | solution.py:598
  31.4 1.6 %copy-done.4 = f32[4096,128]{1,0:T(8,128)S(1)} copy-done((f32[4096,128]{1,0:T(8,128)S(1)}, f32[4096,128]{1,0:T(8,128)}, u32[]{:S(2)}) %copy-start.4) | copy-done | bytes 2097176
  32.9 7.1 %raw_rows.1 = (f32[2,16,128,128]{3,2,1,0:T(8,128)S(1)}, f32[2,16,16,128]{3,2,1,0:T(8,128)S(1)}, f32[2,16,16,128]{3,2,1,0:T(8,128)S(1)}) custom-call(s32[1]{0:T(128)} %bitcast.4.side_ref, f32[4096,128]{1,0:T(8,128)S(1)} %bitcast.16, f32[4096,128]{1,0:T(8,128)S(1)} %copy-done.4, f32[4096,128]{1,0:T(8,128)} %collective-permute-done.1.far_ref, ...), custom_call_target="tpu_custom_call" | custom-call | flops 60000000 | bytes 8000000 | tf_op jit(solution)/shard_map/raw_rows/pallas_call | solution.py:251
  40.0 3.5 %collective-permute-start.2 = (f32[2,16,16,128]{3,2,1,0:T(8,128)S(1)}, f32[2,16,16,128]{3,2,1,0:T(8,128)S(1)}, u32[]{:S(2)}, u32[]{:S(2)}) collective-permute-start(f32[2,16,16,128]{3,2,1,0:T(8,128)S(1)} %get-tuple-element.31), channel_id=1, source_target_pairs={{0,1},{1,2},{2,3},{4,5},{5,6},{6,7},{8,9},{9,10},{10,11},{12,13},{... | collective-permute-start | bytes 786440 | tf_op jit(solution)/shard_map/ppermute | solution.py:601
  43.5 1.5 %collective-permute-start.3 = (f32[2,16,16,128]{3,2,1,0:T(8,128)S(1)}, f32[2,16,16,128]{3,2,1,0:T(8,128)S(1)}, u32[]{:S(2)}, u32[]{:S(2)}) collective-permute-start(f32[2,16,16,128]{3,2,1,0:T(8,128)S(1)} %get-tuple-element.32), channel_id=1, source_target_pairs={{1,0},{2,1},{3,2},{5,4},{6,5},{7,6},{9,8},{10,9},{11,10},{13,12},{... | collective-permute-start | bytes 786440 | tf_op jit(solution)/shard_map/ppermute | solution.py:602
  45.0 3.6 %rows.3.refs_3_ = f32[128,2048]{1,0:T(8,128)S(1)} custom-call(s32[1]{0:T(128)} %bitcast.4.side_ref, f32[16,128,128]{2,1,0:T(8,128)} %columns.7.x_ref, f32[16,128,128]{2,1,0:T(8,128)} %collective-permute-done.8.near_ref, f32[16,128,128]{2,1,0:T(8,128)} %collective-permute-done.9.far_ref, f32[4,40,128]{2,1,0:T(8,128)S(1)} %bitcast_bitcast_fusion.taps_ref), custom_call_target="tpu_custom_call" | custom-call | flops 20000000 | bytes 4000000 | tf_op jit(solution)/shard_map/rows/pallas_call | solution.py:295
  48.6 3.5 %rows.2.refs_2_ = f32[128,2048]{1,0:T(8,128)S(1)} custom-call(s32[1]{0:T(128)} %bitcast.4.side_ref, f32[16,128,128]{2,1,0:T(8,128)S(1)} %columns.6.x_ref, f32[16,128,128]{2,1,0:T(8,128)} %collective-permute-done.6.near_ref, f32[16,128,128]{2,1,0:T(8,128)} %collective-permute-done.7.far_ref, f32[4,40,128]{2,1,0:T(8,128)S(1)} %bitcast_bitcast_fusion.taps_ref), custom_call_target="tpu_custom_call" | custom-call | flops 20000000 | bytes 4000000 | tf_op jit(solution)/shard_map/rows/pallas_call | solution.py:295
  52.2 2.3 %collective-permute-done.3.after_ref = f32[2,16,16,128]{3,2,1,0:T(8,128)S(1)} collective-permute-done((f32[2,16,16,128]{3,2,1,0:T(8,128)S(1)}, f32[2,16,16,128]{3,2,1,0:T(8,128)S(1)}, u32[]{:S(2)}, u32[]{:S(2)}) %collective-permute-start.3) | collective-permute-done | bytes 262176 | tf_op jit(solution)/shard_map/ppermute | solution.py:602
  54.5 2.3 %columns.5.refs_1_ = f32[128,2048]{1,0:T(8,128)S(1)} custom-call(f32[2,16,128,128]{3,2,1,0:T(8,128)S(1)} %get-tuple-element.30.x_ref, f32[2,16,16,128]{3,2,1,0:T(8,128)S(1)} %collective-permute-done.2.before_ref, f32[2,16,16,128]{3,2,1,0:T(8,128)S(1)} %collective-permute-done.3.after_ref, f32[4,40,128]{2,1,0:T(8,128)S(1)} %bitcast_bitcast_fusion.taps_ref), custom_call_target="tpu_custom_call" | custom-call | flops 20000000 | bytes 2500000 | tf_op jit(solution)/shard_map/columns/pallas_call | solution.py:207
  56.8 2.4 %columns.4.refs_0_ = f32[128,2048]{1,0:T(8,128)S(1)} custom-call(f32[2,16,128,128]{3,2,1,0:T(8,128)S(1)} %get-tuple-element.30.x_ref, f32[2,16,16,128]{3,2,1,0:T(8,128)S(1)} %collective-permute-done.2.before_ref, f32[2,16,16,128]{3,2,1,0:T(8,128)S(1)} %collective-permute-done.3.after_ref, f32[4,40,128]{2,1,0:T(8,128)S(1)} %bitcast_bitcast_fusion.taps_ref), custom_call_target="tpu_custom_call" | custom-call | flops 20000000 | bytes 2500000 | tf_op jit(solution)/shard_map/columns/pallas_call | solution.py:207
  59.2 3.2 %gram.1 = (f32[320,128]{1,0:T(8,128)S(1)}, f32[320,128]{1,0:T(8,128)}, f32[320,128]{1,0:T(8,128)}, f32[320,128]{1,0:T(8,128)}, f32[8,512]{1,0:T(8,128)S(1)}) custom-call(s32[1]{0:T(128)} %bitcast.me_ref, f32[4,512]{1,0:T(4,128)S(1)} %multiply_cosine_fusion.cosine_ref, f32[128,2048]{1,0:T(8,128)S(1)} %columns.4.refs_0_, f32[128,2048]{1,0:T(8,128)S(1)} %columns.5.refs_1_, ...), custom_call_target="tpu_custom_call" | custom-call | flops 4000000000 | bytes 5000000 | tf_op jit(solution)/shard_map/gram/pallas_call | solution.py:344
  62.4 2.6 %collective-permute-start.10 = (f32[320,128]{1,0:T(8,128)}, f32[320,128]{1,0:T(8,128)S(1)}, u32[]{:S(2)}, u32[]{:S(2)}) collective-permute-start(f32[320,128]{1,0:T(8,128)} %get-tuple-element.38), channel_id=1, source_target_pairs={{0,4},{4,0},{8,12},{12,8},{1,5},{5,1},{9,13},{13,9},{2,6},{6,2},{1... | collective-permute-start | bytes 491528 | tf_op jit(solution)/shard_map/ppermute | solution.py:423
  65.0 1.4 %collective-permute-start.11 = (f32[320,128]{1,0:T(8,128)}, f32[320,128]{1,0:T(8,128)}, u32[]{:S(2)}, u32[]{:S(2)}) collective-permute-start(f32[320,128]{1,0:T(8,128)} %get-tuple-element.39), channel_id=1, source_target_pairs={{0,8},{4,12},{8,0},{12,4},{1,9},{5,13},{9,1},{13,5},{2,10},{6,14},... | collective-permute-start | bytes 491528 | tf_op jit(solution)/shard_map/ppermute | solution.py:423
  66.4 0.1 collective-permute-start.12
  66.5 5.8 %collective-permute-done.11.refs_2_ = f32[320,128]{1,0:T(8,128)} collective-permute-done((f32[320,128]{1,0:T(8,128)}, f32[320,128]{1,0:T(8,128)}, u32[]{:S(2)}, u32[]{:S(2)}) %collective-permute-start.11) | collective-permute-done | bytes 163872 | tf_op jit(solution)/shard_map/ppermute | solution.py:423
  72.4 2.0 %collective-permute-done.12.refs_3_ = f32[320,128]{1,0:T(8,128)} collective-permute-done((f32[320,128]{1,0:T(8,128)}, f32[320,128]{1,0:T(8,128)}, u32[]{:S(2)}, u32[]{:S(2)}) %collective-permute-start.12) | collective-permute-done | bytes 163872 | tf_op jit(solution)/shard_map/ppermute | solution.py:423
  74.4 1.5 %sum_and_split.1 = (f32[80,128]{1,0:T(8,128)S(1)}, f32[80,128]{1,0:T(8,128)S(1)}, f32[80,128]{1,0:T(8,128)S(1)}, f32[80,128]{1,0:T(8,128)S(1)}) custom-call(s32[1]{0:T(128)} %bitcast.5.me_ref, f32[320,128]{1,0:T(8,128)S(1)} %get-tuple-element.37.refs_0_, f32[320,128]{1,0:T(8,128)S(1)} %collective-permute-done.10.refs_1_, ...), custom_call_target="tpu_custom_call" | custom-call | tf_op jit(solution)/shard_map/sum_and_split/pallas_call | solution.py:377
  75.8 1.8 %collective-permute-start.13 = (f32[80,128]{1,0:T(8,128)S(1)}, f32[80,128]{1,0:T(8,128)S(1)}, u32[]{:S(2)}, u32[]{:S(2)}) collective-permute-start(f32[80,128]{1,0:T(8,128)S(1)} %get-tuple-element.42), channel_id=1, source_target_pairs={{0,1},{1,0},{2,3},{3,2},{4,5},{5,4},{6,7},{7,6},{8,9},{9,8},{10,11... | collective-permute-start | bytes 122888 | tf_op jit(solution)/shard_map/ppermute | solution.py:423
  77.6 2.4 %collective-permute-start.14 = (f32[80,128]{1,0:T(8,128)S(1)}, f32[80,128]{1,0:T(8,128)S(1)}, u32[]{:S(2)}, u32[]{:S(2)}) collective-permute-start(f32[80,128]{1,0:T(8,128)S(1)} %get-tuple-element.43), channel_id=1, source_target_pairs={{0,2},{1,3},{2,0},{3,1},{4,6},{5,7},{6,4},{7,5},{8,10},{9,11},{10,... | collective-permute-start | bytes 122888 | tf_op jit(solution)/shard_map/ppermute | solution.py:423
  80.1 0.2 collective-permute-start.15
  80.3 3.4 %collective-permute-done.14 = f32[80,128]{1,0:T(8,128)S(1)} collective-permute-done((f32[80,128]{1,0:T(8,128)S(1)}, f32[80,128]{1,0:T(8,128)S(1)}, u32[]{:S(2)}, u32[]{:S(2)}) %collective-permute-start.14) | collective-permute-done | bytes 40992 | tf_op jit(solution)/shard_map/ppermute | solution.py:423
  83.6 2.2 %collective-permute-done.15 = f32[80,128]{1,0:T(8,128)S(1)} collective-permute-done((f32[80,128]{1,0:T(8,128)S(1)}, f32[80,128]{1,0:T(8,128)S(1)}, u32[]{:S(2)}, u32[]{:S(2)}) %collective-permute-start.15) | collective-permute-done | bytes 40992 | tf_op jit(solution)/shard_map/ppermute | solution.py:423
  86.0 1.7 %collective-permute-start.17 = (f32[80,128]{1,0:T(8,128)S(1)}, f32[80,128]{1,0:T(8,128)S(1)}, u32[]{:S(2)}, u32[]{:S(2)}) collective-permute-start(f32[80,128]{1,0:T(8,128)S(1)} %add_add_fusion.refs_0_), channel_id=1, source_target_pairs={{0,2},{1,3},{2,0},{3,1},{4,6},{5,7},{6,4},{7,5},{8,10},{9,11},{10,... | collective-permute-start | bytes 122888 | tf_op jit(solution)/shard_map/ppermute | solution.py:423
  87.6 2.7 %collective-permute-start.18 = (f32[80,128]{1,0:T(8,128)S(1)}, f32[80,128]{1,0:T(8,128)S(1)}, u32[]{:S(2)}, u32[]{:S(2)}) collective-permute-start(f32[80,128]{1,0:T(8,128)S(1)} %add_add_fusion.refs_0_), channel_id=1, source_target_pairs={{0,3},{1,2},{2,1},{3,0},{4,7},{5,6},{6,5},{7,4},{8,11},{9,10},{10,... | collective-permute-start | bytes 122888 | tf_op jit(solution)/shard_map/ppermute | solution.py:423
  90.3 1.0 collective-permute-done.17.refs_2_
  91.4 2.1 %collective-permute-done.18.refs_3_ = f32[80,128]{1,0:T(8,128)S(1)} collective-permute-done((f32[80,128]{1,0:T(8,128)S(1)}, f32[80,128]{1,0:T(8,128)S(1)}, u32[]{:S(2)}, u32[]{:S(2)}) %collective-permute-start.18) | collective-permute-done | bytes 40992 | tf_op jit(solution)/shard_map/ppermute | solution.py:423
  93.4 0.2 join.1.refs_4_
  93.8 1.7 %collective-permute-start.20 = (f32[320,128]{1,0:T(8,128)S(1)}, f32[320,128]{1,0:T(8,128)S(1)}, u32[]{:S(2)}, u32[]{:S(2)}) collective-permute-start(f32[320,128]{1,0:T(8,128)S(1)} %join.1.refs_4_), channel_id=1, source_target_pairs={{0,8},{4,12},{8,0},{12,4},{1,9},{5,13},{9,1},{13,5},{2,10},{6,14},... | collective-permute-start | bytes 491528 | tf_op jit(solution)/shard_map/ppermute | solution.py:423
  95.4 0.2 collective-permute-start.21
  95.6 5.3 %collective-permute-done.20.refs_6_ = f32[320,128]{1,0:T(8,128)S(1)} collective-permute-done((f32[320,128]{1,0:T(8,128)S(1)}, f32[320,128]{1,0:T(8,128)S(1)}, u32[]{:S(2)}, u32[]{:S(2)}) %collective-permute-start.20) | collective-permute-done | bytes 163872 | tf_op jit(solution)/shard_map/ppermute | solution.py:423
  100.9 2.4 %collective-permute-done.21.refs_7_ = f32[320,128]{1,0:T(8,128)S(1)} collective-permute-done((f32[320,128]{1,0:T(8,128)S(1)}, f32[320,128]{1,0:T(8,128)S(1)}, u32[]{:S(2)}, u32[]{:S(2)}) %collective-permute-start.21) | collective-permute-done | bytes 163872 | tf_op jit(solution)/shard_map/ppermute | solution.py:423
  103.3 1.2 %copy-done.2 = f32[128,2048]{1,0:T(8,128)S(1)} copy-done((f32[128,2048]{1,0:T(8,128)S(1)}, f32[128,2048]{1,0:T(8,128)}, u32[]{:S(2)}) %copy-start.2) | copy-done | bytes 1048600
  104.5 12.4 %clean.1 = f32[8192,128]{1,0:T(8,128)} custom-call(s32[1]{0:T(128)} %bitcast.me_ref, f32[8,512]{1,0:T(8,128)S(1)} %get-tuple-element.36.start_ref, f32[128,2048]{1,0:T(8,128)S(1)} %copy-done.2, f32[128,2048]{1,0:T(8,128)S(1)} %columns.5.refs_1_, f32[128,2048]{1,0:T(8,128)S(1)} %rows.2.refs_2_, f32[128,2048]{1,0:T(8,128)S(1)} %rows.3.refs_3_, ...), custom_call_target="tpu_custom_call" | custom-call | flops 40000000 | bytes 9000000 | tf_op jit(solution)/shard_map/clean/pallas_call | solution.py:545
  (26 shorter events, 0.2 us)
Async XLA Ops:
  0.0 4.5 %copy-start = (f32[512,16,128]{2,1,0:T(8,128)S(1)}, f32[512,16,128]{2,1,0:T(8,128)}, u32[]{:S(2)}) copy-start(f32[512,16,128]{2,1,0:T(8,128)} %param.2) | copy-start | bytes 12582916
  1.9 9.2 %copy-start.5 = (f32[512,33]{0,1:T(8,128)S(1)}, f32[512,33]{0,1:T(8,128)}, u32[]{:S(2)}) copy-start(f32[512,33]{0,1:T(8,128)} %param.3) | copy-start | bytes 202756
  1.9 26.5 %collective-permute-start = (f32[4096,128]{1,0:T(8,128)S(1)}, f32[4096,128]{1,0:T(8,128)S(1)}, u32[]{:S(2)}, u32[]{:S(2)}) collective-permute-start(f32[4096,128]{1,0:T(8,128)S(1)} %bitcast.14), channel_id=1, source_target_pairs={{0,4},{4,0},{8,12},{12,8},{1,5},{5,1},{9,13},{13,9},{2,6},{6,2},{1... | collective-permute-start | bytes 6291464 | tf_op jit(solution)/shard_map/ppermute | solution.py:589
  2.5 28.9 %collective-permute-start.1 = (f32[4096,128]{1,0:T(8,128)S(1)}, f32[4096,128]{1,0:T(8,128)}, u32[]{:S(2)}, u32[]{:S(2)}) collective-permute-start(f32[4096,128]{1,0:T(8,128)S(1)} %bitcast.15), channel_id=1, source_target_pairs={{4,8},{8,4},{5,9},{9,5},{6,10},{10,6},{7,11},{11,7},{20,24},{24,20... | collective-permute-start | bytes 6291464 | tf_op jit(solution)/shard_map/ppermute | solution.py:588
  5.2 10.6 %collective-permute-start.4 = (f32[2,16,16,128]{3,2,1,0:T(8,128)S(1)}, f32[2,16,16,128]{3,2,1,0:T(8,128)S(1)}, u32[]{:S(2)}, u32[]{:S(2)}) collective-permute-start(f32[2,16,16,128]{3,2,1,0:T(8,128)S(1)} %get-tuple-element.34), channel_id=1, source_target_pairs={{0,1},{1,2},{2,3},{4,5},{5,6},{6,7},{8,9},{9,10},{10,11},{12,13},{... | collective-permute-start | bytes 786440 | tf_op jit(solution)/shard_map/ppermute | solution.py:591
  9.7 10.8 %collective-permute-start.5 = (f32[2,16,16,128]{3,2,1,0:T(8,128)S(1)}, f32[2,16,16,128]{3,2,1,0:T(8,128)S(1)}, u32[]{:S(2)}, u32[]{:S(2)}) collective-permute-start(f32[2,16,16,128]{3,2,1,0:T(8,128)S(1)} %get-tuple-element.35), channel_id=1, source_target_pairs={{1,0},{2,1},{3,2},{5,4},{6,5},{7,6},{9,8},{10,9},{11,10},{13,12},{... | collective-permute-start | bytes 786440 | tf_op jit(solution)/shard_map/ppermute | solution.py:592
  23.3 20.2 %collective-permute-start.8 = (f32[16,128,128]{2,1,0:T(8,128)}, f32[16,128,128]{2,1,0:T(8,128)}, u32[]{:S(2)}, u32[]{:S(2)}) collective-permute-start(f32[16,128,128]{2,1,0:T(8,128)} %columns.7.x_ref), channel_id=1, source_target_pairs={{0,4},{4,0},{8,12},{12,8},{1,5},{5,1},{9,13},{13,9},{2,6},{6,2},{1... | collective-permute-start | bytes 3145736 | tf_op jit(solution)/shard_map/ppermute | solution.py:599
  23.5 21.5 %collective-permute-start.9 = (f32[16,128,128]{2,1,0:T(8,128)}, f32[16,128,128]{2,1,0:T(8,128)}, u32[]{:S(2)}, u32[]{:S(2)}) collective-permute-start(f32[16,128,128]{2,1,0:T(8,128)} %columns.7.x_ref), channel_id=1, source_target_pairs={{4,8},{8,4},{5,9},{9,5},{6,10},{10,6},{7,11},{11,7},{20,24},{24,20... | collective-permute-start | bytes 3145736 | tf_op jit(solution)/shard_map/ppermute | solution.py:598
  27.0 21.6 %collective-permute-start.6 = (f32[16,128,128]{2,1,0:T(8,128)S(1)}, f32[16,128,128]{2,1,0:T(8,128)}, u32[]{:S(2)}, u32[]{:S(2)}) collective-permute-start(f32[16,128,128]{2,1,0:T(8,128)S(1)} %columns.6.x_ref), channel_id=1, source_target_pairs={{0,4},{4,0},{8,12},{12,8},{1,5},{5,1},{9,13},{13,9},{2,6},{6,2},{1... | collective-permute-start | bytes 3145736 | tf_op jit(solution)/shard_map/ppermute | solution.py:599
  28.4 1.3 %copy-start.3 = (f32[4096,128]{1,0:T(8,128)}, f32[4096,128]{1,0:T(8,128)S(1)}, u32[]{:S(2)}) copy-start(f32[4096,128]{1,0:T(8,128)S(1)} %collective-permute-done.near_ref) | copy-start | bytes 6291460
  29.7 18.9 %collective-permute-start.7 = (f32[16,128,128]{2,1,0:T(8,128)S(1)}, f32[16,128,128]{2,1,0:T(8,128)}, u32[]{:S(2)}, u32[]{:S(2)}) collective-permute-start(f32[16,128,128]{2,1,0:T(8,128)S(1)} %columns.6.x_ref), channel_id=1, source_target_pairs={{4,8},{8,4},{5,9},{9,5},{6,10},{10,6},{7,11},{11,7},{20,24},{24,20... | collective-permute-start | bytes 3145736 | tf_op jit(solution)/shard_map/ppermute | solution.py:598
  31.4 1.6 %copy-start.4 = (f32[4096,128]{1,0:T(8,128)S(1)}, f32[4096,128]{1,0:T(8,128)}, u32[]{:S(2)}) copy-start(f32[4096,128]{1,0:T(8,128)} %copy-done.3) | copy-start | bytes 6291460
  40.0 12.2 %collective-permute-start.2 = (f32[2,16,16,128]{3,2,1,0:T(8,128)S(1)}, f32[2,16,16,128]{3,2,1,0:T(8,128)S(1)}, u32[]{:S(2)}, u32[]{:S(2)}) collective-permute-start(f32[2,16,16,128]{3,2,1,0:T(8,128)S(1)} %get-tuple-element.31), channel_id=1, source_target_pairs={{0,1},{1,2},{2,3},{4,5},{5,6},{6,7},{8,9},{9,10},{10,11},{12,13},{... | collective-permute-start | bytes 786440 | tf_op jit(solution)/shard_map/ppermute | solution.py:601
  43.5 10.9 %collective-permute-start.3 = (f32[2,16,16,128]{3,2,1,0:T(8,128)S(1)}, f32[2,16,16,128]{3,2,1,0:T(8,128)S(1)}, u32[]{:S(2)}, u32[]{:S(2)}) collective-permute-start(f32[2,16,16,128]{3,2,1,0:T(8,128)S(1)} %get-tuple-element.32), channel_id=1, source_target_pairs={{1,0},{2,1},{3,2},{5,4},{6,5},{7,6},{9,8},{10,9},{11,10},{13,12},{... | collective-permute-start | bytes 786440 | tf_op jit(solution)/shard_map/ppermute | solution.py:602
  59.2 3.2 %copy-start.1 = (f32[128,2048]{1,0:T(8,128)}, f32[128,2048]{1,0:T(8,128)S(1)}, u32[]{:S(2)}) copy-start(f32[128,2048]{1,0:T(8,128)S(1)} %columns.4.refs_0_) | copy-start | bytes 3145732
  62.4 4.1 %collective-permute-start.10 = (f32[320,128]{1,0:T(8,128)}, f32[320,128]{1,0:T(8,128)S(1)}, u32[]{:S(2)}, u32[]{:S(2)}) collective-permute-start(f32[320,128]{1,0:T(8,128)} %get-tuple-element.38), channel_id=1, source_target_pairs={{0,4},{4,0},{8,12},{12,8},{1,5},{5,1},{9,13},{13,9},{2,6},{6,2},{1... | collective-permute-start | bytes 491528 | tf_op jit(solution)/shard_map/ppermute | solution.py:423
  65.0 7.4 %collective-permute-start.11 = (f32[320,128]{1,0:T(8,128)}, f32[320,128]{1,0:T(8,128)}, u32[]{:S(2)}, u32[]{:S(2)}) collective-permute-start(f32[320,128]{1,0:T(8,128)} %get-tuple-element.39), channel_id=1, source_target_pairs={{0,8},{4,12},{8,0},{12,4},{1,9},{5,13},{9,1},{13,5},{2,10},{6,14},... | collective-permute-start | bytes 491528 | tf_op jit(solution)/shard_map/ppermute | solution.py:423
  66.4 8.0 %collective-permute-start.12 = (f32[320,128]{1,0:T(8,128)}, f32[320,128]{1,0:T(8,128)}, u32[]{:S(2)}, u32[]{:S(2)}) collective-permute-start(f32[320,128]{1,0:T(8,128)} %get-tuple-element.40), channel_id=1, source_target_pairs={{0,12},{4,8},{8,4},{12,0},{1,13},{5,9},{9,5},{13,1},{2,14},{6,10},... | collective-permute-start | bytes 491528 | tf_op jit(solution)/shard_map/ppermute | solution.py:423
  75.8 4.5 %collective-permute-start.13 = (f32[80,128]{1,0:T(8,128)S(1)}, f32[80,128]{1,0:T(8,128)S(1)}, u32[]{:S(2)}, u32[]{:S(2)}) collective-permute-start(f32[80,128]{1,0:T(8,128)S(1)} %get-tuple-element.42), channel_id=1, source_target_pairs={{0,1},{1,0},{2,3},{3,2},{4,5},{5,4},{6,7},{7,6},{8,9},{9,8},{10,11... | collective-permute-start | bytes 122888 | tf_op jit(solution)/shard_map/ppermute | solution.py:423
  77.6 6.0 %collective-permute-start.14 = (f32[80,128]{1,0:T(8,128)S(1)}, f32[80,128]{1,0:T(8,128)S(1)}, u32[]{:S(2)}, u32[]{:S(2)}) collective-permute-start(f32[80,128]{1,0:T(8,128)S(1)} %get-tuple-element.43), channel_id=1, source_target_pairs={{0,2},{1,3},{2,0},{3,1},{4,6},{5,7},{6,4},{7,5},{8,10},{9,11},{10,... | collective-permute-start | bytes 122888 | tf_op jit(solution)/shard_map/ppermute | solution.py:423
  80.1 5.8 %collective-permute-start.15 = (f32[80,128]{1,0:T(8,128)S(1)}, f32[80,128]{1,0:T(8,128)S(1)}, u32[]{:S(2)}, u32[]{:S(2)}) collective-permute-start(f32[80,128]{1,0:T(8,128)S(1)} %get-tuple-element.44), channel_id=1, source_target_pairs={{0,3},{1,2},{2,1},{3,0},{4,7},{5,6},{6,5},{7,4},{8,11},{9,10},{10,... | collective-permute-start | bytes 122888 | tf_op jit(solution)/shard_map/ppermute | solution.py:423
  85.9 4.5 %collective-permute-start.16 = (f32[80,128]{1,0:T(8,128)S(1)}, f32[80,128]{1,0:T(8,128)S(1)}, u32[]{:S(2)}, u32[]{:S(2)}) collective-permute-start(f32[80,128]{1,0:T(8,128)S(1)} %add_add_fusion.refs_0_), channel_id=1, source_target_pairs={{0,1},{1,0},{2,3},{3,2},{4,5},{5,4},{6,7},{7,6},{8,9},{9,8},{10,11... | collective-permute-start | bytes 122888 | tf_op jit(solution)/shard_map/ppermute | solution.py:423
  86.0 5.4 %collective-permute-start.17 = (f32[80,128]{1,0:T(8,128)S(1)}, f32[80,128]{1,0:T(8,128)S(1)}, u32[]{:S(2)}, u32[]{:S(2)}) collective-permute-start(f32[80,128]{1,0:T(8,128)S(1)} %add_add_fusion.refs_0_), channel_id=1, source_target_pairs={{0,2},{1,3},{2,0},{3,1},{4,6},{5,7},{6,4},{7,5},{8,10},{9,11},{10,... | collective-permute-start | bytes 122888 | tf_op jit(solution)/shard_map/ppermute | solution.py:423
  87.6 5.8 %collective-permute-start.18 = (f32[80,128]{1,0:T(8,128)S(1)}, f32[80,128]{1,0:T(8,128)S(1)}, u32[]{:S(2)}, u32[]{:S(2)}) collective-permute-start(f32[80,128]{1,0:T(8,128)S(1)} %add_add_fusion.refs_0_), channel_id=1, source_target_pairs={{0,3},{1,2},{2,1},{3,0},{4,7},{5,6},{6,5},{7,4},{8,11},{9,10},{10,... | collective-permute-start | bytes 122888 | tf_op jit(solution)/shard_map/ppermute | solution.py:423
  93.7 1.9 %collective-permute-start.19 = (f32[320,128]{1,0:T(8,128)S(1)}, f32[320,128]{1,0:T(8,128)S(1)}, u32[]{:S(2)}, u32[]{:S(2)}) collective-permute-start(f32[320,128]{1,0:T(8,128)S(1)} %join.1.refs_4_), channel_id=1, source_target_pairs={{0,4},{4,0},{8,12},{12,8},{1,5},{5,1},{9,13},{13,9},{2,6},{6,2},{1... | collective-permute-start | bytes 491528 | tf_op jit(solution)/shard_map/ppermute | solution.py:423
  93.8 7.1 %collective-permute-start.20 = (f32[320,128]{1,0:T(8,128)S(1)}, f32[320,128]{1,0:T(8,128)S(1)}, u32[]{:S(2)}, u32[]{:S(2)}) collective-permute-start(f32[320,128]{1,0:T(8,128)S(1)} %join.1.refs_4_), channel_id=1, source_target_pairs={{0,8},{4,12},{8,0},{12,4},{1,9},{5,13},{9,1},{13,5},{2,10},{6,14},... | collective-permute-start | bytes 491528 | tf_op jit(solution)/shard_map/ppermute | solution.py:423
  95.4 7.9 %collective-permute-start.21 = (f32[320,128]{1,0:T(8,128)S(1)}, f32[320,128]{1,0:T(8,128)S(1)}, u32[]{:S(2)}, u32[]{:S(2)}) collective-permute-start(f32[320,128]{1,0:T(8,128)S(1)} %join.1.refs_4_), channel_id=1, source_target_pairs={{0,12},{4,8},{8,4},{12,0},{1,13},{5,9},{9,5},{13,1},{2,14},{6,10},... | collective-permute-start | bytes 491528 | tf_op jit(solution)/shard_map/ppermute | solution.py:423
  103.3 1.2 %copy-start.2 = (f32[128,2048]{1,0:T(8,128)S(1)}, f32[128,2048]{1,0:T(8,128)}, u32[]{:S(2)}) copy-start(f32[128,2048]{1,0:T(8,128)} %copy-done.1) | copy-start | bytes 3145732

commit v4 on v3

--- a/solution.py
+++ b/solution.py
@@ -16,7 +16,7 @@
 VM = pl.BlockSpec(memory_space=pltpu.VMEM)
 SM = pl.BlockSpec(memory_space=pltpu.SMEM)
 f32 = jnp.float32
-GRANT = pltpu.CompilerParams(vmem_limit_bytes=24 * 2**20)
+GRANT = pltpu.CompilerParams(vmem_limit_bytes=16 * 2**20)
 
 
 def shape(*dims):
@@ -459,14 +459,10 @@
             wide[k, c:c + LANES, :] = jnp.broadcast_to(tall[:, k:k + 1], (LANES, LANES))
 
 
-def load_all(xs, x_buf, sems):
-    return start_all([(x, x_buf.at[pl.ds(k * LANES, LANES)]) for k, x in enumerate(xs)], sems)
-
-
-def project(x_buf, wide, part, channels):
+def project(xs, wide, part, channels):
     totals = [None] * MODES
     for c in range(0, channels, SUB):
-        x = x_buf[c:c + SUB, part]
+        x = xs[c // LANES][c % LANES:c % LANES + SUB, part]
         for k in range(MODES):
             term = wide[k, c:c + SUB, :] * x
             totals[k] = term if totals[k] is None else totals[k] + term
@@ -475,10 +471,9 @@
 
 def clean_kernel(chunks, peers, rows, cols, me_ref, start_ref, *refs):
     xs, pieces, out_ref = refs[:chunks], refs[chunks:chunks + peers], refs[chunks + peers]
-    x_buf, packed, gram, wide, coef, out_buf, sems, piece_sems, out_sems = refs[chunks + peers + 1:]
+    packed, gram, wide, coef, out_buf, piece_sems, out_sems = refs[chunks + peers + 1:]
     channels = chunks * LANES
     placed = place(pieces, packed, me_ref[0], piece_sems)
-    started = load_all(xs, x_buf, sems)
     for copy in placed:
         copy.wait()
     diagonal = jnp.zeros((1, LANES), f32)
@@ -492,8 +487,7 @@
         else:
             diagonal = diagonal + jnp.sum(jnp.where(row_id == col_id, block, 0.0), axis=0, keepdims=True)
     scale = channels / jnp.sum(diagonal, axis=1, keepdims=True)
-    basis = start_ref[...]
-    for sweep in range(SWEEPS):
+    def sweep(turn, basis):
         spread(basis, wide, channels)
         vectors = []
         for k in range(MODES):
@@ -502,18 +496,16 @@
                 lanes = slice(t * LANES, (t + 1) * LANES)
                 total = None
                 for c in range(0, channels, SUB):
-                    term = wide[k, c:c + SUB, :] * gram[c:c + SUB, lanes]
-                    total = term if total is None else total + term
+                    total = add_to(total, wide[k, c:c + SUB, :] * gram[c:c + SUB, lanes])
                 row.append(jnp.sum(total, axis=0, keepdims=True))
             vectors.append(jnp.concatenate(row, axis=1) * scale)
         new = orthonormal_rows(vectors, channels)
-        basis = jnp.concatenate(new + [jnp.zeros((SUB - MODES, channels), f32)], axis=0)
-    spread(basis, wide, channels)
-    for copy in started:
-        copy.wait()
+        return jnp.concatenate(new + [jnp.zeros((SUB - MODES, channels), f32)], axis=0)
+
+    spread(lax.fori_loop(0, SWEEPS, sweep, start_ref[...]), wide, channels)
 
     def coefficients(r, carry):
-        values = project(x_buf, wide, pl.ds(pl.multiple_of(r * cols, cols), cols), channels)
+        values = project(xs, wide, pl.ds(pl.multiple_of(r * cols, cols), cols), channels)
         for k in range(MODES):
             coef[r, k] = values[k]
         return carry
@@ -528,7 +520,8 @@
                 model = wide[0, c:c + SUB, :] * factors[0]
                 for k in range(1, MODES):
                     model = model + wide[k, c:c + SUB, :] * factors[k]
-                out_buf[pl.ds(c * rows + r, SUB, stride=rows), :] = x_buf[c:c + SUB, part] - model
+                here = c - n * LANES
+                out_buf[pl.ds(c * rows + r, SUB, stride=rows), :] = xs[n][here:here + SUB, part] - model
             return carry
 
         lax.fori_loop(0, rows, subtract, 0)
@@ -544,17 +537,15 @@
     chunks, channels = len(xs), len(xs) * LANES
     return pl.pallas_call(
         functools.partial(clean_kernel, chunks, len(pieces), rows, cols),
-        in_specs=[SM, VM] + [ANY] * (chunks + len(pieces)),
+        in_specs=[SM, VM] + [VM] * chunks + [ANY] * len(pieces),
         out_specs=ANY,
         out_shape=shape(channels * rows, cols),
         scratch_shapes=[
-            pltpu.VMEM((channels, rows * cols), f32),
             pltpu.VMEM((len(upper(chunks)) * LANES, LANES), f32),
             pltpu.VMEM((channels, channels), f32),
             pltpu.VMEM((MODES, channels, LANES), f32),
             pltpu.VMEM((rows, MODES, SUB, LANES), f32),
             pltpu.VMEM((channels * rows, cols), f32),
-            pltpu.SemaphoreType.DMA((chunks,)),
             pltpu.SemaphoreType.DMA((len(pieces),)),
             pltpu.SemaphoreType.DMA((chunks,)),
         ],

time: 117 us -> 116 us (level)
  Pallas kernels: 41.5 us -> 40.3 us
    pallas_call x1, Pallas kernels: 12.4 us -> 11.2 us  [clean(): pl.pallas_call(functools.partial(clean_kernel, chunks, len(pieces), rows,...]
where the time goes in v4:
time: 116 us
  Pallas kernels  40.3 us (35%)
  waiting for transfers between devices  35.8 us (31%)
  starting transfers between devices  33.1 us (29%)
  local copies, waits for them, and re-layouts  6.04 us (5%)
    ppermute x12, waiting for transfers between devices, exchange(): lax.ppermute(pieces[d], axis, [(i, i ^ d) for i in range(peers)])  24.2 us
    ppermute x12, starting transfers between devices, exchange(): lax.ppermute(pieces[d], axis, [(i, i ^ d) for i in range(peers)])  14.9 us
    pallas_call x1, Pallas kernels, clean(): pl.pallas_call(functools.partial(clean_kernel, chunks, len(pieces), rows,...  11.2 us
    pallas_call x4, Pallas kernels, columns(): pl.pallas_call(functools.partial(columns_kernel, which, rows, cols, margi...  9.33 us
    pallas_call x2, Pallas kernels, rows_of(): pl.pallas_call(functools.partial(rows_kernel, rows, cols, margin, taps),...  7.12 us
    pallas_call x1, Pallas kernels, raw_rows(): pl.pallas_call(functools.partial(raw_rows_kernel, count, rows, cols, marg...  7.07 us
    ppermute x1, waiting for transfers between devices, per_device(): after = lax.ppermute(first, 'col', left)  4.69 us
    ppermute x1, waiting for transfers between devices, per_device(): before = lax.ppermute(last, 'col', right)  4.58 us
  transfers between devices with their start and end apart: 22, of which 11 were waited for; matrix products, arithmetic and copies ran while one was open for 0% of the time, Pallas kernels for 17%

profile of v4, /device:TPU:0, one launch (start us, length us, event | category | flops | bytes accessed | tf_op | source)
XLA Modules:
  0.0 115.9 jit_solution(14562798454270233785)
XLA Ops:
  0.0 1.9 %slice.6 = f32[256,16,128]{2,1,0:T(8,128)S(1)} slice(f32[512,16,128]{2,1,0:T(8,128)} %param.2), slice={[0:256], [0:16], [0:128]} | slice | bytes 4194304 | tf_op jit(solution)/shard_map/slice | solution.py:578
  1.9 0.6 collective-permute-start
  2.5 2.0 %collective-permute-start.1 = (f32[4096,128]{1,0:T(8,128)S(1)}, f32[4096,128]{1,0:T(8,128)}, u32[]{:S(2)}, u32[]{:S(2)}) collective-permute-start(f32[4096,128]{1,0:T(8,128)S(1)} %bitcast.15), channel_id=1, source_target_pairs={{4,8},{8,4},{5,9},{9,5},{6,10},{10,6},{7,11},{11,7},{20,24},{24,20... | collective-permute-start | bytes 6291464 | tf_op jit(solution)/shard_map/ppermute | solution.py:579
  4.5 0.8 prep.1
  5.2 4.5 %collective-permute-start.4 = (f32[2,16,16,128]{3,2,1,0:T(8,128)S(1)}, f32[2,16,16,128]{3,2,1,0:T(8,128)S(1)}, u32[]{:S(2)}, u32[]{:S(2)}) collective-permute-start(f32[2,16,16,128]{3,2,1,0:T(8,128)S(1)} %get-tuple-element.34), channel_id=1, source_target_pairs={{0,1},{1,2},{2,3},{4,5},{5,6},{6,7},{8,9},{9,10},{10,11},{12,13},{... | collective-permute-start | bytes 786440 | tf_op jit(solution)/shard_map/ppermute | solution.py:582
  9.7 1.3 %collective-permute-start.5 = (f32[2,16,16,128]{3,2,1,0:T(8,128)S(1)}, f32[2,16,16,128]{3,2,1,0:T(8,128)S(1)}, u32[]{:S(2)}, u32[]{:S(2)}) collective-permute-start(f32[2,16,16,128]{3,2,1,0:T(8,128)S(1)} %get-tuple-element.35), channel_id=1, source_target_pairs={{1,0},{2,1},{3,2},{5,4},{6,5},{7,6},{9,8},{10,9},{11,10},{13,12},{... | collective-permute-start | bytes 786440 | tf_op jit(solution)/shard_map/ppermute | solution.py:583
  11.1 0.1 multiply_cosine_fusion.cosine_ref
  11.2 4.6 %collective-permute-done.4.before_ref = f32[2,16,16,128]{3,2,1,0:T(8,128)S(1)} collective-permute-done((f32[2,16,16,128]{3,2,1,0:T(8,128)S(1)}, f32[2,16,16,128]{3,2,1,0:T(8,128)S(1)}, u32[]{:S(2)}, u32[]{:S(2)}) %collective-permute-start.4) | collective-permute-done | bytes 262176 | tf_op jit(solution)/shard_map/ppermute | solution.py:582
  15.8 4.7 %collective-permute-done.5.after_ref = f32[2,16,16,128]{3,2,1,0:T(8,128)S(1)} collective-permute-done((f32[2,16,16,128]{3,2,1,0:T(8,128)S(1)}, f32[2,16,16,128]{3,2,1,0:T(8,128)S(1)}, u32[]{:S(2)}, u32[]{:S(2)}) %collective-permute-start.5) | collective-permute-done | bytes 262176 | tf_op jit(solution)/shard_map/ppermute | solution.py:583
  20.5 2.8 %columns.7.x_ref = f32[16,128,128]{2,1,0:T(8,128)} custom-call(f32[2,16,128,128]{3,2,1,0:T(8,128)S(1)} %get-tuple-element.33.x_ref, f32[2,16,16,128]{3,2,1,0:T(8,128)S(1)} %collective-permute-done.4.before_ref, f32[2,16,16,128]{3,2,1,0:T(8,128)S(1)} %collective-permute-done.5.after_ref, f32[4,40,128]{2,1,0:T(8,128)S(1)} %bitcast_bitcast_fusion.taps_ref), custom_call_target="tpu_custom_call" | custom-call | flops 20000000 | bytes 2500000 | tf_op jit(solution)/shard_map/columns/pallas_call | solution.py:207
  23.3 0.2 collective-permute-start.8
  23.5 1.6 %collective-permute-start.9 = (f32[16,128,128]{2,1,0:T(8,128)}, f32[16,128,128]{2,1,0:T(8,128)}, u32[]{:S(2)}, u32[]{:S(2)}) collective-permute-start(f32[16,128,128]{2,1,0:T(8,128)} %columns.7.x_ref), channel_id=1, source_target_pairs={{4,8},{8,4},{5,9},{9,5},{6,10},{10,6},{7,11},{11,7},{20,24},{24,20... | collective-permute-start | bytes 3145736 | tf_op jit(solution)/shard_map/ppermute | solution.py:589
  25.2 1.8 %columns.6.x_ref = f32[16,128,128]{2,1,0:T(8,128)S(1)} custom-call(f32[2,16,128,128]{3,2,1,0:T(8,128)S(1)} %get-tuple-element.33.x_ref, f32[2,16,16,128]{3,2,1,0:T(8,128)S(1)} %collective-permute-done.4.before_ref, f32[2,16,16,128]{3,2,1,0:T(8,128)S(1)} %collective-permute-done.5.after_ref, f32[4,40,128]{2,1,0:T(8,128)S(1)} %bitcast_bitcast_fusion.taps_ref), custom_call_target="tpu_custom_call" | custom-call | flops 20000000 | bytes 2500000 | tf_op jit(solution)/shard_map/columns/pallas_call | solution.py:207
  27.0 1.4 %collective-permute-start.6 = (f32[16,128,128]{2,1,0:T(8,128)S(1)}, f32[16,128,128]{2,1,0:T(8,128)}, u32[]{:S(2)}, u32[]{:S(2)}) collective-permute-start(f32[16,128,128]{2,1,0:T(8,128)S(1)} %columns.6.x_ref), channel_id=1, source_target_pairs={{0,4},{4,0},{8,12},{12,8},{1,5},{5,1},{9,13},{13,9},{2,6},{6,2},{1... | collective-permute-start | bytes 3145736 | tf_op jit(solution)/shard_map/ppermute | solution.py:590
  28.4 1.3 %copy-done.3 = f32[4096,128]{1,0:T(8,128)} copy-done((f32[4096,128]{1,0:T(8,128)}, f32[4096,128]{1,0:T(8,128)S(1)}, u32[]{:S(2)}) %copy-start.3) | copy-done | bytes 2097176
  29.7 1.6 %collective-permute-start.7 = (f32[16,128,128]{2,1,0:T(8,128)S(1)}, f32[16,128,128]{2,1,0:T(8,128)}, u32[]{:S(2)}, u32[]{:S(2)}) collective-permute-start(f32[16,128,128]{2,1,0:T(8,128)S(1)} %columns.6.x_ref), channel_id=1, source_target_pairs={{4,8},{8,4},{5,9},{9,5},{6,10},{10,6},{7,11},{11,7},{20,24},{24,20... | collective-permute-start | bytes 3145736 | tf_op jit(solution)/shard_map/ppermute | solution.py:589
  31.4 1.6 %copy-done.4 = f32[4096,128]{1,0:T(8,128)S(1)} copy-done((f32[4096,128]{1,0:T(8,128)S(1)}, f32[4096,128]{1,0:T(8,128)}, u32[]{:S(2)}) %copy-start.4) | copy-done | bytes 2097176
  32.9 7.1 %raw_rows.1 = (f32[2,16,128,128]{3,2,1,0:T(8,128)S(1)}, f32[2,16,16,128]{3,2,1,0:T(8,128)S(1)}, f32[2,16,16,128]{3,2,1,0:T(8,128)S(1)}) custom-call(s32[1]{0:T(128)} %bitcast.4.side_ref, f32[4096,128]{1,0:T(8,128)S(1)} %bitcast.16, f32[4096,128]{1,0:T(8,128)S(1)} %copy-done.4, f32[4096,128]{1,0:T(8,128)} %collective-permute-done.1.far_ref, ...), custom_call_target="tpu_custom_call" | custom-call | flops 60000000 | bytes 8000000 | tf_op jit(solution)/shard_map/raw_rows/pallas_call | solution.py:251
  40.0 3.5 %collective-permute-start.2 = (f32[2,16,16,128]{3,2,1,0:T(8,128)S(1)}, f32[2,16,16,128]{3,2,1,0:T(8,128)S(1)}, u32[]{:S(2)}, u32[]{:S(2)}) collective-permute-start(f32[2,16,16,128]{3,2,1,0:T(8,128)S(1)} %get-tuple-element.31), channel_id=1, source_target_pairs={{0,1},{1,2},{2,3},{4,5},{5,6},{6,7},{8,9},{9,10},{10,11},{12,13},{... | collective-permute-start | bytes 786440 | tf_op jit(solution)/shard_map/ppermute | solution.py:592
  43.5 1.5 %collective-permute-start.3 = (f32[2,16,16,128]{3,2,1,0:T(8,128)S(1)}, f32[2,16,16,128]{3,2,1,0:T(8,128)S(1)}, u32[]{:S(2)}, u32[]{:S(2)}) collective-permute-start(f32[2,16,16,128]{3,2,1,0:T(8,128)S(1)} %get-tuple-element.32), channel_id=1, source_target_pairs={{1,0},{2,1},{3,2},{5,4},{6,5},{7,6},{9,8},{10,9},{11,10},{13,12},{... | collective-permute-start | bytes 786440 | tf_op jit(solution)/shard_map/ppermute | solution.py:593
  45.0 3.6 %rows.3.refs_3_ = f32[128,2048]{1,0:T(8,128)S(1)} custom-call(s32[1]{0:T(128)} %bitcast.4.side_ref, f32[16,128,128]{2,1,0:T(8,128)} %columns.7.x_ref, f32[16,128,128]{2,1,0:T(8,128)} %collective-permute-done.8.near_ref, f32[16,128,128]{2,1,0:T(8,128)} %collective-permute-done.9.far_ref, f32[4,40,128]{2,1,0:T(8,128)S(1)} %bitcast_bitcast_fusion.taps_ref), custom_call_target="tpu_custom_call" | custom-call | flops 20000000 | bytes 4000000 | tf_op jit(solution)/shard_map/rows/pallas_call | solution.py:295
  48.6 3.5 %rows.2.refs_2_ = f32[128,2048]{1,0:T(8,128)S(1)} custom-call(s32[1]{0:T(128)} %bitcast.4.side_ref, f32[16,128,128]{2,1,0:T(8,128)S(1)} %columns.6.x_ref, f32[16,128,128]{2,1,0:T(8,128)} %collective-permute-done.6.near_ref, f32[16,128,128]{2,1,0:T(8,128)} %collective-permute-done.7.far_ref, f32[4,40,128]{2,1,0:T(8,128)S(1)} %bitcast_bitcast_fusion.taps_ref), custom_call_target="tpu_custom_call" | custom-call | flops 20000000 | bytes 4000000 | tf_op jit(solution)/shard_map/rows/pallas_call | solution.py:295
  52.2 2.3 %collective-permute-done.3.after_ref = f32[2,16,16,128]{3,2,1,0:T(8,128)S(1)} collective-permute-done((f32[2,16,16,128]{3,2,1,0:T(8,128)S(1)}, f32[2,16,16,128]{3,2,1,0:T(8,128)S(1)}, u32[]{:S(2)}, u32[]{:S(2)}) %collective-permute-start.3) | collective-permute-done | bytes 262176 | tf_op jit(solution)/shard_map/ppermute | solution.py:593
  54.5 2.3 %columns.5.refs_1_ = f32[128,2048]{1,0:T(8,128)S(1)} custom-call(f32[2,16,128,128]{3,2,1,0:T(8,128)S(1)} %get-tuple-element.30.x_ref, f32[2,16,16,128]{3,2,1,0:T(8,128)S(1)} %collective-permute-done.2.before_ref, f32[2,16,16,128]{3,2,1,0:T(8,128)S(1)} %collective-permute-done.3.after_ref, f32[4,40,128]{2,1,0:T(8,128)S(1)} %bitcast_bitcast_fusion.taps_ref), custom_call_target="tpu_custom_call" | custom-call | flops 20000000 | bytes 2500000 | tf_op jit(solution)/shard_map/columns/pallas_call | solution.py:207
  56.8 2.4 %columns.4.refs_0_ = f32[128,2048]{1,0:T(8,128)S(1)} custom-call(f32[2,16,128,128]{3,2,1,0:T(8,128)S(1)} %get-tuple-element.30.x_ref, f32[2,16,16,128]{3,2,1,0:T(8,128)S(1)} %collective-permute-done.2.before_ref, f32[2,16,16,128]{3,2,1,0:T(8,128)S(1)} %collective-permute-done.3.after_ref, f32[4,40,128]{2,1,0:T(8,128)S(1)} %bitcast_bitcast_fusion.taps_ref), custom_call_target="tpu_custom_call" | custom-call | flops 20000000 | bytes 2500000 | tf_op jit(solution)/shard_map/columns/pallas_call | solution.py:207
  59.2 3.2 %gram.1 = (f32[320,128]{1,0:T(8,128)S(1)}, f32[320,128]{1,0:T(8,128)}, f32[320,128]{1,0:T(8,128)}, f32[320,128]{1,0:T(8,128)}, f32[8,512]{1,0:T(8,128)S(1)}) custom-call(s32[1]{0:T(128)} %bitcast.me_ref, f32[4,512]{1,0:T(4,128)S(1)} %multiply_cosine_fusion.cosine_ref, f32[128,2048]{1,0:T(8,128)S(1)} %columns.4.refs_0_, f32[128,2048]{1,0:T(8,128)S(1)} %columns.5.refs_1_, ...), custom_call_target="tpu_custom_call" | custom-call | flops 4000000000 | bytes 5000000 | tf_op jit(solution)/shard_map/gram/pallas_call | solution.py:344
  62.4 2.6 %collective-permute-start.10 = (f32[320,128]{1,0:T(8,128)}, f32[320,128]{1,0:T(8,128)S(1)}, u32[]{:S(2)}, u32[]{:S(2)}) collective-permute-start(f32[320,128]{1,0:T(8,128)} %get-tuple-element.38), channel_id=1, source_target_pairs={{0,4},{4,0},{8,12},{12,8},{1,5},{5,1},{9,13},{13,9},{2,6},{6,2},{1... | collective-permute-start | bytes 491528 | tf_op jit(solution)/shard_map/ppermute | solution.py:423
  65.0 1.4 %collective-permute-start.11 = (f32[320,128]{1,0:T(8,128)}, f32[320,128]{1,0:T(8,128)}, u32[]{:S(2)}, u32[]{:S(2)}) collective-permute-start(f32[320,128]{1,0:T(8,128)} %get-tuple-element.39), channel_id=1, source_target_pairs={{0,8},{4,12},{8,0},{12,4},{1,9},{5,13},{9,1},{13,5},{2,10},{6,14},... | collective-permute-start | bytes 491528 | tf_op jit(solution)/shard_map/ppermute | solution.py:423
  66.4 0.1 collective-permute-start.12
  66.5 5.8 %collective-permute-done.11.refs_2_ = f32[320,128]{1,0:T(8,128)} collective-permute-done((f32[320,128]{1,0:T(8,128)}, f32[320,128]{1,0:T(8,128)}, u32[]{:S(2)}, u32[]{:S(2)}) %collective-permute-start.11) | collective-permute-done | bytes 163872 | tf_op jit(solution)/shard_map/ppermute | solution.py:423
  72.4 2.0 %collective-permute-done.12.refs_3_ = f32[320,128]{1,0:T(8,128)} collective-permute-done((f32[320,128]{1,0:T(8,128)}, f32[320,128]{1,0:T(8,128)}, u32[]{:S(2)}, u32[]{:S(2)}) %collective-permute-start.12) | collective-permute-done | bytes 163872 | tf_op jit(solution)/shard_map/ppermute | solution.py:423
  74.4 1.5 %sum_and_split.1 = (f32[80,128]{1,0:T(8,128)S(1)}, f32[80,128]{1,0:T(8,128)S(1)}, f32[80,128]{1,0:T(8,128)S(1)}, f32[80,128]{1,0:T(8,128)S(1)}) custom-call(s32[1]{0:T(128)} %bitcast.5.me_ref, f32[320,128]{1,0:T(8,128)S(1)} %get-tuple-element.37.refs_0_, f32[320,128]{1,0:T(8,128)S(1)} %collective-permute-done.10.refs_1_, ...), custom_call_target="tpu_custom_call" | custom-call | tf_op jit(solution)/shard_map/sum_and_split/pallas_call | solution.py:377
  75.8 1.8 %collective-permute-start.13 = (f32[80,128]{1,0:T(8,128)S(1)}, f32[80,128]{1,0:T(8,128)S(1)}, u32[]{:S(2)}, u32[]{:S(2)}) collective-permute-start(f32[80,128]{1,0:T(8,128)S(1)} %get-tuple-element.42), channel_id=1, source_target_pairs={{0,1},{1,0},{2,3},{3,2},{4,5},{5,4},{6,7},{7,6},{8,9},{9,8},{10,11... | collective-permute-start | bytes 122888 | tf_op jit(solution)/shard_map/ppermute | solution.py:423
  77.6 2.4 %collective-permute-start.14 = (f32[80,128]{1,0:T(8,128)S(1)}, f32[80,128]{1,0:T(8,128)S(1)}, u32[]{:S(2)}, u32[]{:S(2)}) collective-permute-start(f32[80,128]{1,0:T(8,128)S(1)} %get-tuple-element.43), channel_id=1, source_target_pairs={{0,2},{1,3},{2,0},{3,1},{4,6},{5,7},{6,4},{7,5},{8,10},{9,11},{10,... | collective-permute-start | bytes 122888 | tf_op jit(solution)/shard_map/ppermute | solution.py:423
  80.1 0.2 collective-permute-start.15
  80.3 3.4 %collective-permute-done.14 = f32[80,128]{1,0:T(8,128)S(1)} collective-permute-done((f32[80,128]{1,0:T(8,128)S(1)}, f32[80,128]{1,0:T(8,128)S(1)}, u32[]{:S(2)}, u32[]{:S(2)}) %collective-permute-start.14) | collective-permute-done | bytes 40992 | tf_op jit(solution)/shard_map/ppermute | solution.py:423
  83.6 2.2 %collective-permute-done.15 = f32[80,128]{1,0:T(8,128)S(1)} collective-permute-done((f32[80,128]{1,0:T(8,128)S(1)}, f32[80,128]{1,0:T(8,128)S(1)}, u32[]{:S(2)}, u32[]{:S(2)}) %collective-permute-start.15) | collective-permute-done | bytes 40992 | tf_op jit(solution)/shard_map/ppermute | solution.py:423
  86.0 1.7 %collective-permute-start.17 = (f32[80,128]{1,0:T(8,128)S(1)}, f32[80,128]{1,0:T(8,128)S(1)}, u32[]{:S(2)}, u32[]{:S(2)}) collective-permute-start(f32[80,128]{1,0:T(8,128)S(1)} %add_add_fusion.refs_0_), channel_id=1, source_target_pairs={{0,2},{1,3},{2,0},{3,1},{4,6},{5,7},{6,4},{7,5},{8,10},{9,11},{10,... | collective-permute-start | bytes 122888 | tf_op jit(solution)/shard_map/ppermute | solution.py:423
  87.6 2.7 %collective-permute-start.18 = (f32[80,128]{1,0:T(8,128)S(1)}, f32[80,128]{1,0:T(8,128)S(1)}, u32[]{:S(2)}, u32[]{:S(2)}) collective-permute-start(f32[80,128]{1,0:T(8,128)S(1)} %add_add_fusion.refs_0_), channel_id=1, source_target_pairs={{0,3},{1,2},{2,1},{3,0},{4,7},{5,6},{6,5},{7,4},{8,11},{9,10},{10,... | collective-permute-start | bytes 122888 | tf_op jit(solution)/shard_map/ppermute | solution.py:423
  90.3 1.0 collective-permute-done.17.refs_2_
  91.4 2.1 %collective-permute-done.18.refs_3_ = f32[80,128]{1,0:T(8,128)S(1)} collective-permute-done((f32[80,128]{1,0:T(8,128)S(1)}, f32[80,128]{1,0:T(8,128)S(1)}, u32[]{:S(2)}, u32[]{:S(2)}) %collective-permute-start.18) | collective-permute-done | bytes 40992 | tf_op jit(solution)/shard_map/ppermute | solution.py:423
  93.4 0.2 join.1.refs_4_
  93.8 1.7 %collective-permute-start.20 = (f32[320,128]{1,0:T(8,128)S(1)}, f32[320,128]{1,0:T(8,128)S(1)}, u32[]{:S(2)}, u32[]{:S(2)}) collective-permute-start(f32[320,128]{1,0:T(8,128)S(1)} %join.1.refs_4_), channel_id=1, source_target_pairs={{0,8},{4,12},{8,0},{12,4},{1,9},{5,13},{9,1},{13,5},{2,10},{6,14},... | collective-permute-start | bytes 491528 | tf_op jit(solution)/shard_map/ppermute | solution.py:423
  95.4 0.2 collective-permute-start.21
  95.6 5.3 %collective-permute-done.20.refs_6_ = f32[320,128]{1,0:T(8,128)S(1)} collective-permute-done((f32[320,128]{1,0:T(8,128)S(1)}, f32[320,128]{1,0:T(8,128)S(1)}, u32[]{:S(2)}, u32[]{:S(2)}) %collective-permute-start.20) | collective-permute-done | bytes 163872 | tf_op jit(solution)/shard_map/ppermute | solution.py:423
  100.9 2.4 %collective-permute-done.21.refs_7_ = f32[320,128]{1,0:T(8,128)S(1)} collective-permute-done((f32[320,128]{1,0:T(8,128)S(1)}, f32[320,128]{1,0:T(8,128)S(1)}, u32[]{:S(2)}, u32[]{:S(2)}) %collective-permute-start.21) | collective-permute-done | bytes 163872 | tf_op jit(solution)/shard_map/ppermute | solution.py:423
  103.3 1.2 %copy-done.2 = f32[128,2048]{1,0:T(8,128)S(1)} copy-done((f32[128,2048]{1,0:T(8,128)S(1)}, f32[128,2048]{1,0:T(8,128)}, u32[]{:S(2)}) %copy-start.2) | copy-done | bytes 1048600
  104.5 11.2 %clean.1 = f32[8192,128]{1,0:T(8,128)} custom-call(s32[1]{0:T(128)} %bitcast.me_ref, f32[8,512]{1,0:T(8,128)S(1)} %get-tuple-element.36.start_ref, f32[128,2048]{1,0:T(8,128)S(1)} %copy-done.2, f32[128,2048]{1,0:T(8,128)S(1)} %columns.5.refs_1_, f32[128,2048]{1,0:T(8,128)S(1)} %rows.2.refs_2_, f32[128,2048]{1,0:T(8,128)S(1)} %rows.3.refs_3_, ...), custom_call_target="tpu_custom_call" | custom-call | flops 40000000 | bytes 9000000 | tf_op jit(solution)/shard_map/clean/pallas_call | solution.py:538
  (26 shorter events, 0.2 us)
Async XLA Ops:
  0.0 4.5 %copy-start = (f32[512,16,128]{2,1,0:T(8,128)S(1)}, f32[512,16,128]{2,1,0:T(8,128)}, u32[]{:S(2)}) copy-start(f32[512,16,128]{2,1,0:T(8,128)} %param.2) | copy-start | bytes 12582916
  1.9 9.2 %copy-start.5 = (f32[512,33]{0,1:T(8,128)S(1)}, f32[512,33]{0,1:T(8,128)}, u32[]{:S(2)}) copy-start(f32[512,33]{0,1:T(8,128)} %param.3) | copy-start | bytes 202756
  1.9 26.5 %collective-permute-start = (f32[4096,128]{1,0:T(8,128)S(1)}, f32[4096,128]{1,0:T(8,128)S(1)}, u32[]{:S(2)}, u32[]{:S(2)}) collective-permute-start(f32[4096,128]{1,0:T(8,128)S(1)} %bitcast.14), channel_id=1, source_target_pairs={{0,4},{4,0},{8,12},{12,8},{1,5},{5,1},{9,13},{13,9},{2,6},{6,2},{1... | collective-permute-start | bytes 6291464 | tf_op jit(solution)/shard_map/ppermute | solution.py:580
  2.5 28.9 %collective-permute-start.1 = (f32[4096,128]{1,0:T(8,128)S(1)}, f32[4096,128]{1,0:T(8,128)}, u32[]{:S(2)}, u32[]{:S(2)}) collective-permute-start(f32[4096,128]{1,0:T(8,128)S(1)} %bitcast.15), channel_id=1, source_target_pairs={{4,8},{8,4},{5,9},{9,5},{6,10},{10,6},{7,11},{11,7},{20,24},{24,20... | collective-permute-start | bytes 6291464 | tf_op jit(solution)/shard_map/ppermute | solution.py:579
  5.2 10.6 %collective-permute-start.4 = (f32[2,16,16,128]{3,2,1,0:T(8,128)S(1)}, f32[2,16,16,128]{3,2,1,0:T(8,128)S(1)}, u32[]{:S(2)}, u32[]{:S(2)}) collective-permute-start(f32[2,16,16,128]{3,2,1,0:T(8,128)S(1)} %get-tuple-element.34), channel_id=1, source_target_pairs={{0,1},{1,2},{2,3},{4,5},{5,6},{6,7},{8,9},{9,10},{10,11},{12,13},{... | collective-permute-start | bytes 786440 | tf_op jit(solution)/shard_map/ppermute | solution.py:582
  9.7 10.8 %collective-permute-start.5 = (f32[2,16,16,128]{3,2,1,0:T(8,128)S(1)}, f32[2,16,16,128]{3,2,1,0:T(8,128)S(1)}, u32[]{:S(2)}, u32[]{:S(2)}) collective-permute-start(f32[2,16,16,128]{3,2,1,0:T(8,128)S(1)} %get-tuple-element.35), channel_id=1, source_target_pairs={{1,0},{2,1},{3,2},{5,4},{6,5},{7,6},{9,8},{10,9},{11,10},{13,12},{... | collective-permute-start | bytes 786440 | tf_op jit(solution)/shard_map/ppermute | solution.py:583
  23.3 20.2 %collective-permute-start.8 = (f32[16,128,128]{2,1,0:T(8,128)}, f32[16,128,128]{2,1,0:T(8,128)}, u32[]{:S(2)}, u32[]{:S(2)}) collective-permute-start(f32[16,128,128]{2,1,0:T(8,128)} %columns.7.x_ref), channel_id=1, source_target_pairs={{0,4},{4,0},{8,12},{12,8},{1,5},{5,1},{9,13},{13,9},{2,6},{6,2},{1... | collective-permute-start | bytes 3145736 | tf_op jit(solution)/shard_map/ppermute | solution.py:590
  23.5 21.5 %collective-permute-start.9 = (f32[16,128,128]{2,1,0:T(8,128)}, f32[16,128,128]{2,1,0:T(8,128)}, u32[]{:S(2)}, u32[]{:S(2)}) collective-permute-start(f32[16,128,128]{2,1,0:T(8,128)} %columns.7.x_ref), channel_id=1, source_target_pairs={{4,8},{8,4},{5,9},{9,5},{6,10},{10,6},{7,11},{11,7},{20,24},{24,20... | collective-permute-start | bytes 3145736 | tf_op jit(solution)/shard_map/ppermute | solution.py:589
  27.0 21.6 %collective-permute-start.6 = (f32[16,128,128]{2,1,0:T(8,128)S(1)}, f32[16,128,128]{2,1,0:T(8,128)}, u32[]{:S(2)}, u32[]{:S(2)}) collective-permute-start(f32[16,128,128]{2,1,0:T(8,128)S(1)} %columns.6.x_ref), channel_id=1, source_target_pairs={{0,4},{4,0},{8,12},{12,8},{1,5},{5,1},{9,13},{13,9},{2,6},{6,2},{1... | collective-permute-start | bytes 3145736 | tf_op jit(solution)/shard_map/ppermute | solution.py:590
  28.4 1.3 %copy-start.3 = (f32[4096,128]{1,0:T(8,128)}, f32[4096,128]{1,0:T(8,128)S(1)}, u32[]{:S(2)}) copy-start(f32[4096,128]{1,0:T(8,128)S(1)} %collective-permute-done.near_ref) | copy-start | bytes 6291460
  29.7 18.9 %collective-permute-start.7 = (f32[16,128,128]{2,1,0:T(8,128)S(1)}, f32[16,128,128]{2,1,0:T(8,128)}, u32[]{:S(2)}, u32[]{:S(2)}) collective-permute-start(f32[16,128,128]{2,1,0:T(8,128)S(1)} %columns.6.x_ref), channel_id=1, source_target_pairs={{4,8},{8,4},{5,9},{9,5},{6,10},{10,6},{7,11},{11,7},{20,24},{24,20... | collective-permute-start | bytes 3145736 | tf_op jit(solution)/shard_map/ppermute | solution.py:589
  31.4 1.6 %copy-start.4 = (f32[4096,128]{1,0:T(8,128)S(1)}, f32[4096,128]{1,0:T(8,128)}, u32[]{:S(2)}) copy-start(f32[4096,128]{1,0:T(8,128)} %copy-done.3) | copy-start | bytes 6291460
  40.0 12.2 %collective-permute-start.2 = (f32[2,16,16,128]{3,2,1,0:T(8,128)S(1)}, f32[2,16,16,128]{3,2,1,0:T(8,128)S(1)}, u32[]{:S(2)}, u32[]{:S(2)}) collective-permute-start(f32[2,16,16,128]{3,2,1,0:T(8,128)S(1)} %get-tuple-element.31), channel_id=1, source_target_pairs={{0,1},{1,2},{2,3},{4,5},{5,6},{6,7},{8,9},{9,10},{10,11},{12,13},{... | collective-permute-start | bytes 786440 | tf_op jit(solution)/shard_map/ppermute | solution.py:592
  43.5 10.9 %collective-permute-start.3 = (f32[2,16,16,128]{3,2,1,0:T(8,128)S(1)}, f32[2,16,16,128]{3,2,1,0:T(8,128)S(1)}, u32[]{:S(2)}, u32[]{:S(2)}) collective-permute-start(f32[2,16,16,128]{3,2,1,0:T(8,128)S(1)} %get-tuple-element.32), channel_id=1, source_target_pairs={{1,0},{2,1},{3,2},{5,4},{6,5},{7,6},{9,8},{10,9},{11,10},{13,12},{... | collective-permute-start | bytes 786440 | tf_op jit(solution)/shard_map/ppermute | solution.py:593
  59.2 3.2 %copy-start.1 = (f32[128,2048]{1,0:T(8,128)}, f32[128,2048]{1,0:T(8,128)S(1)}, u32[]{:S(2)}) copy-start(f32[128,2048]{1,0:T(8,128)S(1)} %columns.4.refs_0_) | copy-start | bytes 3145732
  62.4 4.1 %collective-permute-start.10 = (f32[320,128]{1,0:T(8,128)}, f32[320,128]{1,0:T(8,128)S(1)}, u32[]{:S(2)}, u32[]{:S(2)}) collective-permute-start(f32[320,128]{1,0:T(8,128)} %get-tuple-element.38), channel_id=1, source_target_pairs={{0,4},{4,0},{8,12},{12,8},{1,5},{5,1},{9,13},{13,9},{2,6},{6,2},{1... | collective-permute-start | bytes 491528 | tf_op jit(solution)/shard_map/ppermute | solution.py:423
  65.0 7.4 %collective-permute-start.11 = (f32[320,128]{1,0:T(8,128)}, f32[320,128]{1,0:T(8,128)}, u32[]{:S(2)}, u32[]{:S(2)}) collective-permute-start(f32[320,128]{1,0:T(8,128)} %get-tuple-element.39), channel_id=1, source_target_pairs={{0,8},{4,12},{8,0},{12,4},{1,9},{5,13},{9,1},{13,5},{2,10},{6,14},... | collective-permute-start | bytes 491528 | tf_op jit(solution)/shard_map/ppermute | solution.py:423
  66.4 8.0 %collective-permute-start.12 = (f32[320,128]{1,0:T(8,128)}, f32[320,128]{1,0:T(8,128)}, u32[]{:S(2)}, u32[]{:S(2)}) collective-permute-start(f32[320,128]{1,0:T(8,128)} %get-tuple-element.40), channel_id=1, source_target_pairs={{0,12},{4,8},{8,4},{12,0},{1,13},{5,9},{9,5},{13,1},{2,14},{6,10},... | collective-permute-start | bytes 491528 | tf_op jit(solution)/shard_map/ppermute | solution.py:423
  75.8 4.5 %collective-permute-start.13 = (f32[80,128]{1,0:T(8,128)S(1)}, f32[80,128]{1,0:T(8,128)S(1)}, u32[]{:S(2)}, u32[]{:S(2)}) collective-permute-start(f32[80,128]{1,0:T(8,128)S(1)} %get-tuple-element.42), channel_id=1, source_target_pairs={{0,1},{1,0},{2,3},{3,2},{4,5},{5,4},{6,7},{7,6},{8,9},{9,8},{10,11... | collective-permute-start | bytes 122888 | tf_op jit(solution)/shard_map/ppermute | solution.py:423
  77.6 6.0 %collective-permute-start.14 = (f32[80,128]{1,0:T(8,128)S(1)}, f32[80,128]{1,0:T(8,128)S(1)}, u32[]{:S(2)}, u32[]{:S(2)}) collective-permute-start(f32[80,128]{1,0:T(8,128)S(1)} %get-tuple-element.43), channel_id=1, source_target_pairs={{0,2},{1,3},{2,0},{3,1},{4,6},{5,7},{6,4},{7,5},{8,10},{9,11},{10,... | collective-permute-start | bytes 122888 | tf_op jit(solution)/shard_map/ppermute | solution.py:423
  80.1 5.8 %collective-permute-start.15 = (f32[80,128]{1,0:T(8,128)S(1)}, f32[80,128]{1,0:T(8,128)S(1)}, u32[]{:S(2)}, u32[]{:S(2)}) collective-permute-start(f32[80,128]{1,0:T(8,128)S(1)} %get-tuple-element.44), channel_id=1, source_target_pairs={{0,3},{1,2},{2,1},{3,0},{4,7},{5,6},{6,5},{7,4},{8,11},{9,10},{10,... | collective-permute-start | bytes 122888 | tf_op jit(solution)/shard_map/ppermute | solution.py:423
  85.9 4.5 %collective-permute-start.16 = (f32[80,128]{1,0:T(8,128)S(1)}, f32[80,128]{1,0:T(8,128)S(1)}, u32[]{:S(2)}, u32[]{:S(2)}) collective-permute-start(f32[80,128]{1,0:T(8,128)S(1)} %add_add_fusion.refs_0_), channel_id=1, source_target_pairs={{0,1},{1,0},{2,3},{3,2},{4,5},{5,4},{6,7},{7,6},{8,9},{9,8},{10,11... | collective-permute-start | bytes 122888 | tf_op jit(solution)/shard_map/ppermute | solution.py:423
  86.0 5.4 %collective-permute-start.17 = (f32[80,128]{1,0:T(8,128)S(1)}, f32[80,128]{1,0:T(8,128)S(1)}, u32[]{:S(2)}, u32[]{:S(2)}) collective-permute-start(f32[80,128]{1,0:T(8,128)S(1)} %add_add_fusion.refs_0_), channel_id=1, source_target_pairs={{0,2},{1,3},{2,0},{3,1},{4,6},{5,7},{6,4},{7,5},{8,10},{9,11},{10,... | collective-permute-start | bytes 122888 | tf_op jit(solution)/shard_map/ppermute | solution.py:423
  87.6 5.8 %collective-permute-start.18 = (f32[80,128]{1,0:T(8,128)S(1)}, f32[80,128]{1,0:T(8,128)S(1)}, u32[]{:S(2)}, u32[]{:S(2)}) collective-permute-start(f32[80,128]{1,0:T(8,128)S(1)} %add_add_fusion.refs_0_), channel_id=1, source_target_pairs={{0,3},{1,2},{2,1},{3,0},{4,7},{5,6},{6,5},{7,4},{8,11},{9,10},{10,... | collective-permute-start | bytes 122888 | tf_op jit(solution)/shard_map/ppermute | solution.py:423
  93.7 1.9 %collective-permute-start.19 = (f32[320,128]{1,0:T(8,128)S(1)}, f32[320,128]{1,0:T(8,128)S(1)}, u32[]{:S(2)}, u32[]{:S(2)}) collective-permute-start(f32[320,128]{1,0:T(8,128)S(1)} %join.1.refs_4_), channel_id=1, source_target_pairs={{0,4},{4,0},{8,12},{12,8},{1,5},{5,1},{9,13},{13,9},{2,6},{6,2},{1... | collective-permute-start | bytes 491528 | tf_op jit(solution)/shard_map/ppermute | solution.py:423
  93.8 7.1 %collective-permute-start.20 = (f32[320,128]{1,0:T(8,128)S(1)}, f32[320,128]{1,0:T(8,128)S(1)}, u32[]{:S(2)}, u32[]{:S(2)}) collective-permute-start(f32[320,128]{1,0:T(8,128)S(1)} %join.1.refs_4_), channel_id=1, source_target_pairs={{0,8},{4,12},{8,0},{12,4},{1,9},{5,13},{9,1},{13,5},{2,10},{6,14},... | collective-permute-start | bytes 491528 | tf_op jit(solution)/shard_map/ppermute | solution.py:423
  95.4 7.9 %collective-permute-start.21 = (f32[320,128]{1,0:T(8,128)S(1)}, f32[320,128]{1,0:T(8,128)S(1)}, u32[]{:S(2)}, u32[]{:S(2)}) collective-permute-start(f32[320,128]{1,0:T(8,128)S(1)} %join.1.refs_4_), channel_id=1, source_target_pairs={{0,12},{4,8},{8,4},{12,0},{1,13},{5,9},{9,5},{13,1},{2,14},{6,10},... | collective-permute-start | bytes 491528 | tf_op jit(solution)/shard_map/ppermute | solution.py:423
  103.3 1.2 %copy-start.2 = (f32[128,2048]{1,0:T(8,128)S(1)}, f32[128,2048]{1,0:T(8,128)}, u32[]{:S(2)}) copy-start(f32[128,2048]{1,0:T(8,128)} %copy-done.1) | copy-start | bytes 3145732
